TPU v7x, 128 devices: a whole 4x4x4 slice. The times are simulated.
128 devices in a mesh: room: 4 (over x_hi, core), geom: 32 (over z, x_lo, y).
Axes of the slice: x: 4 (x_hi: 2, x_lo: 2; x = x_hi * 2 + x_lo), y: 4, z: 4, core: 2. Of those that a mesh axis runs over, the one named last changes fastest.
Arguments:
- queries: bfloat16 [4, 4096, 512], P('room', 'geom'), may hold values from -6 to 6
- features: bfloat16 [4, 4096, 512], P('room', 'geom'), may hold values from -45 to 45
- visible: int32 [4, 32, 32], P('room', 'geom'), may hold values from 0 to 1, as said below
- cotangent: bfloat16 [4, 4096, 512], P('room', 'geom'), may hold values from -0.125 to 0.125
- w_query: bfloat16 [512, 512], replicated, may hold values from -0.25 to 0.25
- w_key: bfloat16 [512, 512], replicated, may hold values from -0.25 to 0.25
- w_value: bfloat16 [512, 512], replicated, may hold values from -0.25 to 0.25
- w_out: bfloat16 [512, 512], replicated, may hold values from -0.25 to 0.25
- w_up: bfloat16 [512, 1024], replicated, may hold values from -0.25 to 0.25
- w_down: bfloat16 [1024, 512], replicated, may hold values from -0.1875 to 0.1875
- gain_attn: float32 [512], replicated, may hold values from 0.25 to 1.75
- gain_mlp: float32 [512], replicated, may hold values from 0.25 to 1.75
Outputs:
- output: bfloat16 [4, 4096, 512], P('room', 'geom')
- grad_query_w: bfloat16 [512, 512], replicated
- grad_key_w: bfloat16 [512, 512], replicated
- grad_value_w: bfloat16 [512, 512], replicated
- grad_out_w: bfloat16 [512, 512], replicated
- grad_up_w: bfloat16 [512, 1024], replicated
- grad_down_w: bfloat16 [1024, 512], replicated
- grad_gain_attn: bfloat16 [512], replicated
- grad_gain_mlp: bfloat16 [512], replicated
Inputs may be any that keep to these rules, and one draw needn't show every extreme that they name: `visible`: every query block sees at least one key block.
All inputs are finite; a program needn't handle non-finite values.
Results may differ from a plain program's by a relative error of at most 0.017.
The roundings to bfloat16 on the way count: a program that leaves them out, or rounds other values in their place, can miss the bound.
Values may be sent and summed in bfloat16 or wider, within the bound.
No kernel may reach another device: no remote copies, remote signals or barrier semaphores. Data moves between devices by JAX's collectives and lax.ppermute only.
A program may use at most 128 MiB of HBM per device.

v0:
```python
import math

import jax
import jax.numpy as jnp
from jax import lax
from jax.sharding import PartitionSpec as P

HEADS = 4
BLK = 128


EPSILON = 1e-05
GELU_COEF = math.sqrt(2.0 / math.pi)


def normalize(inputs, gain):
    center = inputs - jnp.mean(inputs, axis=-1, keepdims=True)
    inverse = lax.rsqrt(jnp.mean(center * center, axis=-1, keepdims=True) + EPSILON)
    scaled = center * inverse
    return (scaled, inverse, scaled * gain)


def gelu_pair(inputs):
    inner = GELU_COEF * (inputs + 0.044715 * inputs * inputs * inputs)
    tangent = jnp.tanh(inner)
    value = 0.5 * inputs * (1.0 + tangent)
    slope = 0.5 * (1.0 + tangent) + 0.5 * inputs * (1.0 - tangent * tangent) * GELU_COEF * (
        1.0 + 3.0 * 0.044715 * inputs * inputs
    )
    return (value, slope)


def mult_nt(left, right):
    return lax.dot_general(
        left, right, (((1,), (1,)), ((), ())), preferred_element_type=jnp.float32
    )


def mult_tn(left, right):
    return lax.dot_general(
        left, right, (((0,), (0,)), ((), ())), preferred_element_type=jnp.float32
    )


def device_step(
    queries,
    visible,
    cotangent,
    key_rows,
    value_rows,
    w_query,
    w_out,
    w_up,
    w_down,
    gain_attn,
    gain_mlp,
):
    head_size = key_rows.shape[1] // HEADS
    factor = 1.0 / math.sqrt(head_size)
    allowed = jnp.repeat(jnp.repeat(visible > 0, BLK, axis=0), BLK, axis=1)
    inputs = queries.astype(jnp.float32)
    scaled_one, inverse_one, normed = normalize(inputs, gain_attn)
    normed_b = normed.astype(jnp.bfloat16)
    query_rows = jnp.dot(normed_b, w_query, preferred_element_type=jnp.float32).astype(jnp.bfloat16)
    contexts = []
    saved = []
    for head_index in range(HEADS):
        lower = head_index * head_size
        query_head = query_rows[:, lower : lower + head_size]
        key_head = key_rows[:, lower : lower + head_size]
        value_head = value_rows[:, lower : lower + head_size]
        scores = mult_nt(query_head, key_head) * factor
        scores = jnp.where(allowed, scores, -1e30)
        highest = jnp.max(scores, axis=-1, keepdims=True)
        expo = jnp.exp(scores - highest)
        attend = expo / jnp.sum(expo, axis=-1, keepdims=True)
        attend_b = attend.astype(jnp.bfloat16)
        contexts.append(
            jnp.dot(attend_b, value_head, preferred_element_type=jnp.float32).astype(jnp.bfloat16)
        )
        saved.append((attend, attend_b))
    context = jnp.concatenate(contexts, axis=1)
    mixed = inputs + jnp.dot(context, w_out, preferred_element_type=jnp.float32)
    scaled_two, inverse_two, normed_two = normalize(mixed, gain_mlp)
    normed_two_b = normed_two.astype(jnp.bfloat16)
    upper = jnp.dot(normed_two_b, w_up, preferred_element_type=jnp.float32)
    activated, slope = gelu_pair(upper)
    activated_b = activated.astype(jnp.bfloat16)
    output = (mixed + jnp.dot(activated_b, w_down, preferred_element_type=jnp.float32)).astype(
        jnp.bfloat16
    )
    grad_down = mult_tn(activated_b, cotangent)
    grad_activated = mult_nt(cotangent, w_down)
    grad_upper_b = (grad_activated * slope).astype(jnp.bfloat16)
    grad_up = mult_tn(normed_two_b, grad_upper_b)
    grad_normed_two = mult_nt(grad_upper_b, w_up)
    grad_gain_mlp = jnp.sum(grad_normed_two * scaled_two, axis=0)
    grad_scaled = grad_normed_two * gain_mlp
    mean_one = jnp.mean(grad_scaled, axis=-1, keepdims=True)
    mean_two = jnp.mean(grad_scaled * scaled_two, axis=-1, keepdims=True)
    grad_mixed = cotangent.astype(jnp.float32) + inverse_two * (
        grad_scaled - mean_one - scaled_two * mean_two
    )
    grad_mixed_b = grad_mixed.astype(jnp.bfloat16)
    grad_out = mult_tn(context, grad_mixed_b)
    grad_context = mult_nt(grad_mixed_b, w_out).astype(jnp.bfloat16)
    grad_queries = []
    grad_keys = []
    grad_values = []
    for head_index in range(HEADS):
        lower = head_index * head_size
        query_head = query_rows[:, lower : lower + head_size]
        key_head = key_rows[:, lower : lower + head_size]
        value_head = value_rows[:, lower : lower + head_size]
        attend, attend_b = saved[head_index]
        grad_head = grad_context[:, lower : lower + head_size]
        grad_attend = mult_nt(grad_head, value_head)
        grad_values.append(mult_tn(attend_b, grad_head))
        centre = jnp.sum(attend * grad_attend, axis=-1, keepdims=True)
        grad_scores = (attend * (grad_attend - centre) * factor).astype(jnp.bfloat16)
        grad_queries.append(jnp.dot(grad_scores, key_head, preferred_element_type=jnp.float32))
        grad_keys.append(mult_tn(grad_scores, query_head))
    grad_query_rows = jnp.concatenate(grad_queries, axis=1).astype(jnp.bfloat16)
    partial_keys = jnp.concatenate(grad_keys, axis=1).astype(jnp.bfloat16)
    partial_values = jnp.concatenate(grad_values, axis=1).astype(jnp.bfloat16)
    grad_query = mult_tn(normed_b, grad_query_rows)
    grad_normed = mult_nt(grad_query_rows, w_query)
    grad_gain_attn = jnp.sum(grad_normed * scaled_one, axis=0)
    grads = (grad_query, grad_out, grad_up, grad_down, grad_gain_attn, grad_gain_mlp)
    return (output, grads, partial_keys, partial_values)


def local(
    queries,
    features,
    visible,
    cotangent,
    w_query,
    w_key,
    w_value,
    w_out,
    w_up,
    w_down,
    gain_attn,
    gain_mlp,
):
    local_feat = features[0]
    local_keys = jnp.dot(local_feat, w_key, preferred_element_type=jnp.float32).astype(jnp.bfloat16)
    local_values = jnp.dot(local_feat, w_value, preferred_element_type=jnp.float32).astype(
        jnp.bfloat16
    )
    key_rows, value_rows = (
        lax.all_gather(local_keys, "geom", axis=0, tiled=True),
        lax.all_gather(local_values, "geom", axis=0, tiled=True),
    )
    output, grads, partial_keys, partial_values = device_step(
        queries[0],
        visible[0],
        cotangent[0],
        key_rows,
        value_rows,
        w_query,
        w_out,
        w_up,
        w_down,
        gain_attn,
        gain_mlp,
    )
    key_sum, value_sum = (
        lax.psum_scatter(partial_keys.astype(jnp.float32), "geom", scatter_dimension=0, tiled=True),
        lax.psum_scatter(
            partial_values.astype(jnp.float32), "geom", scatter_dimension=0, tiled=True
        ),
    )
    feat_float = local_feat.astype(jnp.float32)
    grad_key = lax.dot_general(
        feat_float,
        key_sum,
        (((0,), (0,)), ((), ())),
        precision=lax.Precision.HIGHEST,
        preferred_element_type=jnp.float32,
    )
    grad_value = lax.dot_general(
        feat_float,
        value_sum,
        (((0,), (0,)), ((), ())),
        precision=lax.Precision.HIGHEST,
        preferred_element_type=jnp.float32,
    )
    grad_query, grad_out, grad_up, grad_down, grad_gain_attn, grad_gain_mlp = grads
    totals = lax.psum(
        (
            grad_query,
            grad_key,
            grad_value,
            grad_out,
            grad_up,
            grad_down,
            grad_gain_attn,
            grad_gain_mlp,
        ),
        ("room", "geom"),
    )
    summed = [piece.astype(jnp.bfloat16) for piece in totals]
    return (
        output[None],
        summed[0],
        summed[1],
        summed[2],
        summed[3],
        summed[4],
        summed[5],
        summed[6],
        summed[7],
    )


def solution(mesh):
    placed = (
        P("room", "geom", None),
        P("room", "geom", None),
        P("room", "geom", None),
        P("room", "geom", None),
        P(),
        P(),
        P(),
        P(),
        P(),
        P(),
        P(),
        P(),
    )
    return jax.shard_map(
        local,
        mesh=mesh,
        in_specs=placed,
        out_specs=(P("room", "geom", None), P(), P(), P(), P(), P(), P(), P(), P()),
        check_vma=False,
    )
```

profile of v0, /device:TPU:1, one launch (start us, length us, event | category | flops | bytes accessed | tf_op | source)
XLA Modules:
  0.0 831.7 jit_solution(216690923784676051)
XLA Ops:
  7.3 2.1 convolution_convert_fusion.10
  9.5 2.0 convolution_convert_fusion.9
  11.5 1.0 convert_reduce_fusion
  12.6 1.1 fusion.54
  14.1 137.4 %all-gather.3.cloned.1.call-done = bf16[4096,512]{1,0:T(8,128)(2,1)} async-done(((bf16[128,512]{1,0:T(8,128)(2,1)}), bf16[4096,512]{1,0:T(8,128)(2,1)}) %all-gather.3.cloned.1.call-update) | async-done | bytes 4194320 | tf_op jit(solution)/shard_map/all_gather | solution.py:153
  151.5 1.9 fusion.99
  153.4 1.4 copy-done.8
  155.8 1.3 copy-done.5
  159.9 151.2 %all-gather.5.cloned.1.call-done = bf16[4096,512]{1,0:T(8,128)(2,1)} async-done(((bf16[128,512]{1,0:T(8,128)(2,1)}), bf16[4096,512]{1,0:T(8,128)(2,1)}) %all-gather.5.cloned.1.call-update) | async-done | bytes 4194320 | tf_op jit(solution)/shard_map/all_gather | solution.py:154
  311.0 2.7 convolution_convert_fusion.19
  313.8 1.0 copy-done.78
  320.2 1.1 multiply_reduce_fusion.4
  322.5 1.0 copy-done.9
  325.4 3.6 maximum_convert_fusion.1
  329.7 2.7 multiply_reduce_fusion.3
  333.8 0.9 copy-done.79
  337.5 1.5 copy-done.4
  342.6 1.0 copy-done.17
  344.0 3.8 maximum_convert_fusion
  347.9 1.9 convolution_convert_fusion.15
  349.8 2.0 convolution_convert_fusion.14
  354.6 1.3 fusion.79
  355.8 1.4 fusion.78
  357.2 1.9 fusion.55
  359.1 1.0 fusion.15
  360.1 145.4 %reduce-scatter.5.cloned.1.call-done = f32[128,512]{1,0:T(8,128)} async-done(((f32[4096,512]{1,0:T(8,128)}), f32[128,512]{1,0:T(8,128)}) %reduce-scatter.5.cloned.1.call-update) | async-done | bytes 262160 | tf_op jit(solution)/shard_map/reduce_scatter | solution.py:171
  505.5 2.5 convolution_bitcast_fusion
  508.1 174.8 %reduce-scatter.3.cloned.1.call-done = f32[128,512]{1,0:T(8,128)} async-done(((f32[4096,512]{1,0:T(8,128)}), f32[128,512]{1,0:T(8,128)}) %reduce-scatter.3.cloned.1.call-update) | async-done | bytes 262160 | tf_op jit(solution)/shard_map/reduce_scatter | solution.py:170
  682.8 2.6 convolution_bitcast_fusion.1
  685.4 135.7 %all-reduce.2 = (bf16[512,512]{1,0:T(8,128)(2,1)}, bf16[512,512]{0,1:T(8,128)(2,1)}, bf16[512,512]{0,1:T(8,128)(2,1)}, bf16[512,512]{1,0:T(8,128)(2,1)}, bf16[51...) all-reduce(f32[512,512]{1,0:T(8,128)} %fusion.78, ...), channel_id=1, replica_groups=mesh['room'=4,'geom'=32] {'room','geom'}, use_global_device_ids=true, to_apply=%region_18.19 | all-reduce | flops 2098176 | bytes 12589056 | tf_op jit(solution)/shard_map/psum | solution.py:191
  821.1 2.0 copy.21
  823.2 2.0 copy.22
  (210 shorter events, 23.8 us)
Async XLA Ops:
  7.2 311.6 %copy-start = (bf16[512,1024]{1,0:T(8,128)(2,1)S(1)}, bf16[512,1024]{1,0:T(8,128)(2,1)}, u32[]{:S(2)}) copy-start(bf16[512,1024]{1,0:T(8,128)(2,1)} %param.20) | copy-start | bytes 3145732
  7.2 6.6 copy-start.19
  7.2 6.5 copy-start.82
  7.2 6.6 copy-start.30
  7.2 6.6 copy-start.45
  7.2 144.3 %all-gather.3.cloned.1.call-start = ((), (), s32[]{:S(2)}) async-start(), calls=%async_computation.2 | async-start | bytes 4325376 | tf_op jit(solution)/shard_map/all_gather | solution.py:153
  9.4 301.6 %all-gather.5.cloned.1.call-start = ((), (), s32[]{:S(2)}) async-start(), calls=%async_computation.3 | async-start | bytes 4325376 | tf_op jit(solution)/shard_map/all_gather | solution.py:154
  11.5 494.0 %reduce-scatter.5.cloned.1.call-start = ((), (), s32[]{:S(2)}) async-start(), calls=%async_computation.5 | async-start | bytes 8650752 | tf_op jit(solution)/shard_map/reduce_scatter | solution.py:171
  12.6 142.7 %copy-start.47 = (f32[128]{0:T(128)}, f32[128]{0:T(128)S(1)}, u32[]{:S(2)}) copy-start(f32[128]{0:T(128)S(1)} %broadcast_multiply_fusion.3) | copy-start | bytes 1540
  13.7 141.5 %copy-start.62 = (f32[128]{0:T(128)}, f32[128]{0:T(128)S(1)}, u32[]{:S(2)}) copy-start(f32[128]{0:T(128)S(1)} %add_rsqrt_fusion.1) | copy-start | bytes 1540
  14.1 144.5 %copy-start.24 = (bf16[128,512]{1,0:T(8,128)(2,1)}, bf16[128,512]{1,0:T(8,128)(2,1)S(1)}, u32[]{:S(2)}) copy-start(bf16[128,512]{1,0:T(8,128)(2,1)S(1)} %convolution_convert_fusion.11) | copy-start | bytes 393220
  151.5 3.7 copy-start.11
  153.4 157.6 %copy-start.58 = (f32[128]{0:T(128)}, f32[128]{0:T(128)S(1)}, u32[]{:S(2)}) copy-start(f32[128]{0:T(128)S(1)} %get-tuple-element.35) | copy-start | bytes 1540
  155.3 155.8 %copy-start.73 = (f32[128]{0:T(128)}, f32[128]{0:T(128)S(1)}, u32[]{:S(2)}) copy-start(f32[128]{0:T(128)S(1)} %fusion.5) | copy-start | bytes 1540
  155.8 157.9 %copy-start.55 = (f32[128]{0:T(128)}, f32[128]{0:T(128)S(1)}, u32[]{:S(2)}) copy-start(f32[128]{0:T(128)S(1)} %get-tuple-element.33) | copy-start | bytes 1540
  157.5 156.2 %copy-start.70 = (f32[128]{0:T(128)}, f32[128]{0:T(128)S(1)}, u32[]{:S(2)}) copy-start(f32[128]{0:T(128)S(1)} %fusion.7) | copy-start | bytes 1540
  158.1 157.5 %copy-start.52 = (f32[128]{0:T(128)}, f32[128]{0:T(128)S(1)}, u32[]{:S(2)}) copy-start(f32[128]{0:T(128)S(1)} %get-tuple-element.31) | copy-start | bytes 1540
  158.6 157.0 %copy-start.67 = (f32[128]{0:T(128)}, f32[128]{0:T(128)S(1)}, u32[]{:S(2)}) copy-start(f32[128]{0:T(128)S(1)} %fusion.9) | copy-start | bytes 1540
  159.4 157.8 %copy-start.49 = (f32[128]{0:T(128)}, f32[128]{0:T(128)S(1)}, u32[]{:S(2)}) copy-start(f32[128]{0:T(128)S(1)} %get-tuple-element.29) | copy-start | bytes 1540
  159.8 157.3 %copy-start.64 = (f32[128]{0:T(128)}, f32[128]{0:T(128)S(1)}, u32[]{:S(2)}) copy-start(f32[128]{0:T(128)S(1)} %fusion.11) | copy-start | bytes 1540
  311.0 3.8 copy-start.78
  314.8 3.1 copy-start.36
  329.0 353.8 %reduce-scatter.3.cloned.1.call-start = ((), (), s32[]{:S(2)}) async-start(), calls=%async_computation.4 | async-start | bytes 8650752 | tf_op jit(solution)/shard_map/reduce_scatter | solution.py:170
  347.8 3.9 copy-start.16
  347.9 3.9 copy-start.12
  354.0 3.3 copy-start.22
  354.0 3.3 copy-start.33
  355.8 3.3 copy-start.81
  357.2 148.3 %copy-start.23 = (bf16[1,128,512]{2,1,0:T(8,128)(2,1)S(1)}, bf16[1,128,512]{2,1,0:T(8,128)(2,1)}, u32[]{:S(2)}) copy-start(bf16[1,128,512]{2,1,0:T(8,128)(2,1)} %param.13) | copy-start | bytes 393220
  359.1 326.3 %copy-start.46 = (f32[512]{0:T(512)S(1)}, f32[512]{0:T(512)}, u32[]{:S(2)}) copy-start(f32[512]{0:T(512)} %get-tuple-element.18) | copy-start | bytes 6148
  359.1 326.3 %copy-start.77 = (f32[512]{0:T(512)S(1)}, f32[512]{0:T(512)}, u32[]{:S(2)}) copy-start(f32[512]{0:T(512)} %fusion.14) | copy-start | bytes 6148
  685.4 139.8 %copy-start.1 = (bf16[512,1024]{1,0:T(8,128)(2,1)S(1)}, bf16[512,1024]{1,0:T(8,128)(2,1)}, u32[]{:S(2)}) copy-start(bf16[512,1024]{1,0:T(8,128)(2,1)} %param.20) | copy-start | bytes 3145732
  (55 other events, 85.8 us)
Sparse Core Ops, SparseCore 0:
  10.3 141.1 all-gather.2
  153.7 157.2 all-gather.4
  329.1 176.3 reduce-scatter.4
  507.8 174.9 reduce-scatter.2
where the time goes:
time: 833 us; the launch traced here: 832 us
  waiting for transfers between devices  609 us (73%)
  blocking collectives  136 us (16%)
  matrix products  41.5 us (5%)
  local copies, waits for them, and re-layouts  16 us (2%)
  between operations  14.8 us (2%)
  other arithmetic  14.5 us (2%)
    reduce_scatter x1, waiting for transfers between devices, local(): lax.psum_scatter(partial_keys.astype(jnp.float32), 'geom', scatter_dimens...  175 us
    all_gather x1, waiting for transfers between devices, local(): lax.all_gather(local_values, 'geom', axis=0, tiled=True)  151 us
    reduce_scatter x1, waiting for transfers between devices, local(): lax.psum_scatter(partial_values.astype(jnp.float32), 'geom', scatter_dime...  145 us
    all_gather x1, waiting for transfers between devices, local(): lax.all_gather(local_keys, 'geom', axis=0, tiled=True)  137 us
    psum x1, blocking collectives, local(): lax.psum((grad_query, grad_key, grad_value, grad_out, grad_up, grad_down,...  136 us
  transfers between devices with their start and end apart: 4, of which 4 were waited for; matrix products, arithmetic and copies ran while one was open for 5% of the time, Pallas kernels for 0%

commit v1 on v0

v1 whole, which is shorter than its diff:
```python
import math

import jax
import jax.numpy as jnp
from jax import lax
from jax.sharding import Mesh, PartitionSpec as P

HEADS = 4
BLK = 128
EPSILON = 1e-05
GELU_COEF = math.sqrt(2.0 / math.pi)

AXES = ("x_hi", "core", "z", "x_lo", "y")
ROOM = ("x_hi", "core")
GEOM = ("z", "x_lo", "y")


def normalize(inputs, gain):
    center = inputs - jnp.mean(inputs, axis=-1, keepdims=True)
    inverse = lax.rsqrt(jnp.mean(center * center, axis=-1, keepdims=True) + EPSILON)
    scaled = center * inverse
    return (scaled, inverse, scaled * gain)


def gelu_pair(inputs):
    inner = GELU_COEF * (inputs + 0.044715 * inputs * inputs * inputs)
    tangent = jnp.tanh(inner)
    value = 0.5 * inputs * (1.0 + tangent)
    slope = 0.5 * (1.0 + tangent) + 0.5 * inputs * (1.0 - tangent * tangent) * GELU_COEF * (
        1.0 + 3.0 * 0.044715 * inputs * inputs
    )
    return (value, slope)


def mult(left, right):
    return jnp.dot(left, right, preferred_element_type=jnp.float32)


def mult_nt(left, right):
    return lax.dot_general(
        left, right, (((1,), (1,)), ((), ())), preferred_element_type=jnp.float32
    )


def mult_tn(left, right):
    return lax.dot_general(
        left, right, (((0,), (0,)), ((), ())), preferred_element_type=jnp.float32
    )


def two_parts(value):
    high = value.astype(jnp.bfloat16)
    low = (value - high.astype(jnp.float32)).astype(jnp.bfloat16)
    return high, low


def device_step(
    queries,
    visible,
    cotangent,
    feats,
    w_query,
    w_key,
    w_value,
    w_out,
    w_up,
    w_down,
    gain_attn,
    gain_mlp,
):
    head = w_query.shape[1] // HEADS
    rows = queries.shape[0]
    factor = 1.0 / math.sqrt(head)
    allowed = jnp.repeat(jnp.repeat(visible > 0, BLK, axis=0), BLK, axis=1)
    inputs = queries.astype(jnp.float32)
    scaled_one, _, normed = normalize(inputs, gain_attn)
    normed_b = normed.astype(jnp.bfloat16)
    query_rows = mult(normed_b, w_query).astype(jnp.bfloat16)
    key_rows = mult(feats, w_key).astype(jnp.bfloat16)
    cols = [slice(h * head, (h + 1) * head) for h in range(HEADS)]
    scores = []
    for c in cols:
        part = mult_nt(query_rows[:, c], key_rows[:, c]) * factor
        scores.append(jnp.where(allowed, part, -1e30))
    scores = jnp.concatenate(scores, axis=0)
    expo = jnp.exp(scores - jnp.max(scores, axis=-1, keepdims=True))
    attend = expo / jnp.sum(expo, axis=-1, keepdims=True)
    attend_b = attend.astype(jnp.bfloat16)
    u_high, u_low = two_parts(mult(attend_b, feats))
    heads = [slice(h * rows, (h + 1) * rows) for h in range(HEADS)]
    context = jnp.concatenate(
        [mult(u_high[r], w_value[:, c]) + mult(u_low[r], w_value[:, c]) for r, c in zip(heads, cols)],
        axis=1,
    ).astype(jnp.bfloat16)
    mixed = inputs + mult(context, w_out)
    scaled_two, inverse_two, normed_two = normalize(mixed, gain_mlp)
    normed_two_b = normed_two.astype(jnp.bfloat16)
    activated, slope = gelu_pair(mult(normed_two_b, w_up))
    activated_b = activated.astype(jnp.bfloat16)
    output = (mixed + mult(activated_b, w_down)).astype(jnp.bfloat16)
    grad_down = mult_tn(activated_b, cotangent)
    grad_upper_b = (mult_nt(cotangent, w_down) * slope).astype(jnp.bfloat16)
    grad_up = mult_tn(normed_two_b, grad_upper_b)
    grad_normed_two = mult_nt(grad_upper_b, w_up)
    grad_gain_mlp = jnp.sum(grad_normed_two * scaled_two, axis=0)
    grad_scaled = grad_normed_two * gain_mlp
    mean_one = jnp.mean(grad_scaled, axis=-1, keepdims=True)
    mean_two = jnp.mean(grad_scaled * scaled_two, axis=-1, keepdims=True)
    grad_mixed = cotangent.astype(jnp.float32) + inverse_two * (
        grad_scaled - mean_one - scaled_two * mean_two
    )
    grad_mixed_b = grad_mixed.astype(jnp.bfloat16)
    grad_out = mult_tn(context, grad_mixed_b)
    grad_context = mult_nt(grad_mixed_b, w_out).astype(jnp.bfloat16)
    grad_value = jnp.concatenate(
        [
            mult_tn(u_high[r], grad_context[:, c]) + mult_tn(u_low[r], grad_context[:, c])
            for r, c in zip(heads, cols)
        ],
        axis=1,
    )
    pulled = jnp.concatenate(
        [mult_nt(grad_context[:, c], w_value[:, c]) for c in cols], axis=0
    ).astype(jnp.bfloat16)
    grad_attend = mult_nt(pulled, feats)
    centre = jnp.sum(attend * grad_attend, axis=-1, keepdims=True)
    grad_scores = (attend * (grad_attend - centre) * factor).astype(jnp.bfloat16)
    t_high, t_low = two_parts(mult(grad_scores, feats))
    grad_query_rows = jnp.concatenate(
        [mult(t_high[r], w_key[:, c]) + mult(t_low[r], w_key[:, c]) for r, c in zip(heads, cols)],
        axis=1,
    ).astype(jnp.bfloat16)
    grad_key = jnp.concatenate(
        [
            mult_tn(t_high[r], query_rows[:, c]) + mult_tn(t_low[r], query_rows[:, c])
            for r, c in zip(heads, cols)
        ],
        axis=1,
    )
    grad_query = mult_tn(normed_b, grad_query_rows)
    grad_normed = mult_nt(grad_query_rows, w_query)
    grad_gain_attn = jnp.sum(grad_normed * scaled_one, axis=0)
    return output, (
        grad_query,
        grad_key,
        grad_value,
        grad_out,
        grad_up,
        grad_down,
        grad_gain_attn,
        grad_gain_mlp,
    )


def local(
    queries,
    features,
    visible,
    cotangent,
    w_query,
    w_key,
    w_value,
    w_out,
    w_up,
    w_down,
    gain_attn,
    gain_mlp,
):
    own = features[0]
    many = visible.shape[-1]
    feats = lax.all_to_all(
        jnp.broadcast_to(own[None], (many,) + own.shape), GEOM, 0, 0, tiled=True
    ).reshape(many * own.shape[0], own.shape[1])
    output, grads = device_step(
        queries[0],
        visible[0],
        cotangent[0],
        feats,
        w_query,
        w_key,
        w_value,
        w_out,
        w_up,
        w_down,
        gain_attn,
        gain_mlp,
    )
    totals = lax.psum(grads, AXES)
    return (output[None],) + tuple(piece.astype(jnp.bfloat16) for piece in totals)


def solution(mesh):
    parts = Mesh(mesh.devices.reshape(2, 2, 4, 2, 4), AXES)
    split = P(ROOM, GEOM, None)
    return jax.shard_map(
        local,
        mesh=parts,
        in_specs=(split,) * 4 + (P(),) * 8,
        out_specs=(split,) + (P(),) * 8,
        check_vma=False,
    )
```

time: 833 us -> 238 us (0.29)
  waiting for transfers between devices: 609 us -> 52.8 us
  blocking collectives: 136 us -> 117 us
  between operations: 14.8 us -> 1.24 us
  starting transfers between devices: 0.34 us -> 10.1 us
    reduce_scatter x2 -> x0, waiting for transfers between devices: 320 us -> none  [the longest x1 175 us: local(): lax.psum_scatter(partial_keys.astype(jnp.float32), 'geom', scatter_dimens...]
    all_gather x2 -> x0, waiting for transfers between devices: 289 us -> none  [the longest x1 151 us: local(): lax.all_gather(local_values, 'geom', axis=0, tiled=True)]
    all_to_all x0 -> x1, waiting for transfers between devices: none -> 52.8 us  [local(): lax.all_to_all(jnp.broadcast_to(own[None], (many,) + own.shape), GEOM, 0,...]
    psum x1, blocking collectives: 136 us -> 117 us  [local(): totals = lax.psum(grads, AXES)]
    unnamed x168 -> x30, local copies, waits for them, and re-layouts: 15.9 us -> 4.17 us
    convert_element_type x6 -> x0, other arithmetic: 10.3 us -> none  [the longest x1 3.83 us: local(): partial_keys.astype(jnp.float32)]
    all_to_all x0 -> x1, starting transfers between devices: none -> 10.1 us  [local(): lax.all_to_all(jnp.broadcast_to(own[None], (many,) + own.shape), GEOM, 0,...]
    dot_general x16 -> x23, matrix products: 21.1 us -> 19.4 us  [mult(): return jnp.dot(left, right, preferred_element_type=jnp.float32)]
  transfers between devices with their start and end apart: 4 -> 1, of which waited for: 4 -> 1; matrix products, arithmetic and copies ran while one was open for 5% -> 0% of each run, Pallas kernels for 0% -> 0%
where the time goes in v1:
time: 238 us; the launch traced here: 236 us
  blocking collectives  117 us (49%)
  waiting for transfers between devices  52.8 us (22%)
  matrix products  37.2 us (16%)
  starting transfers between devices  10.1 us (4%)
  other arithmetic  10 us (4%)
  local copies, waits for them, and re-layouts  7.68 us (3%)
    psum x1, blocking collectives, local(): totals = lax.psum(grads, AXES)  117 us
    all_to_all x1, waiting for transfers between devices, local(): lax.all_to_all(jnp.broadcast_to(own[None], (many,) + own.shape), GEOM, 0,...  52.8 us
    dot_general x23, matrix products, mult(): return jnp.dot(left, right, preferred_element_type=jnp.float32)  19.4 us
    all_to_all x1, starting transfers between devices, local(): lax.all_to_all(jnp.broadcast_to(own[None], (many,) + own.shape), GEOM, 0,...  10.1 us
    dot_general x13, matrix products, mult_nt(): lax.dot_general(left, right, (((1,), (1,)), ((), ())), preferred_element_...  9.03 us
    dot_general x20, matrix products, mult_tn(): lax.dot_general(left, right, (((0,), (0,)), ((), ())), preferred_element_...  8.84 us
    div x1, other arithmetic, device_step(): attend = expo / jnp.sum(expo, axis=-1, keepdims=True)  5.31 us
  transfers between devices with their start and end apart: 1, of which 1 were waited for; matrix products, arithmetic and copies ran while one was open for 0% of the time, Pallas kernels for 0%

profile of v1, /device:TPU:1, one launch (start us, length us, event | category | flops | bytes accessed | tf_op | source)
XLA Modules:
  0.0 236.3 jit_solution(14405453402815862925)
XLA Ops:
  0.7 3.4 %broadcast_in_dim.41 = bf16[32,128,512]{2,1,0:T(8,128)(2,1)} broadcast(bf16[128,512]{1,0:T(8,128)(2,1)} %bitcast.51), dimensions={1,2} | broadcast | bytes 4325376 | tf_op jit(solution)/shard_map/broadcast_in_dim | solution.py:172
  4.1 10.1 %all-to-all-start = ((bf16[32,128,512]{2,1,0:T(8,128)(2,1)}), bf16[32,128,512]{2,1,0:T(8,128)(2,1)}, u32[]{:S(2)}, u32[]{:S(2)}) async-start(bf16[32,128,512]{2,1,0:T(8,128)(2,1)} %broadcast_in_dim.41), calls=%async_computation | async-start | bytes 8388608 | tf_op jit(solution)/shard_map/all_to_all | solution.py:171
  14.6 0.3 convolution_convert_fusion.2
  14.9 52.8 %all-to-all-done = bf16[32,128,512]{2,1,0:T(8,128)(2,1)} async-done(((bf16[32,128,512]{2,1,0:T(8,128)(2,1)}), bf16[32,128,512]{2,1,0:T(8,128)(2,1)}, u32[]{:S(2)}, u32[]{:S(2)}) %all-to-all-start) | async-done | bytes 4194336 | tf_op jit(solution)/shard_map/all_to_all | solution.py:171
  67.8 4.5 %convolution_convert_fusion = bf16[4096,512]{1,0:T(8,128)(2,1)S(1)} fusion(bf16[4096,512]{1,0:T(8,128)(2,1)} %bitcast.4, bf16[512,512]{1,0:T(8,128)(2,1)S(1)} %copy-done.4), kind=kOutput, calls=%fused_computation.6 | convolution fusion | flops 2149580800 | bytes 8912896 | tf_op jit(solution)/shard_map/dot_general | solution.py:36
  72.3 0.5 fusion.3
  72.8 0.5 fusion.4
  73.2 0.5 fusion.5
  73.7 0.5 fusion.2
  74.2 0.6 fusion.11
  74.7 1.4 fusion.1
  76.1 5.3 %fusion = f32[512,4096]{1,0:T(8,128)S(1)} fusion(f32[512]{0:T(512)S(1)} %fusion.1, f32[512]{0:T(512)S(1)} %fusion.11, f32[128,4096]{1,0:T(8,128)S(1)} %fusion.2, f32[128,4096]{1,0:T(8,128)S(1)} %fusion.3, f32[128,4096]{1,0:T(8,128)S(1)} %fusion.4, f32[128,4096]{1,0:T(8,128)S(1)} %fusion.5), kind=kLoop, calls=%fused_computation.4 | loop fusion | flops 10485760 | bytes 16781312 | tf_op jit(solution)/shard_map/div | solution.py:87
  81.5 4.6 %subtract_convert_fusion.1 = (bf16[512,512]{1,0:T(8,128)(2,1)S(1)}, bf16[512,512]{1,0:T(8,128)(2,1)S(1)}) fusion(bf16[4096,512]{1,0:T(8,128)(2,1)} %bitcast.4, f32[512,4096]{1,0:T(8,128)S(1)} %fusion), kind=kOutput, calls=%fused_computation.66 | convolution fusion | flops 2150629376 | bytes 13631488 | tf_op jit(solution)/shard_map/dot_general | solution.py:36
  88.0 0.3 fusion.154
  88.6 0.4 fusion.153
  89.0 0.6 fusion.12
  89.6 0.6 multiply_reduce_fusion.1
  90.3 0.3 convolution_convert_fusion.1
  91.4 4.6 %multiply_reduce_fusion = (f32[512]{0:T(512)S(1)}, f32[512,4096]{1,0:T(8,128)S(1)}) fusion(f32[512,4096]{1,0:T(8,128)S(1)} %fusion, bf16[4096,512]{1,0:T(8,128)(2,1)} %bitcast.4, bf16[128,512]{1,0:T(8,128)(2,1)S(1)} %convolution_convert_fusion.3, bf16[128,512]{1,0:T(8,128)(2,1)S(1)} %convolution_convert_fusion.4, ...), kind=kOutput, calls=%fused_computation.2 | convolution fusion | flops 2153774592 | bytes 21497856 | tf_op jit(solution)/shard_map/dot_general | solution.py:40
  96.1 4.6 %subtract_convert_fusion = (bf16[512,512]{1,0:T(8,128)(2,1)S(1)}, bf16[512,512]{1,0:T(8,128)(2,1)S(1)}) fusion(bf16[4096,512]{1,0:T(8,128)(2,1)} %bitcast.4, f32[512,4096]{1,0:T(8,128)S(1)} %fusion, f32[512,4096]{1,0:T(8,128)S(1)} %get-tuple-element.38, f32[512]{0:T(512)S(1)} %get-tuple-element.37), kind=kOutput, calls=%fused_computation.65 | convolution fusion | flops 2156920832 | bytes 22022144 | tf_op jit(solution)/shard_map/dot_general | solution.py:36
  101.6 0.5 fusion.152
  102.2 1.3 fusion.143
  106.3 0.3 fusion.14
  106.6 1.4 fusion.142
  108.0 1.8 fusion.47
  109.8 1.0 fusion.15
  111.8 1.0 pad_maximum_fusion.2
  113.0 0.4 convolution_add_fusion.6
  113.9 1.1 pad_maximum_fusion.1
  115.0 117.3 %all-reduce.2 = (bf16[512,512]{1,0:T(8,128)(2,1)}, bf16[512,512]{0,1:T(8,128)(2,1)}, bf16[512,512]{0,1:T(8,128)(2,1)}, bf16[512,512]{1,0:T(8,128)(2,1)}, bf16[51...) all-reduce(f32[512,512]{1,0:T(8,128)} %fusion.142, ...), channel_id=1, replica_groups=mesh['x_hi'=2,'core'=2,'z'=4,'x_lo'=2,'y'=4] {'x_hi','core','z','x_lo','y'}, use_global_device_ids=true, to_apply=%region_9.10 | all-reduce | flops 2098176 | bytes 12589056 | tf_op jit(solution)/shard_map/psum | solution.py:188
  232.3 2.0 copy.21
  234.3 2.0 copy.22
  (74 shorter events, 8.6 us)
Async XLA Ops:
  0.6 87.9 %copy-start = (bf16[512,1024]{1,0:T(8,128)(2,1)S(1)}, bf16[512,1024]{1,0:T(8,128)(2,1)}, u32[]{:S(2)}) copy-start(bf16[512,1024]{1,0:T(8,128)(2,1)} %param.20) | copy-start | bytes 3145732
  4.1 10.1 %copy-start.2 = (bf16[1,128,512]{2,1,0:T(8,128)(2,1)S(1)}, bf16[1,128,512]{2,1,0:T(8,128)(2,1)}, u32[]{:S(2)}) copy-start(bf16[1,128,512]{2,1,0:T(8,128)(2,1)} %param.12) | copy-start | bytes 393220
  4.1 10.4 %copy-start.13 = (s32[1,1,32]{2,1,0:T(1,128)S(1)}, s32[1,1,32]{2,1,0:T(1,128)}, u32[]{:S(2)}) copy-start(s32[1,1,32]{2,1,0:T(1,128)} %param.14) | copy-start | bytes 388
  4.1 10.5 %copy-start.6 = (bf16[512,512]{1,0:T(8,128)(2,1)S(1)}, bf16[512,512]{1,0:T(8,128)(2,1)}, u32[]{:S(2)}) copy-start(bf16[512,512]{1,0:T(8,128)(2,1)} %param.16) | copy-start | bytes 1572868
  4.1 10.5 %copy-start.10 = (f32[512]{0:T(512)S(1)}, f32[512]{0:T(512)}, u32[]{:S(2)}) copy-start(f32[512]{0:T(512)} %param.22) | copy-start | bytes 6148
  4.1 63.7 %copy-start.4 = (bf16[512,512]{1,0:T(8,128)(2,1)S(1)}, bf16[512,512]{1,0:T(8,128)(2,1)}, u32[]{:S(2)}) copy-start(bf16[512,512]{1,0:T(8,128)(2,1)} %param.17) | copy-start | bytes 1572868
  4.1 63.6 %all-to-all-start = ((bf16[32,128,512]{2,1,0:T(8,128)(2,1)}), bf16[32,128,512]{2,1,0:T(8,128)(2,1)}, u32[]{:S(2)}, u32[]{:S(2)}) async-start(bf16[32,128,512]{2,1,0:T(8,128)(2,1)} %broadcast_in_dim.41), calls=%async_computation | async-start | bytes 8388608 | tf_op jit(solution)/shard_map/all_to_all | solution.py:171
  81.4 4.7 %copy-start.1 = (bf16[512,512]{1,0:T(8,128)(2,1)S(1)}, bf16[512,512]{1,0:T(8,128)(2,1)}, u32[]{:S(2)}) copy-start(bf16[512,512]{1,0:T(8,128)(2,1)} %param.18) | copy-start | bytes 1572868
  81.5 6.6 %copy-start.3 = (bf16[512,512]{1,0:T(8,128)(2,1)S(1)}, bf16[512,512]{1,0:T(8,128)(2,1)}, u32[]{:S(2)}) copy-start(bf16[512,512]{1,0:T(8,128)(2,1)} %param.19) | copy-start | bytes 1572868
  81.5 7.1 %copy-start.9 = (f32[512]{0:T(512)S(1)}, f32[512]{0:T(512)}, u32[]{:S(2)}) copy-start(f32[512]{0:T(512)} %param.23) | copy-start | bytes 6148
  86.1 2.9 %copy-start.8 = (bf16[1,128,512]{2,1,0:T(8,128)(2,1)S(1)}, bf16[1,128,512]{2,1,0:T(8,128)(2,1)}, u32[]{:S(2)}) copy-start(bf16[1,128,512]{2,1,0:T(8,128)(2,1)} %param.15) | copy-start | bytes 393220
  86.1 2.9 %copy-start.11 = (bf16[1024,512]{1,0:T(8,128)(2,1)S(1)}, bf16[1024,512]{1,0:T(8,128)(2,1)}, u32[]{:S(2)}) copy-start(bf16[1024,512]{1,0:T(8,128)(2,1)} %param.21) | copy-start | bytes 3145732
  100.9 4.4 %copy-start.5 = (bf16[512,512]{1,0:T(8,128)(2,1)S(1)}, bf16[512,512]{1,0:T(8,128)(2,1)}, u32[]{:S(2)}) copy-start(bf16[512,512]{1,0:T(8,128)(2,1)} %param.17) | copy-start | bytes 1572868
  101.6 4.6 %copy-start.7 = (bf16[512,512]{1,0:T(8,128)(2,1)S(1)}, bf16[512,512]{1,0:T(8,128)(2,1)}, u32[]{:S(2)}) copy-start(bf16[512,512]{1,0:T(8,128)(2,1)} %param.16) | copy-start | bytes 1572868
  104.4 5.4 %copy-start.12 = (bf16[1024,512]{1,0:T(8,128)(2,1)S(1)}, bf16[1024,512]{1,0:T(8,128)(2,1)}, u32[]{:S(2)}) copy-start(bf16[1024,512]{1,0:T(8,128)(2,1)} %param.21) | copy-start | bytes 3145732

commit v2 on v1

--- a/solution.py
+++ b/solution.py
@@ -2,7 +2,10 @@
 
 import jax
 import jax.numpy as jnp
+import numpy as np
 from jax import lax
+from jax.experimental import pallas as pl
+from jax.experimental.pallas import tpu as pltpu
 from jax.sharding import Mesh, PartitionSpec as P
 
 HEADS = 4
@@ -11,8 +14,43 @@
 GELU_COEF = math.sqrt(2.0 / math.pi)
 
 AXES = ("x_hi", "core", "z", "x_lo", "y")
+SIZES = (2, 2, 4, 2, 4)
 ROOM = ("x_hi", "core")
 GEOM = ("z", "x_lo", "y")
+VMEM = pl.BlockSpec(memory_space=pltpu.VMEM)
+SMEM = pl.BlockSpec(memory_space=pltpu.SMEM)
+
+
+def pairs_of(move):
+    pairs = []
+    for source in range(math.prod(SIZES)):
+        target = move(*(int(i) for i in np.unravel_index(source, SIZES)))
+        pairs.append((source, int(np.ravel_multi_index(target, SIZES))))
+    return pairs
+
+
+SWAP = pairs_of(lambda xh, c, z, xl, y: (xh, xl, z, c, y))
+CORE = pairs_of(lambda xh, c, z, xl, y: (xh, 1 - c, z, xl, y))
+
+
+def first(mask):
+    return pairs_of(
+        lambda xh, c, z, xl, y: (xh, c, z, xl, y ^ mask) if c == 0 else (xh, c, z ^ mask, xl, y)
+    )
+
+
+def second(mask):
+    return pairs_of(
+        lambda xh, c, z, xl, y: (xh, c, z ^ mask, xl, y) if c == 0 else (xh, c, z, xl, y ^ mask)
+    )
+
+
+def along_x(mask):
+    return pairs_of(lambda xh, c, z, xl, y: (xh ^ (mask >> 1), c, z, xl ^ (mask & 1), y))
+
+
+def send(value, pairs):
+    return lax.ppermute(value, AXES, pairs)
 
 
 def normalize(inputs, gain):
@@ -71,7 +109,7 @@
     head = w_query.shape[1] // HEADS
     rows = queries.shape[0]
     factor = 1.0 / math.sqrt(head)
-    allowed = jnp.repeat(jnp.repeat(visible > 0, BLK, axis=0), BLK, axis=1)
+    allowed = jnp.repeat(visible > 0, BLK)[None, :]
     inputs = queries.astype(jnp.float32)
     scaled_one, _, normed = normalize(inputs, gain_attn)
     normed_b = normed.astype(jnp.bfloat16)
@@ -152,6 +190,178 @@
     )
 
 
+PIECES = 32
+CHUNK = 128
+TAIL = 16
+
+
+def pieces_of(refs, k):
+    query, key, value, out, up, down = refs
+    rows = pl.ds(pl.multiple_of(k * 16, 16), 16)
+    return (
+        (0, query.at[rows, :]),
+        (16, key.at[rows, :]),
+        (32, value.at[rows, :]),
+        (48, out.at[rows, :]),
+        (64, up.at[rows, pl.ds(0, 512)]),
+        (80, up.at[rows, pl.ds(512, 512)]),
+        (96, down.at[pl.ds(pl.multiple_of(k * 32, 32), 32), :]),
+    )
+
+
+def put_gains(ref, at, gains):
+    high = gains.astype(jnp.bfloat16)
+    low = (gains - high.astype(jnp.float32)).astype(jnp.bfloat16)
+    ref[at : at + TAIL, :] = jnp.concatenate([high, low], axis=0)
+
+
+def take_gains(ref, at):
+    tail = ref[at : at + TAIL, :].astype(jnp.float32)
+    return tail[: TAIL // 2] + tail[TAIL // 2 :]
+
+
+def halves_kernel(core_ref, *refs):
+    grads, gains, give, keep = refs[:6], refs[6], refs[7], refs[8]
+    core = core_ref[0]
+    half = PIECES // 2
+
+    def step(i, carry):
+        row = pl.multiple_of(i * CHUNK, CHUNK)
+        for at, piece in pieces_of(grads, (1 - core) * half + i):
+            give[pl.ds(row + at, piece.shape[0]), :] = piece[...].astype(jnp.bfloat16)
+        for at, piece in pieces_of(grads, core * half + i):
+            keep[pl.ds(row + at, piece.shape[0]), :] = piece[...]
+        return carry
+
+    lax.fori_loop(0, half, step, 0)
+    put_gains(give, half * CHUNK, gains[...])
+
+
+def quarters_kernel(many, index_ref, own_ref, gains_ref, *refs):
+    arrived, gives, keep, gains_out = refs[:many], refs[many : many + 3], refs[many + 3], refs[many + 4]
+    index = index_ref[0]
+    rows = keep.shape[0]
+    total = own_ref.shape[0]
+    for mask in range(4):
+        at = pl.ds(pl.multiple_of((index ^ mask) * rows, rows), rows)
+        value = own_ref[at, :]
+        for ref in arrived:
+            value = value + ref[at, :].astype(jnp.float32)
+        if mask:
+            gives[mask - 1][0:rows, :] = value.astype(jnp.bfloat16)
+        else:
+            keep[...] = value
+    gains = add_gains(gains_ref[...], [take_gains(ref, total) for ref in arrived])
+    for give in gives:
+        put_gains(give, rows, gains)
+    gains_out[...] = gains
+
+
+def add_gains(own, arrived):
+    high = own.astype(jnp.bfloat16).astype(jnp.float32)
+    own = high + (own - high).astype(jnp.bfloat16).astype(jnp.float32)
+    if len(arrived) == 1:
+        return own + arrived[0]
+    return (own + arrived[0]) + (arrived[1] + arrived[2])
+
+
+def chunk_kernel(own_ref, gains_ref, *refs):
+    arrived, give = refs[:3], refs[3]
+    rows = own_ref.shape[0]
+    value = own_ref[...]
+    for ref in arrived:
+        value = value + ref[0:rows, :].astype(jnp.float32)
+    give[0:rows, :] = value.astype(jnp.bfloat16)
+    put_gains(give, rows, add_gains(gains_ref[...], [take_gains(ref, rows) for ref in arrived]))
+
+
+def last_kernel(own_ref, *refs):
+    arrived, chunk, gains = refs[:3], refs[3], refs[4]
+    rows = chunk.shape[0]
+    a, b, c, d = (ref[0:rows, :].astype(jnp.float32) for ref in (own_ref, *arrived))
+    chunk[...] = ((a + b) + (c + d)).astype(jnp.bfloat16)
+    a, b, c, d = (take_gains(ref, rows) for ref in (own_ref, *arrived))
+    put_gains(gains, 0, (a + b) + (c + d))
+
+
+def place_kernel(where_ref, *refs):
+    own, other, gains_own, gains_other = refs[0:4], refs[4:8], refs[8], refs[9]
+    grads, gains_out = refs[10:16], refs[16]
+    core, y, z = where_ref[0], where_ref[1], where_ref[2]
+    for side, group in enumerate((own, other)):
+        holder = core ^ side
+        one = jnp.where(holder == 0, y, z)
+        two = jnp.where(holder == 0, z, y)
+        for m1 in range(4):
+            for m2 in range(4):
+                k = holder * 16 + (one ^ m1) * 4 + (two ^ m2)
+                for at, piece in pieces_of(grads, k):
+                    piece[...] = group[m1][m2 * CHUNK + at : m2 * CHUNK + at + piece.shape[0], :]
+    gains = jnp.where(core == 0, take_gains(gains_own, 0), take_gains(gains_other, 0))
+    gains_out[...] = gains.astype(jnp.bfloat16)
+
+
+def call(kernel, outs, *operands, scalars=0):
+    return pl.pallas_call(
+        kernel,
+        out_shape=[jax.ShapeDtypeStruct(shape, dtype) for shape, dtype in outs],
+        in_specs=[SMEM] * scalars + [VMEM] * (len(operands) - scalars),
+        out_specs=[VMEM] * len(outs),
+        compiler_params=pltpu.CompilerParams(vmem_limit_bytes=48 << 20),
+    )(*operands)
+
+
+def sum_everywhere(grads):
+    weights, (gain_attn, gain_mlp) = grads[:6], grads[6:]
+    core, y, z = (lax.axis_index(name) for name in ("core", "y", "z"))
+    gains = jnp.concatenate([gain_attn[None], gain_mlp[None], jnp.zeros((6, 512), jnp.float32)])
+    core_at = jnp.asarray(core, jnp.int32).reshape(1)
+    one_at = jnp.where(core == 0, y, z).astype(jnp.int32).reshape(1)
+    two_at = jnp.where(core == 0, z, y).astype(jnp.int32).reshape(1)
+    b16, f32 = jnp.bfloat16, jnp.float32
+
+    give, keep = call(
+        halves_kernel,
+        [((2048 + TAIL, 512), b16), ((2048, 512), f32)],
+        core_at, *weights, gains, scalars=1,
+    )
+    arrived = [send(give, CORE)]
+    for rows, index, route, count in ((512, one_at, first, 1), (128, two_at, second, 3)):
+        *gives, keep, gains = call(
+            lambda *refs, count=count: quarters_kernel(count, *refs),
+            [((rows + TAIL, 512), b16)] * 3 + [((rows, 512), f32), ((8, 512), f32)],
+            index, keep, gains, *arrived, scalars=1,
+        )
+        arrived = [send(give, route(mask)) for mask, give in enumerate(gives, 1)]
+    (give,) = call(chunk_kernel, [((128 + TAIL, 512), b16)], keep, gains, *arrived)
+    arrived = [send(give, along_x(mask)) for mask in (1, 2, 3)]
+    chunk, gains = call(last_kernel, [((128, 512), b16), ((TAIL, 512), b16)], give, *arrived)
+
+    mine = jnp.concatenate([chunk] + [send(chunk, second(mask)) for mask in (1, 2, 3)])
+    own = [mine] + [send(mine, first(mask)) for mask in (1, 2, 3)]
+    other = [send(part, CORE) for part in own]
+    gains_other = send(gains, CORE)
+    where = jnp.stack([core, y, z]).astype(jnp.int32)
+    *weights, gains = call(
+        place_kernel,
+        [((512, 512), b16)] * 4 + [((512, 1024), b16), ((1024, 512), b16), ((8, 512), b16)],
+        where, *own, *other, gains, gains_other, scalars=1,
+    )
+    return (*weights, gains[0], gains[1])
+
+
+def gather_features(own):
+    mine = jnp.concatenate([own] + [send(own, first(mask)) for mask in (1, 2, 3)])
+    group = [mine] + [send(mine, second(mask)) for mask in (1, 2, 3)]
+    parts = group + [send(part, CORE) for part in group]
+    core, y, z = (lax.axis_index(name) for name in ("core", "y", "z"))
+    side, two, one = (jnp.asarray(i) for i in np.unravel_index(np.arange(32), (2, 4, 4)))
+    holder = core ^ side
+    block_y = jnp.where(holder == 0, y ^ one, y ^ two)
+    block_z = jnp.where(holder == 0, z ^ two, z ^ one)
+    return parts, block_z * 8 + holder * 4 + block_y
+
+
 def local(
     queries,
     features,
@@ -166,16 +376,14 @@
     gain_attn,
     gain_mlp,
 ):
-    own = features[0]
-    many = visible.shape[-1]
-    feats = lax.all_to_all(
-        jnp.broadcast_to(own[None], (many,) + own.shape), GEOM, 0, 0, tiled=True
-    ).reshape(many * own.shape[0], own.shape[1])
+    parts, blocks = gather_features(send(features[0], SWAP))
+    moved = send(jnp.concatenate([queries[0], cotangent[0]]), SWAP)
+    seen = send(visible[0], SWAP)
     output, grads = device_step(
-        queries[0],
-        visible[0],
-        cotangent[0],
-        feats,
+        moved[:BLK],
+        jnp.take(seen[0], blocks),
+        moved[BLK:],
+        jnp.concatenate(parts),
         w_query,
         w_key,
         w_value,
@@ -185,12 +393,12 @@
         gain_attn,
         gain_mlp,
     )
-    totals = lax.psum(grads, AXES)
-    return (output[None],) + tuple(piece.astype(jnp.bfloat16) for piece in totals)
+    output = send(output, SWAP)
+    return (output[None],) + sum_everywhere(grads)
 
 
 def solution(mesh):
-    parts = Mesh(mesh.devices.reshape(2, 2, 4, 2, 4), AXES)
+    parts = Mesh(mesh.devices.reshape(SIZES), AXES)
     split = P(ROOM, GEOM, None)
     return jax.shard_map(
         local,

time: 238 us -> 182 us (0.76)
  blocking collectives: 117 us -> 0 us
  starting transfers between devices: 10.1 us -> 66.2 us
  Pallas kernels: 0 us -> 12.5 us
  matrix products: 37.2 us -> 29 us
  waiting for transfers between devices: 52.8 us -> 60.2 us
  local copies, waits for them, and re-layouts: 7.68 us -> 2.54 us
    psum x1 -> x0, blocking collectives: 117 us -> none  [local(): totals = lax.psum(grads, AXES)]
    ppermute x0 -> x35, starting transfers between devices: none -> 66.2 us  [send(): return lax.ppermute(value, AXES, pairs)]
    ppermute x0 -> x35, waiting for transfers between devices: none -> 60.2 us  [send(): return lax.ppermute(value, AXES, pairs)]
    all_to_all x1 -> x0, waiting for transfers between devices: 52.8 us -> none  [local(): lax.all_to_all(jnp.broadcast_to(own[None], (many,) + own.shape), GEOM, 0,...]
    pallas_call x0 -> x6, Pallas kernels: none -> 12.5 us  [call(): pl.pallas_call(kernel, out_shape=[jax.ShapeDtypeStruct(shape, dtype) for...]
    all_to_all x1 -> x0, starting transfers between devices: 10.1 us -> none  [local(): lax.all_to_all(jnp.broadcast_to(own[None], (many,) + own.shape), GEOM, 0,...]
    dot_general x23, matrix products: 19.4 us -> 14.2 us  [mult(): return jnp.dot(left, right, preferred_element_type=jnp.float32)]
    broadcast_in_dim x2, local copies, waits for them, and re-layouts: 3.51 us -> 0.07 us  [the longest x1 0.07 us: device_step(): scores.append(jnp.where(allowed, part, -1e+30))]
  transfers between devices with their start and end apart: 1 -> 35, of which waited for: 1 -> 21; matrix products, arithmetic and copies ran while one was open for 0% -> 3% of each run, Pallas kernels for 0% -> 0%
where the time goes in v2:
time: 182 us
  starting transfers between devices  66.2 us (36%)
  waiting for transfers between devices  60.2 us (33%)
  matrix products  29 us (16%)
  Pallas kernels  12.5 us (7%)
  other arithmetic  9.93 us (5%)
  local copies, waits for them, and re-layouts  2.54 us (1%)
    ppermute x35, starting transfers between devices, send(): return lax.ppermute(value, AXES, pairs)  66.2 us
    ppermute x35, waiting for transfers between devices, send(): return lax.ppermute(value, AXES, pairs)  60.2 us
    dot_general x23, matrix products, mult(): return jnp.dot(left, right, preferred_element_type=jnp.float32)  14.2 us
    pallas_call x6, Pallas kernels, call(): pl.pallas_call(kernel, out_shape=[jax.ShapeDtypeStruct(shape, dtype) for...  12.5 us
    dot_general x20, matrix products, mult_tn(): lax.dot_general(left, right, (((0,), (0,)), ((), ())), preferred_element_...  7.84 us
    dot_general x13, matrix products, mult_nt(): lax.dot_general(left, right, (((1,), (1,)), ((), ())), preferred_element_...  6.99 us
    div x1, other arithmetic, device_step(): attend = expo / jnp.sum(expo, axis=-1, keepdims=True)  5.31 us
  transfers between devices with their start and end apart: 35, of which 21 were waited for; matrix products, arithmetic and copies ran while one was open for 3% of the time, Pallas kernels for 0%

profile of v2, /device:TPU:1, one launch (start us, length us, event | category | flops | bytes accessed | tf_op | source)
XLA Modules:
  0.0 181.8 jit_solution(9685301433007267589)
XLA Ops:
  0.7 4.6 %collective-permute-start.2 = (bf16[128,512]{1,0:T(8,128)(2,1)}, bf16[128,512]{1,0:T(8,128)(2,1)S(1)}, u32[]{:S(2)}, u32[]{:S(2)}) collective-permute-start(bf16[128,512]{1,0:T(8,128)(2,1)} %bitcast.38), channel_id=1, source_target_pairs={{0,0},{1,1},{2,2},{3,3},{4,32},{5,33},{6,34},{7,35},{8,8},{9,9},{1... | collective-permute-start | bytes 393224 | tf_op jit(solution)/shard_map/ppermute | solution.py:53
  8.2 3.6 %collective-permute-start.1 = (s32[1,32]{1,0:T(1,128)}, s32[1,32]{1,0:T(1,128)S(1)}, u32[]{:S(2)}, u32[]{:S(2)}) collective-permute-start(s32[1,32]{1,0:T(1,128)} %bitcast.39), channel_id=1, source_target_pairs={{0,0},{1,1},{2,2},{3,3},{4,32},{5,33},{6,34},{7,35},{8,8},{9,9},{1... | collective-permute-start | bytes 392 | tf_op jit(solution)/shard_map/ppermute | solution.py:53
  16.6 3.3 %collective-permute-start.4 = (bf16[128,512]{1,0:T(8,128)(2,1)S(1)}, bf16[128,512]{1,0:T(8,128)(2,1)S(1)}, u32[]{:S(2)}, u32[]{:S(2)}) collective-permute-start(bf16[128,512]{1,0:T(8,128)(2,1)S(1)} %collective-permute-done.2), channel_id=1, source_target_pairs={{0,2},{1,3},{2,0},{3,1},{4,6},{5,7},{6,4},{7,5},{8,10},{9,11},{10,... | collective-permute-start | bytes 393224 | tf_op jit(solution)/shard_map/ppermute | solution.py:53
  20.0 3.5 %collective-permute-done.4 = bf16[128,512]{1,0:T(8,128)(2,1)S(1)} collective-permute-done((bf16[128,512]{1,0:T(8,128)(2,1)S(1)}, bf16[128,512]{1,0:T(8,128)(2,1)S(1)}, u32[]{:S(2)}, u32[]{:S(2)}) %collective-permute-start.4) | collective-permute-done | bytes 131104 | tf_op jit(solution)/shard_map/ppermute | solution.py:53
  26.6 2.7 %collective-permute-start.7 = (bf16[512,512]{1,0:T(8,128)(2,1)S(1)}, bf16[512,512]{1,0:T(8,128)(2,1)S(1)}, u32[]{:S(2)}, u32[]{:S(2)}) collective-permute-start(bf16[512,512]{1,0:T(8,128)(2,1)S(1)} %get-tuple-element.60), channel_id=1, source_target_pairs={{0,16},{1,17},{2,18},{3,19},{4,20},{5,21},{6,22},{7,23},{8,24},{9,... | collective-permute-start | bytes 1572872 | tf_op jit(solution)/shard_map/ppermute | solution.py:53
  29.6 3.9 %collective-permute-done.6 = bf16[512,512]{1,0:T(8,128)(2,1)S(1)} collective-permute-done((bf16[512,512]{1,0:T(8,128)(2,1)S(1)}, bf16[512,512]{1,0:T(8,128)(2,1)S(1)}, u32[]{:S(2)}, u32[]{:S(2)}) %collective-permute-start.6) | collective-permute-done | bytes 524320 | tf_op jit(solution)/shard_map/ppermute | solution.py:53
  34.8 6.7 %collective-permute-done.7 = bf16[512,512]{1,0:T(8,128)(2,1)S(1)} collective-permute-done((bf16[512,512]{1,0:T(8,128)(2,1)S(1)}, bf16[512,512]{1,0:T(8,128)(2,1)S(1)}, u32[]{:S(2)}, u32[]{:S(2)}) %collective-permute-start.7) | collective-permute-done | bytes 524320 | tf_op jit(solution)/shard_map/ppermute | solution.py:53
  41.6 2.5 %collective-permute-done.8 = bf16[512,512]{1,0:T(8,128)(2,1)S(1)} collective-permute-done((bf16[512,512]{1,0:T(8,128)(2,1)S(1)}, bf16[512,512]{1,0:T(8,128)(2,1)S(1)}, u32[]{:S(2)}, u32[]{:S(2)}) %collective-permute-start.8) | collective-permute-done | bytes 524320 | tf_op jit(solution)/shard_map/ppermute | solution.py:53
  46.1 2.3 %convolution_convert_fusion = bf16[4096,512]{1,0:T(8,128)(2,1)S(1)} fusion(bf16[4096,512]{1,0:T(8,128)(2,1)S(1)} %constant_dynamic-update-slice_fusion.4, bf16[512,512]{1,0:T(8,128)(2,1)S(1)} %copy-done.4), kind=kOutput, calls=%fused_computation.7 | convolution fusion | flops 2149580800 | bytes 8912896 | tf_op jit(solution)/shard_map/dot_general | solution.py:74
  52.3 5.3 %fusion = f32[512,4096]{1,0:T(8,128)S(1)} fusion(f32[512]{0:T(512)S(1)} %fusion.1, f32[512]{0:T(512)S(1)} %fusion.11, f32[128,4096]{1,0:T(8,128)S(1)} %fusion.2, f32[128,4096]{1,0:T(8,128)S(1)} %fusion.3, f32[128,4096]{1,0:T(8,128)S(1)} %fusion.4, f32[128,4096]{1,0:T(8,128)S(1)} %fusion.5), kind=kLoop, calls=%fused_computation.5 | loop fusion | flops 10485760 | bytes 16781312 | tf_op jit(solution)/shard_map/div | solution.py:125
  57.7 2.3 %subtract_convert_fusion.1 = (bf16[512,512]{1,0:T(8,128)(2,1)S(1)}, bf16[512,512]{1,0:T(8,128)(2,1)S(1)}) fusion(bf16[4096,512]{1,0:T(8,128)(2,1)S(1)} %constant_dynamic-update-slice_fusion.4, f32[512,4096]{1,0:T(8,128)S(1)} %fusion), kind=kOutput, calls=%fused_computation.66 | convolution fusion | flops 2150629376 | bytes 13631488 | tf_op jit(solution)/shard_map/dot_general | solution.py:74
  65.4 2.6 %multiply_reduce_fusion = (f32[512]{0:T(512)S(1)}, f32[512,4096]{1,0:T(8,128)S(1)}) fusion(f32[512,4096]{1,0:T(8,128)S(1)} %fusion, bf16[4096,512]{1,0:T(8,128)(2,1)S(1)} %constant_dynamic-update-slice_fusion.4, bf16[128,512]{1,0:T(8,128)(2,1)S(1)} %convolution_convert_fusion.3, bf16[128,512]{1,0:T(8,128)(2,1)S(1)} %convolution_convert_fusion.4, ...), kind=kOutput, calls=%fused_computation.3 | convolution fusion | flops 2153774592 | bytes 21497856 | tf_op jit(solution)/shard_map/dot_general | solution.py:78
  68.0 2.4 %subtract_convert_fusion = (bf16[512,512]{1,0:T(8,128)(2,1)S(1)}, bf16[512,512]{1,0:T(8,128)(2,1)S(1)}) fusion(bf16[4096,512]{1,0:T(8,128)(2,1)S(1)} %constant_dynamic-update-slice_fusion.4, f32[512,4096]{1,0:T(8,128)S(1)} %fusion, f32[512,4096]{1,0:T(8,128)S(1)} %get-tuple-element.73, f32[512]{0:T(512)S(1)} %get-tuple-element.72), kind=kOutput, calls=%fused_computation.65 | convolution fusion | flops 2156920832 | bytes 22022144 | tf_op jit(solution)/shard_map/dot_general | solution.py:74
  80.9 5.7 %shard_map.214 = (bf16[2064,512]{1,0:T(8,128)(2,1)}, f32[2048,512]{1,0:T(8,128)}) custom-call(s32[1]{0:T(128)} %bitcast.7.core_ref, f32[512,512]{1,0:T(8,128)S(1)} %fusion.140.refs_0_, f32[512,512]{1,0:T(8,128)S(1)} %pad_maximum_fusion.1.refs_1_, f32[512,512]{1,0:T(8,128)S(1)} %pad_maximum_fusion.2.refs_2_, f32[512,512]{1,0:T(8,128)S(1)} %fusion.141.refs_3_, ...), custom_call_target="tpu_custom_call" | custom-call | tf_op jit(solution)/shard_map/pallas_call | solution.py:305
  86.7 4.3 %collective-permute-done.14.refs_3_ = bf16[2064,512]{1,0:T(8,128)(2,1)S(1)} collective-permute-done((bf16[2064,512]{1,0:T(8,128)(2,1)}, bf16[2064,512]{1,0:T(8,128)(2,1)S(1)}, u32[]{:S(2)}, u32[]{:S(2)}) %collective-permute-start.14) | collective-permute-done | bytes 2113568 | tf_op jit(solution)/shard_map/ppermute | solution.py:53
  91.0 3.6 %shard_map.215 = (bf16[528,512]{1,0:T(8,128)(2,1)}, bf16[528,512]{1,0:T(8,128)(2,1)}, bf16[528,512]{1,0:T(8,128)(2,1)}, f32[512,512]{1,0:T(8,128)S(1)}, f32[8,512]{1,0:T(8,128)S(1)}) custom-call(s32[1]{0:T(128)} %bitcast.11.refs_0_, f32[2048,512]{1,0:T(8,128)} %get-tuple-element.30.refs_1_, f32[8,512]{1,0:T(8,128)S(1)} %maximum_maximum_fusion.refs_6_.refs_2_, ...), custom_call_target="tpu_custom_call" | custom-call | tf_op jit(solution)/shard_map/pallas_call | solution.py:305
  98.4 4.9 %collective-permute-done.15.refs_3_ = bf16[528,512]{1,0:T(8,128)(2,1)S(1)} collective-permute-done((bf16[528,512]{1,0:T(8,128)(2,1)}, bf16[528,512]{1,0:T(8,128)(2,1)S(1)}, u32[]{:S(2)}, u32[]{:S(2)}) %collective-permute-start.15) | collective-permute-done | bytes 540704 | tf_op jit(solution)/shard_map/ppermute | solution.py:53
  103.2 6.2 %collective-permute-done.16.refs_4_ = bf16[528,512]{1,0:T(8,128)(2,1)S(1)} collective-permute-done((bf16[528,512]{1,0:T(8,128)(2,1)}, bf16[528,512]{1,0:T(8,128)(2,1)S(1)}, u32[]{:S(2)}, u32[]{:S(2)}) %collective-permute-start.16) | collective-permute-done | bytes 540704 | tf_op jit(solution)/shard_map/ppermute | solution.py:53
  109.5 2.9 %collective-permute-done.17.refs_5_ = bf16[528,512]{1,0:T(8,128)(2,1)S(1)} collective-permute-done((bf16[528,512]{1,0:T(8,128)(2,1)}, bf16[528,512]{1,0:T(8,128)(2,1)S(1)}, u32[]{:S(2)}, u32[]{:S(2)}) %collective-permute-start.17) | collective-permute-done | bytes 540704 | tf_op jit(solution)/shard_map/ppermute | solution.py:53
  113.8 2.7 %collective-permute-start.20 = (bf16[144,512]{1,0:T(8,128)(2,1)S(1)}, bf16[144,512]{1,0:T(8,128)(2,1)S(1)}, u32[]{:S(2)}, u32[]{:S(2)}) collective-permute-start(bf16[144,512]{1,0:T(8,128)(2,1)S(1)} %get-tuple-element.41), channel_id=1, source_target_pairs={{0,24},{1,25},{2,26},{3,27},{4,28},{5,29},{6,30},{7,31},{8,16},{9,... | collective-permute-start | bytes 442376 | tf_op jit(solution)/shard_map/ppermute | solution.py:53
  120.2 5.5 %collective-permute-start.21 = (bf16[144,512]{1,0:T(8,128)(2,1)S(1)}, bf16[144,512]{1,0:T(8,128)(2,1)S(1)}, u32[]{:S(2)}, u32[]{:S(2)}) collective-permute-start(bf16[144,512]{1,0:T(8,128)(2,1)S(1)} %shard_map.217.own_ref), channel_id=1, source_target_pairs={{0,4},{1,5},{2,6},{3,7},{4,0},{5,1},{6,2},{7,3},{8,12},{9,13},{10,... | collective-permute-start | bytes 442376 | tf_op jit(solution)/shard_map/ppermute | solution.py:53
  125.7 2.5 %collective-permute-start.22 = (bf16[144,512]{1,0:T(8,128)(2,1)S(1)}, bf16[144,512]{1,0:T(8,128)(2,1)S(1)}, u32[]{:S(2)}, u32[]{:S(2)}) collective-permute-start(bf16[144,512]{1,0:T(8,128)(2,1)S(1)} %shard_map.217.own_ref), channel_id=1, source_target_pairs={{0,64},{1,65},{2,66},{3,67},{4,68},{5,69},{6,70},{7,71},{8,72},{9,... | collective-permute-start | bytes 442376 | tf_op jit(solution)/shard_map/ppermute | solution.py:53
  128.2 4.1 %collective-permute-done.22.refs_1_ = bf16[144,512]{1,0:T(8,128)(2,1)S(1)} collective-permute-done((bf16[144,512]{1,0:T(8,128)(2,1)S(1)}, bf16[144,512]{1,0:T(8,128)(2,1)S(1)}, u32[]{:S(2)}, u32[]{:S(2)}) %collective-permute-start.22) | collective-permute-done | bytes 147488 | tf_op jit(solution)/shard_map/ppermute | solution.py:53
  133.9 2.2 %collective-permute-start.24 = (bf16[128,512]{1,0:T(8,128)(2,1)S(1)}, bf16[128,512]{1,0:T(8,128)(2,1)S(1)}, u32[]{:S(2)}, u32[]{:S(2)}) collective-permute-start(bf16[128,512]{1,0:T(8,128)(2,1)S(1)} %get-tuple-element.42), channel_id=1, source_target_pairs={{0,8},{1,9},{2,10},{3,11},{4,12},{5,13},{6,14},{7,15},{8,0},{9,1},... | collective-permute-start | bytes 393224 | tf_op jit(solution)/shard_map/ppermute | solution.py:53
  138.7 3.0 %collective-permute-done.25 = bf16[128,512]{1,0:T(8,128)(2,1)S(1)} collective-permute-done((bf16[128,512]{1,0:T(8,128)(2,1)S(1)}, bf16[128,512]{1,0:T(8,128)(2,1)S(1)}, u32[]{:S(2)}, u32[]{:S(2)}) %collective-permute-start.25) | collective-permute-done | bytes 131104 | tf_op jit(solution)/shard_map/ppermute | solution.py:53
  143.2 3.8 %collective-permute-start.28 = (bf16[512,512]{1,0:T(8,128)(2,1)S(1)}, bf16[512,512]{1,0:T(8,128)(2,1)S(1)}, u32[]{:S(2)}, u32[]{:S(2)}) collective-permute-start(bf16[512,512]{1,0:T(8,128)(2,1)S(1)} %constant_dynamic-update-slice_fusion.15.refs_0_), channel_id=1, source_target_pairs={{0,2},{1,3},{2,0},{3,1},{4,6},{5,7},{6,4},{7,5},{8,10},{9,11},{10,... | collective-permute-start | bytes 1572872 | tf_op jit(solution)/shard_map/ppermute | solution.py:53
  147.0 6.0 %collective-permute-start.30 = (bf16[512,512]{1,0:T(8,128)(2,1)S(1)}, bf16[512,512]{1,0:T(8,128)(2,1)S(1)}, u32[]{:S(2)}, u32[]{:S(2)}) collective-permute-start(bf16[512,512]{1,0:T(8,128)(2,1)S(1)} %constant_dynamic-update-slice_fusion.15.refs_0_), channel_id=1, source_target_pairs={{0,32},{1,33},{2,34},{3,35},{4,36},{5,37},{6,38},{7,39},{8,40},{9,... | collective-permute-start | bytes 1572872 | tf_op jit(solution)/shard_map/ppermute | solution.py:53
  153.0 4.5 %collective-permute-start.31 = (bf16[512,512]{1,0:T(8,128)(2,1)S(1)}, bf16[512,512]{1,0:T(8,128)(2,1)S(1)}, u32[]{:S(2)}, u32[]{:S(2)}) collective-permute-start(bf16[512,512]{1,0:T(8,128)(2,1)S(1)} %collective-permute-done.27.refs_1_), channel_id=1, source_target_pairs={{0,32},{1,33},{2,34},{3,35},{4,36},{5,37},{6,38},{7,39},{8,40},{9,... | collective-permute-start | bytes 1572872 | tf_op jit(solution)/shard_map/ppermute | solution.py:53
  159.2 6.5 %collective-permute-start.32 = (bf16[512,512]{1,0:T(8,128)(2,1)S(1)}, bf16[512,512]{1,0:T(8,128)(2,1)S(1)}, u32[]{:S(2)}, u32[]{:S(2)}) collective-permute-start(bf16[512,512]{1,0:T(8,128)(2,1)S(1)} %collective-permute-done.28.refs_2_), channel_id=1, source_target_pairs={{0,32},{1,33},{2,34},{3,35},{4,36},{5,37},{6,38},{7,39},{8,40},{9,... | collective-permute-start | bytes 1572872 | tf_op jit(solution)/shard_map/ppermute | solution.py:53
  165.7 3.1 %collective-permute-start.33 = (bf16[512,512]{1,0:T(8,128)(2,1)S(1)}, bf16[512,512]{1,0:T(8,128)(2,1)S(1)}, u32[]{:S(2)}, u32[]{:S(2)}) collective-permute-start(bf16[512,512]{1,0:T(8,128)(2,1)S(1)} %collective-permute-done.29.refs_3_), channel_id=1, source_target_pairs={{0,32},{1,33},{2,34},{3,35},{4,36},{5,37},{6,38},{7,39},{8,40},{9,... | collective-permute-start | bytes 1572872 | tf_op jit(solution)/shard_map/ppermute | solution.py:53
  172.2 4.4 %collective-permute-done.13 = bf16[128,512]{1,0:T(8,128)(2,1)S(1)} collective-permute-done((bf16[128,512]{1,0:T(8,128)(2,1)S(1)}, bf16[128,512]{1,0:T(8,128)(2,1)S(1)}, u32[]{:S(2)}, u32[]{:S(2)}) %collective-permute-start.13) | collective-permute-done | bytes 131104 | tf_op jit(solution)/shard_map/ppermute | solution.py:53
  177.7 2.9 %shard_map.219 = (bf16[512,512]{1,0:T(8,128)(2,1)}, bf16[512,512]{1,0:T(8,128)(2,1)}, bf16[512,512]{1,0:T(8,128)(2,1)}, bf16[512,512]{1,0:T(8,128)(2,1)}, bf16[5...) custom-call(s32[3]{0:T(128)S(1)} %pad_add_fusion.where_ref, ...), custom_call_target="tpu_custom_call" | custom-call | tf_op jit(solution)/shard_map/pallas_call | solution.py:305
  (171 shorter events, 56.1 us)
Async XLA Ops:
  0.7 14.1 %collective-permute-start.2 = (bf16[128,512]{1,0:T(8,128)(2,1)}, bf16[128,512]{1,0:T(8,128)(2,1)S(1)}, u32[]{:S(2)}, u32[]{:S(2)}) collective-permute-start(bf16[128,512]{1,0:T(8,128)(2,1)} %bitcast.38), channel_id=1, source_target_pairs={{0,0},{1,1},{2,2},{3,3},{4,32},{5,33},{6,34},{7,35},{8,8},{9,9},{1... | collective-permute-start | bytes 393224 | tf_op jit(solution)/shard_map/ppermute | solution.py:53
  6.3 23.0 %collective-permute-start = (bf16[256,512]{1,0:T(8,128)(2,1)S(1)}, bf16[256,512]{1,0:T(8,128)(2,1)S(1)}, u32[]{:S(2)}, u32[]{:S(2)}) collective-permute-start(bf16[256,512]{1,0:T(8,128)(2,1)S(1)} %pad_maximum_fusion.3), channel_id=1, source_target_pairs={{0,0},{1,1},{2,2},{3,3},{4,32},{5,33},{6,34},{7,35},{8,8},{9,9},{1... | collective-permute-start | bytes 786440 | tf_op jit(solution)/shard_map/ppermute | solution.py:53
  8.2 5.8 %collective-permute-start.1 = (s32[1,32]{1,0:T(1,128)}, s32[1,32]{1,0:T(1,128)S(1)}, u32[]{:S(2)}, u32[]{:S(2)}) collective-permute-start(s32[1,32]{1,0:T(1,128)} %bitcast.39), channel_id=1, source_target_pairs={{0,0},{1,1},{2,2},{3,3},{4,32},{5,33},{6,34},{7,35},{8,8},{9,9},{1... | collective-permute-start | bytes 392 | tf_op jit(solution)/shard_map/ppermute | solution.py:53
  14.8 5.2 %collective-permute-start.3 = (bf16[128,512]{1,0:T(8,128)(2,1)S(1)}, bf16[128,512]{1,0:T(8,128)(2,1)S(1)}, u32[]{:S(2)}, u32[]{:S(2)}) collective-permute-start(bf16[128,512]{1,0:T(8,128)(2,1)S(1)} %collective-permute-done.2), channel_id=1, source_target_pairs={{0,1},{1,0},{2,3},{3,2},{4,5},{5,4},{6,7},{7,6},{8,9},{9,8},{10,11... | collective-permute-start | bytes 393224 | tf_op jit(solution)/shard_map/ppermute | solution.py:53
  16.6 7.0 %collective-permute-start.4 = (bf16[128,512]{1,0:T(8,128)(2,1)S(1)}, bf16[128,512]{1,0:T(8,128)(2,1)S(1)}, u32[]{:S(2)}, u32[]{:S(2)}) collective-permute-start(bf16[128,512]{1,0:T(8,128)(2,1)S(1)} %collective-permute-done.2), channel_id=1, source_target_pairs={{0,2},{1,3},{2,0},{3,1},{4,6},{5,7},{6,4},{7,5},{8,10},{9,11},{10,... | collective-permute-start | bytes 393224 | tf_op jit(solution)/shard_map/ppermute | solution.py:53
  19.9 5.1 %collective-permute-start.5 = (bf16[128,512]{1,0:T(8,128)(2,1)S(1)}, bf16[128,512]{1,0:T(8,128)(2,1)S(1)}, u32[]{:S(2)}, u32[]{:S(2)}) collective-permute-start(bf16[128,512]{1,0:T(8,128)(2,1)S(1)} %collective-permute-done.2), channel_id=1, source_target_pairs={{0,3},{1,2},{2,1},{3,0},{4,7},{5,6},{6,5},{7,4},{8,11},{9,10},{10,... | collective-permute-start | bytes 393224 | tf_op jit(solution)/shard_map/ppermute | solution.py:53
  25.0 8.5 %collective-permute-start.6 = (bf16[512,512]{1,0:T(8,128)(2,1)S(1)}, bf16[512,512]{1,0:T(8,128)(2,1)S(1)}, u32[]{:S(2)}, u32[]{:S(2)}) collective-permute-start(bf16[512,512]{1,0:T(8,128)(2,1)S(1)} %get-tuple-element.60), channel_id=1, source_target_pairs={{0,8},{1,9},{2,10},{3,11},{4,12},{5,13},{6,14},{7,15},{8,0},{9,1},... | collective-permute-start | bytes 1572872 | tf_op jit(solution)/shard_map/ppermute | solution.py:53
  26.6 14.9 %collective-permute-start.7 = (bf16[512,512]{1,0:T(8,128)(2,1)S(1)}, bf16[512,512]{1,0:T(8,128)(2,1)S(1)}, u32[]{:S(2)}, u32[]{:S(2)}) collective-permute-start(bf16[512,512]{1,0:T(8,128)(2,1)S(1)} %get-tuple-element.60), channel_id=1, source_target_pairs={{0,16},{1,17},{2,18},{3,19},{4,20},{5,21},{6,22},{7,23},{8,24},{9,... | collective-permute-start | bytes 1572872 | tf_op jit(solution)/shard_map/ppermute | solution.py:53
  29.3 14.9 %collective-permute-start.8 = (bf16[512,512]{1,0:T(8,128)(2,1)S(1)}, bf16[512,512]{1,0:T(8,128)(2,1)S(1)}, u32[]{:S(2)}, u32[]{:S(2)}) collective-permute-start(bf16[512,512]{1,0:T(8,128)(2,1)S(1)} %get-tuple-element.60), channel_id=1, source_target_pairs={{0,24},{1,25},{2,26},{3,27},{4,28},{5,29},{6,30},{7,31},{8,16},{9,... | collective-permute-start | bytes 1572872 | tf_op jit(solution)/shard_map/ppermute | solution.py:53
  29.3 14.9 %collective-permute-start.9 = (bf16[512,512]{1,0:T(8,128)(2,1)S(1)}, bf16[512,512]{1,0:T(8,128)(2,1)S(1)}, u32[]{:S(2)}, u32[]{:S(2)}) collective-permute-start(bf16[512,512]{1,0:T(8,128)(2,1)S(1)} %get-tuple-element.60), channel_id=1, source_target_pairs={{0,32},{1,33},{2,34},{3,35},{4,36},{5,37},{6,38},{7,39},{8,40},{9,... | collective-permute-start | bytes 1572872 | tf_op jit(solution)/shard_map/ppermute | solution.py:53
  33.5 10.8 %collective-permute-start.10 = (bf16[512,512]{1,0:T(8,128)(2,1)S(1)}, bf16[512,512]{1,0:T(8,128)(2,1)S(1)}, u32[]{:S(2)}, u32[]{:S(2)}) collective-permute-start(bf16[512,512]{1,0:T(8,128)(2,1)S(1)} %collective-permute-done.6), channel_id=1, source_target_pairs={{0,32},{1,33},{2,34},{3,35},{4,36},{5,37},{6,38},{7,39},{8,40},{9,... | collective-permute-start | bytes 1572872 | tf_op jit(solution)/shard_map/ppermute | solution.py:53
  86.6 4.4 %collective-permute-start.14 = (bf16[2064,512]{1,0:T(8,128)(2,1)}, bf16[2064,512]{1,0:T(8,128)(2,1)S(1)}, u32[]{:S(2)}, u32[]{:S(2)}) collective-permute-start(bf16[2064,512]{1,0:T(8,128)(2,1)} %get-tuple-element.31), channel_id=1, source_target_pairs={{0,32},{1,33},{2,34},{3,35},{4,36},{5,37},{6,38},{7,39},{8,40},{9,... | collective-permute-start | bytes 6340616 | tf_op jit(solution)/shard_map/ppermute | solution.py:53
  94.5 8.7 %collective-permute-start.15 = (bf16[528,512]{1,0:T(8,128)(2,1)}, bf16[528,512]{1,0:T(8,128)(2,1)S(1)}, u32[]{:S(2)}, u32[]{:S(2)}) collective-permute-start(bf16[528,512]{1,0:T(8,128)(2,1)} %get-tuple-element.34), channel_id=1, source_target_pairs={{0,1},{1,0},{2,3},{3,2},{4,5},{5,4},{6,7},{7,6},{8,9},{9,8},{10,11... | collective-permute-start | bytes 1622024 | tf_op jit(solution)/shard_map/ppermute | solution.py:53
  94.5 14.9 %collective-permute-start.16 = (bf16[528,512]{1,0:T(8,128)(2,1)}, bf16[528,512]{1,0:T(8,128)(2,1)S(1)}, u32[]{:S(2)}, u32[]{:S(2)}) collective-permute-start(bf16[528,512]{1,0:T(8,128)(2,1)} %get-tuple-element.35), channel_id=1, source_target_pairs={{0,2},{1,3},{2,0},{3,1},{4,6},{5,7},{6,4},{7,5},{8,10},{9,11},{10,... | collective-permute-start | bytes 1622024 | tf_op jit(solution)/shard_map/ppermute | solution.py:53
  96.6 15.7 %collective-permute-start.17 = (bf16[528,512]{1,0:T(8,128)(2,1)}, bf16[528,512]{1,0:T(8,128)(2,1)S(1)}, u32[]{:S(2)}, u32[]{:S(2)}) collective-permute-start(bf16[528,512]{1,0:T(8,128)(2,1)} %get-tuple-element.36), channel_id=1, source_target_pairs={{0,3},{1,2},{2,1},{3,0},{4,7},{5,6},{6,5},{7,4},{8,11},{9,10},{10,... | collective-permute-start | bytes 1622024 | tf_op jit(solution)/shard_map/ppermute | solution.py:53
  112.6 4.4 %collective-permute-start.18 = (bf16[144,512]{1,0:T(8,128)(2,1)S(1)}, bf16[144,512]{1,0:T(8,128)(2,1)S(1)}, u32[]{:S(2)}, u32[]{:S(2)}) collective-permute-start(bf16[144,512]{1,0:T(8,128)(2,1)S(1)} %get-tuple-element.39), channel_id=1, source_target_pairs={{0,8},{1,9},{2,10},{3,11},{4,12},{5,13},{6,14},{7,15},{8,0},{9,1},... | collective-permute-start | bytes 442376 | tf_op jit(solution)/shard_map/ppermute | solution.py:53
  112.7 5.7 %collective-permute-start.19 = (bf16[144,512]{1,0:T(8,128)(2,1)S(1)}, bf16[144,512]{1,0:T(8,128)(2,1)S(1)}, u32[]{:S(2)}, u32[]{:S(2)}) collective-permute-start(bf16[144,512]{1,0:T(8,128)(2,1)S(1)} %get-tuple-element.40), channel_id=1, source_target_pairs={{0,16},{1,17},{2,18},{3,19},{4,20},{5,21},{6,22},{7,23},{8,24},{9,... | collective-permute-start | bytes 442376 | tf_op jit(solution)/shard_map/ppermute | solution.py:53
  113.8 6.3 %collective-permute-start.20 = (bf16[144,512]{1,0:T(8,128)(2,1)S(1)}, bf16[144,512]{1,0:T(8,128)(2,1)S(1)}, u32[]{:S(2)}, u32[]{:S(2)}) collective-permute-start(bf16[144,512]{1,0:T(8,128)(2,1)S(1)} %get-tuple-element.41), channel_id=1, source_target_pairs={{0,24},{1,25},{2,26},{3,27},{4,28},{5,29},{6,30},{7,31},{8,16},{9,... | collective-permute-start | bytes 442376 | tf_op jit(solution)/shard_map/ppermute | solution.py:53
  120.2 8.0 %collective-permute-start.21 = (bf16[144,512]{1,0:T(8,128)(2,1)S(1)}, bf16[144,512]{1,0:T(8,128)(2,1)S(1)}, u32[]{:S(2)}, u32[]{:S(2)}) collective-permute-start(bf16[144,512]{1,0:T(8,128)(2,1)S(1)} %shard_map.217.own_ref), channel_id=1, source_target_pairs={{0,4},{1,5},{2,6},{3,7},{4,0},{5,1},{6,2},{7,3},{8,12},{9,13},{10,... | collective-permute-start | bytes 442376 | tf_op jit(solution)/shard_map/ppermute | solution.py:53
  125.7 6.6 %collective-permute-start.22 = (bf16[144,512]{1,0:T(8,128)(2,1)S(1)}, bf16[144,512]{1,0:T(8,128)(2,1)S(1)}, u32[]{:S(2)}, u32[]{:S(2)}) collective-permute-start(bf16[144,512]{1,0:T(8,128)(2,1)S(1)} %shard_map.217.own_ref), channel_id=1, source_target_pairs={{0,64},{1,65},{2,66},{3,67},{4,68},{5,69},{6,70},{7,71},{8,72},{9,... | collective-permute-start | bytes 442376 | tf_op jit(solution)/shard_map/ppermute | solution.py:53
  128.1 5.7 %collective-permute-start.23 = (bf16[144,512]{1,0:T(8,128)(2,1)S(1)}, bf16[144,512]{1,0:T(8,128)(2,1)S(1)}, u32[]{:S(2)}, u32[]{:S(2)}) collective-permute-start(bf16[144,512]{1,0:T(8,128)(2,1)S(1)} %shard_map.217.own_ref), channel_id=1, source_target_pairs={{0,68},{1,69},{2,70},{3,71},{4,64},{5,65},{6,66},{7,67},{8,76},{9,... | collective-permute-start | bytes 442376 | tf_op jit(solution)/shard_map/ppermute | solution.py:53
  133.9 4.7 %collective-permute-start.24 = (bf16[128,512]{1,0:T(8,128)(2,1)S(1)}, bf16[128,512]{1,0:T(8,128)(2,1)S(1)}, u32[]{:S(2)}, u32[]{:S(2)}) collective-permute-start(bf16[128,512]{1,0:T(8,128)(2,1)S(1)} %get-tuple-element.42), channel_id=1, source_target_pairs={{0,8},{1,9},{2,10},{3,11},{4,12},{5,13},{6,14},{7,15},{8,0},{9,1},... | collective-permute-start | bytes 393224 | tf_op jit(solution)/shard_map/ppermute | solution.py:53
  136.1 5.6 %collective-permute-start.25 = (bf16[128,512]{1,0:T(8,128)(2,1)S(1)}, bf16[128,512]{1,0:T(8,128)(2,1)S(1)}, u32[]{:S(2)}, u32[]{:S(2)}) collective-permute-start(bf16[128,512]{1,0:T(8,128)(2,1)S(1)} %get-tuple-element.42), channel_id=1, source_target_pairs={{0,16},{1,17},{2,18},{3,19},{4,20},{5,21},{6,22},{7,23},{8,24},{9,... | collective-permute-start | bytes 393224 | tf_op jit(solution)/shard_map/ppermute | solution.py:53
  138.0 5.1 %collective-permute-start.26 = (bf16[128,512]{1,0:T(8,128)(2,1)S(1)}, bf16[128,512]{1,0:T(8,128)(2,1)S(1)}, u32[]{:S(2)}, u32[]{:S(2)}) collective-permute-start(bf16[128,512]{1,0:T(8,128)(2,1)S(1)} %get-tuple-element.42), channel_id=1, source_target_pairs={{0,24},{1,25},{2,26},{3,27},{4,28},{5,29},{6,30},{7,31},{8,16},{9,... | collective-permute-start | bytes 393224 | tf_op jit(solution)/shard_map/ppermute | solution.py:53
  143.1 10.0 %collective-permute-start.27 = (bf16[512,512]{1,0:T(8,128)(2,1)S(1)}, bf16[512,512]{1,0:T(8,128)(2,1)S(1)}, u32[]{:S(2)}, u32[]{:S(2)}) collective-permute-start(bf16[512,512]{1,0:T(8,128)(2,1)S(1)} %constant_dynamic-update-slice_fusion.15.refs_0_), channel_id=1, source_target_pairs={{0,1},{1,0},{2,3},{3,2},{4,5},{5,4},{6,7},{7,6},{8,9},{9,8},{10,11... | collective-permute-start | bytes 1572872 | tf_op jit(solution)/shard_map/ppermute | solution.py:53
  143.2 16.1 %collective-permute-start.28 = (bf16[512,512]{1,0:T(8,128)(2,1)S(1)}, bf16[512,512]{1,0:T(8,128)(2,1)S(1)}, u32[]{:S(2)}, u32[]{:S(2)}) collective-permute-start(bf16[512,512]{1,0:T(8,128)(2,1)S(1)} %constant_dynamic-update-slice_fusion.15.refs_0_), channel_id=1, source_target_pairs={{0,2},{1,3},{2,0},{3,1},{4,6},{5,7},{6,4},{7,5},{8,10},{9,11},{10,... | collective-permute-start | bytes 1572872 | tf_op jit(solution)/shard_map/ppermute | solution.py:53
  146.9 18.8 %collective-permute-start.29 = (bf16[512,512]{1,0:T(8,128)(2,1)S(1)}, bf16[512,512]{1,0:T(8,128)(2,1)S(1)}, u32[]{:S(2)}, u32[]{:S(2)}) collective-permute-start(bf16[512,512]{1,0:T(8,128)(2,1)S(1)} %constant_dynamic-update-slice_fusion.15.refs_0_), channel_id=1, source_target_pairs={{0,3},{1,2},{2,1},{3,0},{4,7},{5,6},{6,5},{7,4},{8,11},{9,10},{10,... | collective-permute-start | bytes 1572872 | tf_op jit(solution)/shard_map/ppermute | solution.py:53
  147.0 30.7 %collective-permute-start.30 = (bf16[512,512]{1,0:T(8,128)(2,1)S(1)}, bf16[512,512]{1,0:T(8,128)(2,1)S(1)}, u32[]{:S(2)}, u32[]{:S(2)}) collective-permute-start(bf16[512,512]{1,0:T(8,128)(2,1)S(1)} %constant_dynamic-update-slice_fusion.15.refs_0_), channel_id=1, source_target_pairs={{0,32},{1,33},{2,34},{3,35},{4,36},{5,37},{6,38},{7,39},{8,40},{9,... | collective-permute-start | bytes 1572872 | tf_op jit(solution)/shard_map/ppermute | solution.py:53
  153.0 24.7 %collective-permute-start.31 = (bf16[512,512]{1,0:T(8,128)(2,1)S(1)}, bf16[512,512]{1,0:T(8,128)(2,1)S(1)}, u32[]{:S(2)}, u32[]{:S(2)}) collective-permute-start(bf16[512,512]{1,0:T(8,128)(2,1)S(1)} %collective-permute-done.27.refs_1_), channel_id=1, source_target_pairs={{0,32},{1,33},{2,34},{3,35},{4,36},{5,37},{6,38},{7,39},{8,40},{9,... | collective-permute-start | bytes 1572872 | tf_op jit(solution)/shard_map/ppermute | solution.py:53
  159.2 18.5 %collective-permute-start.32 = (bf16[512,512]{1,0:T(8,128)(2,1)S(1)}, bf16[512,512]{1,0:T(8,128)(2,1)S(1)}, u32[]{:S(2)}, u32[]{:S(2)}) collective-permute-start(bf16[512,512]{1,0:T(8,128)(2,1)S(1)} %collective-permute-done.28.refs_2_), channel_id=1, source_target_pairs={{0,32},{1,33},{2,34},{3,35},{4,36},{5,37},{6,38},{7,39},{8,40},{9,... | collective-permute-start | bytes 1572872 | tf_op jit(solution)/shard_map/ppermute | solution.py:53
  165.7 12.0 %collective-permute-start.33 = (bf16[512,512]{1,0:T(8,128)(2,1)S(1)}, bf16[512,512]{1,0:T(8,128)(2,1)S(1)}, u32[]{:S(2)}, u32[]{:S(2)}) collective-permute-start(bf16[512,512]{1,0:T(8,128)(2,1)S(1)} %collective-permute-done.29.refs_3_), channel_id=1, source_target_pairs={{0,32},{1,33},{2,34},{3,35},{4,36},{5,37},{6,38},{7,39},{8,40},{9,... | collective-permute-start | bytes 1572872 | tf_op jit(solution)/shard_map/ppermute | solution.py:53
  170.2 6.3 %collective-permute-start.13 = (bf16[128,512]{1,0:T(8,128)(2,1)S(1)}, bf16[128,512]{1,0:T(8,128)(2,1)S(1)}, u32[]{:S(2)}, u32[]{:S(2)}) collective-permute-start(bf16[128,512]{1,0:T(8,128)(2,1)S(1)} %fusion.13), channel_id=1, source_target_pairs={{0,0},{1,1},{2,2},{3,3},{4,32},{5,33},{6,34},{7,35},{8,8},{9,9},{1... | collective-permute-start | bytes 393224 | tf_op jit(solution)/shard_map/ppermute | solution.py:53
  (18 other events, 269.7 us)

commit v3 on v2

--- a/solution.py
+++ b/solution.py
@@ -92,102 +92,189 @@
     return high, low
 
 
-def device_step(
-    queries,
-    visible,
-    cotangent,
-    feats,
-    w_query,
-    w_key,
-    w_value,
-    w_out,
-    w_up,
-    w_down,
-    gain_attn,
-    gain_mlp,
-):
-    head = w_query.shape[1] // HEADS
-    rows = queries.shape[0]
+PARTS = 8
+def lanes(value, combine):
+    out = value[:, 0:BLK]
+    for at in range(BLK, value.shape[1], BLK):
+        out = combine(out, value[:, at : at + BLK])
+    return out
+
+
+def step_kernel(core_ref, moved, seen, w_query, w_key, w_value, w_out, w_up, w_down, gain_attn, gain_mlp, *refs):
+    parts, (output, give, keep, gains_out) = refs[:PARTS], refs[PARTS : PARTS + 4]
+    feats, scores, pulls, sums, stat, sems = refs[PARTS + 4 :]
+    f32, b16 = jnp.float32, jnp.bfloat16
+    copies = [pltpu.make_async_copy(parts[p], feats.at[p], sems.at[p]) for p in range(PARTS)]
+    for copy in copies:
+        copy.start()
+
+    width = w_query.shape[0]
+    head = width // HEADS
     factor = 1.0 / math.sqrt(head)
-    allowed = jnp.repeat(visible > 0, BLK)[None, :]
-    inputs = queries.astype(jnp.float32)
-    scaled_one, _, normed = normalize(inputs, gain_attn)
-    normed_b = normed.astype(jnp.bfloat16)
-    query_rows = mult(normed_b, w_query).astype(jnp.bfloat16)
-    key_rows = mult(feats, w_key).astype(jnp.bfloat16)
     cols = [slice(h * head, (h + 1) * head) for h in range(HEADS)]
-    scores = []
-    for c in cols:
-        part = mult_nt(query_rows[:, c], key_rows[:, c]) * factor
-        scores.append(jnp.where(allowed, part, -1e30))
-    scores = jnp.concatenate(scores, axis=0)
-    expo = jnp.exp(scores - jnp.max(scores, axis=-1, keepdims=True))
-    attend = expo / jnp.sum(expo, axis=-1, keepdims=True)
-    attend_b = attend.astype(jnp.bfloat16)
-    u_high, u_low = two_parts(mult(attend_b, feats))
-    heads = [slice(h * rows, (h + 1) * rows) for h in range(HEADS)]
+    heads = [slice(h * BLK, (h + 1) * BLK) for h in range(HEADS)]
+    inputs = moved[0:BLK, :].astype(f32)
+    scaled_one, _, normed = normalize(inputs, gain_attn[...])
+    normed_b = normed.astype(b16)
+    query_rows = mult(normed_b, w_query[...]).astype(b16)
+
+    stat[...] = jnp.full_like(stat, -1e30)
+
+    for copy in copies:
+        copy.wait()
+
+    def score(p, carry):
+        key_rows = mult(feats[p], w_key[...]).astype(b16)
+        allowed = seen[pl.ds(p, 1), :] > 0
+        for r, c in zip(heads, cols):
+            part = mult_nt(query_rows[:, c], key_rows[:, c]) * factor
+            part = jnp.where(allowed, part, -1e30)
+            scores[p, r, :] = part
+            stat[r, :] = jnp.maximum(stat[r, :], lanes(part, jnp.maximum))
+        return carry
+
+    lax.fori_loop(0, PARTS, score, 0)
+    highest = jnp.max(stat[...], axis=-1, keepdims=True)
+    stat[...] = jnp.zeros_like(stat)
+
+    def expo(p, carry):
+        part = jnp.exp(scores[p] - highest)
+        scores[p] = part
+        stat[...] += lanes(part, jnp.add)
+        return carry
+
+    lax.fori_loop(0, PARTS, expo, 0)
+    inverse_sum = 1.0 / jnp.sum(stat[...], axis=-1, keepdims=True)
+    sums[...] = jnp.zeros_like(sums)
+
+    def attend(p, carry):
+        part = scores[p] * inverse_sum
+        scores[p] = part
+        sums[...] += mult(part.astype(b16), feats[p])
+        return carry
+
+    lax.fori_loop(0, PARTS, attend, 0)
+    u_high, u_low = two_parts(sums[...])
     context = jnp.concatenate(
         [mult(u_high[r], w_value[:, c]) + mult(u_low[r], w_value[:, c]) for r, c in zip(heads, cols)],
         axis=1,
-    ).astype(jnp.bfloat16)
-    mixed = inputs + mult(context, w_out)
-    scaled_two, inverse_two, normed_two = normalize(mixed, gain_mlp)
-    normed_two_b = normed_two.astype(jnp.bfloat16)
-    activated, slope = gelu_pair(mult(normed_two_b, w_up))
-    activated_b = activated.astype(jnp.bfloat16)
-    output = (mixed + mult(activated_b, w_down)).astype(jnp.bfloat16)
-    grad_down = mult_tn(activated_b, cotangent)
-    grad_upper_b = (mult_nt(cotangent, w_down) * slope).astype(jnp.bfloat16)
-    grad_up = mult_tn(normed_two_b, grad_upper_b)
-    grad_normed_two = mult_nt(grad_upper_b, w_up)
-    grad_gain_mlp = jnp.sum(grad_normed_two * scaled_two, axis=0)
-    grad_scaled = grad_normed_two * gain_mlp
+    ).astype(b16)
+
+    core = core_ref[0]
+    half = PIECES // 2
+
+    def store(at, rows, grad):
+        middle = grad.shape[0] // 2
+        low, high = grad[:middle], grad[middle:]
+        mine = jnp.where(core == 0, low, high)
+        yours = jnp.where(core == 0, high, low).astype(b16)
+        for i in range(half):
+            keep[i * CHUNK + at : i * CHUNK + at + rows, :] = mine[i * rows : (i + 1) * rows]
+            give[i * CHUNK + at : i * CHUNK + at + rows, :] = yours[i * rows : (i + 1) * rows]
+
+    mixed = inputs + mult(context, w_out[...])
+    scaled_two, inverse_two, normed_two = normalize(mixed, gain_mlp[...])
+    normed_two_b = normed_two.astype(b16)
+    activated, slope = gelu_pair(mult(normed_two_b, w_up[...]))
+    activated_b = activated.astype(b16)
+    output[...] = (mixed + mult(activated_b, w_down[...])).astype(b16)
+    cotangent = moved[BLK : 2 * BLK, :]
+    store(96, 32, mult_tn(activated_b, cotangent))
+    grad_upper_b = (mult_nt(cotangent, w_down[...]) * slope).astype(b16)
+    store(64, 16, mult_tn(normed_two_b, grad_upper_b[:, :width]))
+    store(80, 16, mult_tn(normed_two_b, grad_upper_b[:, width:]))
+    grad_normed_two = mult_nt(grad_upper_b, w_up[...])
+    grad_gain_mlp = jnp.sum(grad_normed_two * scaled_two, axis=0, keepdims=True)
+    grad_scaled = grad_normed_two * gain_mlp[...]
     mean_one = jnp.mean(grad_scaled, axis=-1, keepdims=True)
     mean_two = jnp.mean(grad_scaled * scaled_two, axis=-1, keepdims=True)
-    grad_mixed = cotangent.astype(jnp.float32) + inverse_two * (
+    grad_mixed = cotangent.astype(f32) + inverse_two * (
         grad_scaled - mean_one - scaled_two * mean_two
     )
-    grad_mixed_b = grad_mixed.astype(jnp.bfloat16)
-    grad_out = mult_tn(context, grad_mixed_b)
-    grad_context = mult_nt(grad_mixed_b, w_out).astype(jnp.bfloat16)
-    grad_value = jnp.concatenate(
-        [
-            mult_tn(u_high[r], grad_context[:, c]) + mult_tn(u_low[r], grad_context[:, c])
-            for r, c in zip(heads, cols)
-        ],
-        axis=1,
+    grad_mixed_b = grad_mixed.astype(b16)
+    store(48, 16, mult_tn(context, grad_mixed_b))
+    grad_context = mult_nt(grad_mixed_b, w_out[...]).astype(b16)
+    store(
+        32,
+        16,
+        jnp.concatenate(
+            [
+                mult_tn(u_high[r], grad_context[:, c]) + mult_tn(u_low[r], grad_context[:, c])
+                for r, c in zip(heads, cols)
+            ],
+            axis=1,
+        ),
     )
     pulled = jnp.concatenate(
         [mult_nt(grad_context[:, c], w_value[:, c]) for c in cols], axis=0
-    ).astype(jnp.bfloat16)
-    grad_attend = mult_nt(pulled, feats)
-    centre = jnp.sum(attend * grad_attend, axis=-1, keepdims=True)
-    grad_scores = (attend * (grad_attend - centre) * factor).astype(jnp.bfloat16)
-    t_high, t_low = two_parts(mult(grad_scores, feats))
+    ).astype(b16)
+    stat[...] = jnp.zeros_like(stat)
+
+    def pull(p, carry):
+        part = mult_nt(pulled, feats[p])
+        pulls[p] = part
+        stat[...] += lanes(part * scores[p], jnp.add)
+        return carry
+
+    lax.fori_loop(0, PARTS, pull, 0)
+    centre = jnp.sum(stat[...], axis=-1, keepdims=True)
+    sums[...] = jnp.zeros_like(sums)
+
+    def back(p, carry):
+        part = (scores[p] * (pulls[p] - centre) * factor).astype(b16)
+        sums[...] += mult(part, feats[p])
+        return carry
+
+    lax.fori_loop(0, PARTS, back, 0)
+    t_high, t_low = two_parts(sums[...])
     grad_query_rows = jnp.concatenate(
         [mult(t_high[r], w_key[:, c]) + mult(t_low[r], w_key[:, c]) for r, c in zip(heads, cols)],
         axis=1,
-    ).astype(jnp.bfloat16)
-    grad_key = jnp.concatenate(
-        [
-            mult_tn(t_high[r], query_rows[:, c]) + mult_tn(t_low[r], query_rows[:, c])
-            for r, c in zip(heads, cols)
+    ).astype(b16)
+    store(
+        16,
+        16,
+        jnp.concatenate(
+            [
+                mult_tn(t_high[r], query_rows[:, c]) + mult_tn(t_low[r], query_rows[:, c])
+                for r, c in zip(heads, cols)
+            ],
+            axis=1,
+        ),
+    )
+    store(0, 16, mult_tn(normed_b, grad_query_rows))
+    grad_normed = mult_nt(grad_query_rows, w_query[...])
+    grad_gain_attn = jnp.sum(grad_normed * scaled_one, axis=0, keepdims=True)
+    gains = jnp.concatenate([grad_gain_attn, grad_gain_mlp, jnp.zeros((6, width), f32)], axis=0)
+    put_gains(give, half * CHUNK, gains)
+    gains_out[...] = gains
+
+
+def device_step(core_at, moved, seen, parts, weights):
+    f32, b16 = jnp.float32, jnp.bfloat16
+    return pl.pallas_call(
+        step_kernel,
+        out_shape=[
+            jax.ShapeDtypeStruct((BLK, 512), b16),
+            jax.ShapeDtypeStruct((2048 + TAIL, 512), b16),
+            jax.ShapeDtypeStruct((2048, 512), f32),
+            jax.ShapeDtypeStruct((8, 512), f32),
         ],
-        axis=1,
-    )
-    grad_query = mult_tn(normed_b, grad_query_rows)
-    grad_normed = mult_nt(grad_query_rows, w_query)
-    grad_gain_attn = jnp.sum(grad_normed * scaled_one, axis=0)
-    return output, (
-        grad_query,
-        grad_key,
-        grad_value,
-        grad_out,
-        grad_up,
-        grad_down,
-        grad_gain_attn,
-        grad_gain_mlp,
-    )
+        in_specs=[SMEM] + [VMEM] * 10 + [pl.BlockSpec(memory_space=pl.ANY)] * PARTS,
+        out_specs=[VMEM] * 4,
+        scratch_shapes=[
+            pltpu.VMEM((PARTS, 512, 512), b16),
+            pltpu.VMEM((PARTS, 512, 512), f32),
+            pltpu.VMEM((PARTS, 512, 512), f32),
+            pltpu.VMEM((512, 512), f32),
+            pltpu.VMEM((512, BLK), f32),
+            pltpu.SemaphoreType.DMA((PARTS,)),
+        ],
+        compiler_params=pltpu.CompilerParams(vmem_limit_bytes=52 << 20),
+        cost_estimate=pl.CostEstimate(
+            flops=12 * 10**9, bytes_accessed=18 * 10**6, transcendentals=3 * 10**6
+        ),
+    )(core_at, moved, seen, *weights, *parts)
 
 
 PIECES = 32
@@ -218,23 +305,6 @@
 def take_gains(ref, at):
     tail = ref[at : at + TAIL, :].astype(jnp.float32)
     return tail[: TAIL // 2] + tail[TAIL // 2 :]
-
-
-def halves_kernel(core_ref, *refs):
-    grads, gains, give, keep = refs[:6], refs[6], refs[7], refs[8]
-    core = core_ref[0]
-    half = PIECES // 2
-
-    def step(i, carry):
-        row = pl.multiple_of(i * CHUNK, CHUNK)
-        for at, piece in pieces_of(grads, (1 - core) * half + i):
-            give[pl.ds(row + at, piece.shape[0]), :] = piece[...].astype(jnp.bfloat16)
-        for at, piece in pieces_of(grads, core * half + i):
-            keep[pl.ds(row + at, piece.shape[0]), :] = piece[...]
-        return carry
-
-    lax.fori_loop(0, half, step, 0)
-    put_gains(give, half * CHUNK, gains[...])
 
 
 def quarters_kernel(many, index_ref, own_ref, gains_ref, *refs):
@@ -311,20 +381,12 @@
     )(*operands)
 
 
-def sum_everywhere(grads):
-    weights, (gain_attn, gain_mlp) = grads[:6], grads[6:]
+def sum_everywhere(output, give, keep, gains):
     core, y, z = (lax.axis_index(name) for name in ("core", "y", "z"))
-    gains = jnp.concatenate([gain_attn[None], gain_mlp[None], jnp.zeros((6, 512), jnp.float32)])
-    core_at = jnp.asarray(core, jnp.int32).reshape(1)
     one_at = jnp.where(core == 0, y, z).astype(jnp.int32).reshape(1)
     two_at = jnp.where(core == 0, z, y).astype(jnp.int32).reshape(1)
     b16, f32 = jnp.bfloat16, jnp.float32
 
-    give, keep = call(
-        halves_kernel,
-        [((2048 + TAIL, 512), b16), ((2048, 512), f32)],
-        core_at, *weights, gains, scalars=1,
-    )
     arrived = [send(give, CORE)]
     for rows, index, route, count in ((512, one_at, first, 1), (128, two_at, second, 3)):
         *gives, keep, gains = call(
@@ -333,6 +395,7 @@
             index, keep, gains, *arrived, scalars=1,
         )
         arrived = [send(give, route(mask)) for mask, give in enumerate(gives, 1)]
+    output, *arrived = lax.optimization_barrier((send(output, SWAP), *arrived))
     (give,) = call(chunk_kernel, [((128 + TAIL, 512), b16)], keep, gains, *arrived)
     arrived = [send(give, along_x(mask)) for mask in (1, 2, 3)]
     chunk, gains = call(last_kernel, [((128, 512), b16), ((TAIL, 512), b16)], give, *arrived)
@@ -347,11 +410,13 @@
         [((512, 512), b16)] * 4 + [((512, 1024), b16), ((1024, 512), b16), ((8, 512), b16)],
         where, *own, *other, gains, gains_other, scalars=1,
     )
-    return (*weights, gains[0], gains[1])
-
-
-def gather_features(own):
+    return (output[None], *weights, gains[0], gains[1])
+
+
+def gather_features(own, others):
+    own = send(own, SWAP)
     mine = jnp.concatenate([own] + [send(own, first(mask)) for mask in (1, 2, 3)])
+    mine, others = lax.optimization_barrier((mine, others))
     group = [mine] + [send(mine, second(mask)) for mask in (1, 2, 3)]
     parts = group + [send(part, CORE) for part in group]
     core, y, z = (lax.axis_index(name) for name in ("core", "y", "z"))
@@ -359,7 +424,7 @@
     holder = core ^ side
     block_y = jnp.where(holder == 0, y ^ one, y ^ two)
     block_z = jnp.where(holder == 0, z ^ two, z ^ one)
-    return parts, block_z * 8 + holder * 4 + block_y
+    return parts, block_z * 8 + holder * 4 + block_y, send(others, SWAP)
 
 
 def local(
@@ -376,25 +441,21 @@
     gain_attn,
     gain_mlp,
 ):
-    parts, blocks = gather_features(send(features[0], SWAP))
-    moved = send(jnp.concatenate([queries[0], cotangent[0]]), SWAP)
-    seen = send(visible[0], SWAP)
-    output, grads = device_step(
-        moved[:BLK],
-        jnp.take(seen[0], blocks),
-        moved[BLK:],
-        jnp.concatenate(parts),
-        w_query,
-        w_key,
-        w_value,
-        w_out,
-        w_up,
-        w_down,
-        gain_attn,
-        gain_mlp,
-    )
-    output = send(output, SWAP)
-    return (output[None],) + sum_everywhere(grads)
+    seen = jnp.pad(visible[0].astype(jnp.bfloat16), ((0, 15), (0, 512 - visible.shape[-1])))
+    parts, blocks, moved = gather_features(
+        features[0], jnp.concatenate([queries[0], cotangent[0], seen])
+    )
+    seen = jnp.take(moved[2 * BLK].astype(jnp.float32), blocks)
+    core_at = lax.axis_index("core").astype(jnp.int32).reshape(1)
+    return sum_everywhere(
+        *device_step(
+            core_at,
+            moved,
+            jnp.repeat(seen, BLK).reshape(PARTS, 512),
+            parts,
+            (w_query, w_key, w_value, w_out, w_up, w_down, gain_attn[None], gain_mlp[None]),
+        )
+    )
 
 
 def solution(mesh):

time: 182 us -> 163 us (0.90)
  matrix products: 29 us -> 0 us
  Pallas kernels: 12.5 us -> 36.3 us
  waiting for transfers between devices: 60.2 us -> 49.7 us
  other arithmetic: 9.93 us -> 2.47 us
  starting transfers between devices: 66.2 us -> 71.5 us
    pallas_call x0 -> x1, Pallas kernels: none -> 29.5 us  [device_step(): pl.pallas_call(step_kernel, out_shape=[jax.ShapeDtypeStruct((BLK, 512), b...]
    dot_general x56 -> x0, matrix products: 29 us -> none  [the longest x23 14.2 us: mult(): return jnp.dot(left, right, preferred_element_type=jnp.float32)]
    ppermute x35 -> x34, waiting for transfers between devices: 60.2 us -> 49.7 us  [send(): return lax.ppermute(value, AXES, pairs)]
    pallas_call x6 -> x5, Pallas kernels: 12.5 us -> 6.81 us  [call(): pl.pallas_call(kernel, out_shape=[jax.ShapeDtypeStruct(shape, dtype) for...]
    div x4 -> x0, other arithmetic: 5.32 us -> none  [the longest x1 5.31 us: device_step(): attend = expo / jnp.sum(expo, axis=-1, keepdims=True)]
    ppermute x35 -> x34, starting transfers between devices: 66.2 us -> 71.5 us  [send(): return lax.ppermute(value, AXES, pairs)]
    reduce_sum x4 -> x0, other arithmetic: 1.88 us -> none  [the longest x1 1.41 us: device_step(): attend = expo / jnp.sum(expo, axis=-1, keepdims=True)]
  transfers between devices with their start and end apart: 35 -> 34, of which waited for: 21 -> 20; matrix products, arithmetic and copies ran while one was open for 3% -> 2% of each run, Pallas kernels for 0% -> 0%
where the time goes in v3:
time: 163 us
  starting transfers between devices  71.5 us (44%)
  waiting for transfers between devices  49.7 us (30%)
  Pallas kernels  36.3 us (22%)
  other arithmetic  2.47 us (2%)
  local copies, waits for them, and re-layouts  2.26 us (1%)
    ppermute x34, starting transfers between devices, send(): return lax.ppermute(value, AXES, pairs)  71.5 us
    ppermute x34, waiting for transfers between devices, send(): return lax.ppermute(value, AXES, pairs)  49.7 us
    pallas_call x1, Pallas kernels, device_step(): pl.pallas_call(step_kernel, out_shape=[jax.ShapeDtypeStruct((BLK, 512), b...  29.5 us
    pallas_call x5, Pallas kernels, call(): pl.pallas_call(kernel, out_shape=[jax.ShapeDtypeStruct(shape, dtype) for...  6.81 us
  transfers between devices with their start and end apart: 34, of which 20 were waited for; matrix products, arithmetic and copies ran while one was open for 2% of the time, Pallas kernels for 0%

profile of v3, /device:TPU:1, one launch (start us, length us, event | category | flops | bytes accessed | tf_op | source)
XLA Modules:
  0.0 163.0 jit_solution(7991670150340041661)
XLA Ops:
  0.7 4.6 %collective-permute-start = (bf16[128,512]{1,0:T(8,128)(2,1)}, bf16[128,512]{1,0:T(8,128)(2,1)S(1)}, u32[]{:S(2)}, u32[]{:S(2)}) collective-permute-start(bf16[128,512]{1,0:T(8,128)(2,1)} %bitcast.22), channel_id=1, source_target_pairs={{0,0},{1,1},{2,2},{3,3},{4,32},{5,33},{6,34},{7,35},{8,8},{9,9},{1... | collective-permute-start | bytes 393224 | tf_op jit(solution)/shard_map/ppermute | solution.py:53
  5.3 3.0 %collective-permute-done = bf16[128,512]{1,0:T(8,128)(2,1)S(1)} collective-permute-done((bf16[128,512]{1,0:T(8,128)(2,1)}, bf16[128,512]{1,0:T(8,128)(2,1)S(1)}, u32[]{:S(2)}, u32[]{:S(2)}) %collective-permute-start) | collective-permute-done | bytes 131104 | tf_op jit(solution)/shard_map/ppermute | solution.py:53
  8.4 1.7 %collective-permute-start.1 = (bf16[128,512]{1,0:T(8,128)(2,1)S(1)}, bf16[128,512]{1,0:T(8,128)(2,1)S(1)}, u32[]{:S(2)}, u32[]{:S(2)}) collective-permute-start(bf16[128,512]{1,0:T(8,128)(2,1)S(1)} %collective-permute-done), channel_id=1, source_target_pairs={{0,1},{1,0},{2,3},{3,2},{4,5},{5,4},{6,7},{7,6},{8,9},{9,8},{10,11... | collective-permute-start | bytes 393224 | tf_op jit(solution)/shard_map/ppermute | solution.py:53
  10.1 3.3 %collective-permute-start.2 = (bf16[128,512]{1,0:T(8,128)(2,1)S(1)}, bf16[128,512]{1,0:T(8,128)(2,1)S(1)}, u32[]{:S(2)}, u32[]{:S(2)}) collective-permute-start(bf16[128,512]{1,0:T(8,128)(2,1)S(1)} %collective-permute-done), channel_id=1, source_target_pairs={{0,2},{1,3},{2,0},{3,1},{4,6},{5,7},{6,4},{7,5},{8,10},{9,11},{10,... | collective-permute-start | bytes 393224 | tf_op jit(solution)/shard_map/ppermute | solution.py:53
  15.1 2.1 %collective-permute-done.2 = bf16[128,512]{1,0:T(8,128)(2,1)S(1)} collective-permute-done((bf16[128,512]{1,0:T(8,128)(2,1)S(1)}, bf16[128,512]{1,0:T(8,128)(2,1)S(1)}, u32[]{:S(2)}, u32[]{:S(2)}) %collective-permute-start.2) | collective-permute-done | bytes 131104 | tf_op jit(solution)/shard_map/ppermute | solution.py:53
  18.6 10.3 %collective-permute-start.6 = (bf16[512,512]{1,0:T(8,128)(2,1)S(1)}, bf16[512,512]{1,0:T(8,128)(2,1)S(1)}, u32[]{:S(2)}, u32[]{:S(2)}) collective-permute-start(bf16[512,512]{1,0:T(8,128)(2,1)S(1)} %pad_maximum_fusion.refs_0_), channel_id=1, source_target_pairs={{0,16},{1,17},{2,18},{3,19},{4,20},{5,21},{6,22},{7,23},{8,24},{9,... | collective-permute-start | bytes 1572872 | tf_op jit(solution)/shard_map/ppermute | solution.py:53
  29.3 4.8 %collective-permute-start.4 = (bf16[272,512]{1,0:T(8,128)(2,1)S(1)}, bf16[272,512]{1,0:T(8,128)(2,1)S(1)}, u32[]{:S(2)}, u32[]{:S(2)}) collective-permute-start(bf16[272,512]{1,0:T(8,128)(2,1)S(1)} %fusion.1), channel_id=1, source_target_pairs={{0,0},{1,1},{2,2},{3,3},{4,32},{5,33},{6,34},{7,35},{8,8},{9,9},{1... | collective-permute-start | bytes 835592 | tf_op jit(solution)/shard_map/ppermute | solution.py:53
  35.6 5.6 %collective-permute-done.7.refs_3_ = bf16[512,512]{1,0:T(8,128)(2,1)} collective-permute-done((bf16[512,512]{1,0:T(8,128)(2,1)S(1)}, bf16[512,512]{1,0:T(8,128)(2,1)}, u32[]{:S(2)}, u32[]{:S(2)}) %collective-permute-start.7) | collective-permute-done | bytes 524320 | tf_op jit(solution)/shard_map/ppermute | solution.py:53
  44.3 29.5 %shard_map.214 = (bf16[128,512]{1,0:T(8,128)(2,1)S(1)}, bf16[2064,512]{1,0:T(8,128)(2,1)}, f32[2048,512]{1,0:T(8,128)}, f32[8,512]{1,0:T(8,128)S(1)}) custom-call(s32[1]{0:T(128)} %bitcast.core_ref, bf16[272,512]{1,0:T(8,128)(2,1)S(1)} %collective-permute-done.4.moved, f32[8,512]{1,0:T(8,128)S(1)} %broadcast_bitcast_fusion.seen, ...), custom_call_target="tpu_custom_call" | custom-call | flops 12000000000 | bytes 18000000 | tf_op jit(solution)/shard_map/pallas_call | solution.py:255
  74.0 4.3 %collective-permute-done.13.refs_3_ = bf16[2064,512]{1,0:T(8,128)(2,1)S(1)} collective-permute-done((bf16[2064,512]{1,0:T(8,128)(2,1)}, bf16[2064,512]{1,0:T(8,128)(2,1)S(1)}, u32[]{:S(2)}, u32[]{:S(2)}) %collective-permute-start.13) | collective-permute-done | bytes 2113568 | tf_op jit(solution)/shard_map/ppermute | solution.py:53
  78.3 3.5 %shard_map.215 = (bf16[528,512]{1,0:T(8,128)(2,1)}, bf16[528,512]{1,0:T(8,128)(2,1)}, bf16[528,512]{1,0:T(8,128)(2,1)}, f32[512,512]{1,0:T(8,128)S(1)}, f32[8,512]{1,0:T(8,128)S(1)}) custom-call(s32[1]{0:T(128)} %bitcast.10.refs_0_, f32[2048,512]{1,0:T(8,128)} %get-tuple-element.41.refs_1_, f32[8,512]{1,0:T(8,128)S(1)} %get-tuple-element.42.refs_2_, ...), custom_call_target="tpu_custom_call" | custom-call | tf_op jit(solution)/shard_map/pallas_call | solution.py:375
  82.1 3.5 %collective-permute-start.16 = (bf16[528,512]{1,0:T(8,128)(2,1)}, bf16[528,512]{1,0:T(8,128)(2,1)S(1)}, u32[]{:S(2)}, u32[]{:S(2)}) collective-permute-start(bf16[528,512]{1,0:T(8,128)(2,1)} %get-tuple-element.48), channel_id=1, source_target_pairs={{0,3},{1,2},{2,1},{3,0},{4,7},{5,6},{6,5},{7,4},{8,11},{9,10},{10,... | collective-permute-start | bytes 1622024 | tf_op jit(solution)/shard_map/ppermute | solution.py:53
  85.7 4.9 %collective-permute-done.14.refs_3_ = bf16[528,512]{1,0:T(8,128)(2,1)S(1)} collective-permute-done((bf16[528,512]{1,0:T(8,128)(2,1)}, bf16[528,512]{1,0:T(8,128)(2,1)S(1)}, u32[]{:S(2)}, u32[]{:S(2)}) %collective-permute-start.14) | collective-permute-done | bytes 540704 | tf_op jit(solution)/shard_map/ppermute | solution.py:53
  90.5 4.7 %collective-permute-done.15.refs_4_ = bf16[528,512]{1,0:T(8,128)(2,1)S(1)} collective-permute-done((bf16[528,512]{1,0:T(8,128)(2,1)}, bf16[528,512]{1,0:T(8,128)(2,1)S(1)}, u32[]{:S(2)}, u32[]{:S(2)}) %collective-permute-start.15) | collective-permute-done | bytes 540704 | tf_op jit(solution)/shard_map/ppermute | solution.py:53
  95.2 3.5 %collective-permute-done.16.refs_5_ = bf16[528,512]{1,0:T(8,128)(2,1)S(1)} collective-permute-done((bf16[528,512]{1,0:T(8,128)(2,1)}, bf16[528,512]{1,0:T(8,128)(2,1)S(1)}, u32[]{:S(2)}, u32[]{:S(2)}) %collective-permute-start.16) | collective-permute-done | bytes 540704 | tf_op jit(solution)/shard_map/ppermute | solution.py:53
  99.7 3.2 %collective-permute-start.18 = (bf16[144,512]{1,0:T(8,128)(2,1)S(1)}, bf16[144,512]{1,0:T(8,128)(2,1)S(1)}, u32[]{:S(2)}, u32[]{:S(2)}) collective-permute-start(bf16[144,512]{1,0:T(8,128)(2,1)S(1)} %get-tuple-element.50), channel_id=1, source_target_pairs={{0,16},{1,17},{2,18},{3,19},{4,20},{5,21},{6,22},{7,23},{8,24},{9,... | collective-permute-start | bytes 442376 | tf_op jit(solution)/shard_map/ppermute | solution.py:53
  102.9 8.5 %collective-permute-start.12 = (bf16[128,512]{1,0:T(8,128)(2,1)S(1)}, bf16[128,512]{1,0:T(8,128)(2,1)S(1)}, u32[]{:S(2)}, u32[]{:S(2)}) collective-permute-start(bf16[128,512]{1,0:T(8,128)(2,1)S(1)} %get-tuple-element.40), channel_id=1, source_target_pairs={{0,0},{1,1},{2,2},{3,3},{4,32},{5,33},{6,34},{7,35},{8,8},{9,9},{1... | collective-permute-start | bytes 393224 | tf_op jit(solution)/shard_map/ppermute | solution.py:53
  111.4 2.8 %collective-permute-done.12 = bf16[128,512]{1,0:T(8,128)(2,1)S(1)} collective-permute-done((bf16[128,512]{1,0:T(8,128)(2,1)S(1)}, bf16[128,512]{1,0:T(8,128)(2,1)S(1)}, u32[]{:S(2)}, u32[]{:S(2)}) %collective-permute-start.12) | collective-permute-done | bytes 131104 | tf_op jit(solution)/shard_map/ppermute | solution.py:53
  114.4 2.5 %collective-permute-start.21 = (bf16[144,512]{1,0:T(8,128)(2,1)S(1)}, bf16[144,512]{1,0:T(8,128)(2,1)S(1)}, u32[]{:S(2)}, u32[]{:S(2)}) collective-permute-start(bf16[144,512]{1,0:T(8,128)(2,1)S(1)} %shard_map.217.own_ref), channel_id=1, source_target_pairs={{0,64},{1,65},{2,66},{3,67},{4,68},{5,69},{6,70},{7,71},{8,72},{9,... | collective-permute-start | bytes 442376 | tf_op jit(solution)/shard_map/ppermute | solution.py:53
  118.3 1.6 %collective-permute-done.20.refs_0_ = bf16[144,512]{1,0:T(8,128)(2,1)S(1)} collective-permute-done((bf16[144,512]{1,0:T(8,128)(2,1)S(1)}, bf16[144,512]{1,0:T(8,128)(2,1)S(1)}, u32[]{:S(2)}, u32[]{:S(2)}) %collective-permute-start.20) | collective-permute-done | bytes 147488 | tf_op jit(solution)/shard_map/ppermute | solution.py:53
  119.9 2.0 %collective-permute-done.21.refs_1_ = bf16[144,512]{1,0:T(8,128)(2,1)S(1)} collective-permute-done((bf16[144,512]{1,0:T(8,128)(2,1)S(1)}, bf16[144,512]{1,0:T(8,128)(2,1)S(1)}, u32[]{:S(2)}, u32[]{:S(2)}) %collective-permute-start.21) | collective-permute-done | bytes 147488 | tf_op jit(solution)/shard_map/ppermute | solution.py:53
  121.9 2.9 %collective-permute-done.22.refs_2_ = bf16[144,512]{1,0:T(8,128)(2,1)S(1)} collective-permute-done((bf16[144,512]{1,0:T(8,128)(2,1)S(1)}, bf16[144,512]{1,0:T(8,128)(2,1)S(1)}, u32[]{:S(2)}, u32[]{:S(2)}) %collective-permute-start.22) | collective-permute-done | bytes 147488 | tf_op jit(solution)/shard_map/ppermute | solution.py:53
  125.0 2.8 %collective-permute-start.24 = (bf16[128,512]{1,0:T(8,128)(2,1)S(1)}, bf16[128,512]{1,0:T(8,128)(2,1)S(1)}, u32[]{:S(2)}, u32[]{:S(2)}) collective-permute-start(bf16[128,512]{1,0:T(8,128)(2,1)S(1)} %get-tuple-element.58), channel_id=1, source_target_pairs={{0,16},{1,17},{2,18},{3,19},{4,20},{5,21},{6,22},{7,23},{8,24},{9,... | collective-permute-start | bytes 393224 | tf_op jit(solution)/shard_map/ppermute | solution.py:53
  128.9 2.6 %collective-permute-done.24 = bf16[128,512]{1,0:T(8,128)(2,1)S(1)} collective-permute-done((bf16[128,512]{1,0:T(8,128)(2,1)S(1)}, bf16[128,512]{1,0:T(8,128)(2,1)S(1)}, u32[]{:S(2)}, u32[]{:S(2)}) %collective-permute-start.24) | collective-permute-done | bytes 131104 | tf_op jit(solution)/shard_map/ppermute | solution.py:53
  133.0 4.5 %collective-permute-start.27 = (bf16[512,512]{1,0:T(8,128)(2,1)S(1)}, bf16[512,512]{1,0:T(8,128)(2,1)S(1)}, u32[]{:S(2)}, u32[]{:S(2)}) collective-permute-start(bf16[512,512]{1,0:T(8,128)(2,1)S(1)} %constant_dynamic-update-slice_fusion.refs_0_), channel_id=1, source_target_pairs={{0,2},{1,3},{2,0},{3,1},{4,6},{5,7},{6,4},{7,5},{8,10},{9,11},{10,... | collective-permute-start | bytes 1572872 | tf_op jit(solution)/shard_map/ppermute | solution.py:53
  137.5 5.1 %collective-permute-start.29 = (bf16[512,512]{1,0:T(8,128)(2,1)S(1)}, bf16[512,512]{1,0:T(8,128)(2,1)S(1)}, u32[]{:S(2)}, u32[]{:S(2)}) collective-permute-start(bf16[512,512]{1,0:T(8,128)(2,1)S(1)} %constant_dynamic-update-slice_fusion.refs_0_), channel_id=1, source_target_pairs={{0,32},{1,33},{2,34},{3,35},{4,36},{5,37},{6,38},{7,39},{8,40},{9,... | collective-permute-start | bytes 1572872 | tf_op jit(solution)/shard_map/ppermute | solution.py:53
  142.6 4.5 %collective-permute-start.30 = (bf16[512,512]{1,0:T(8,128)(2,1)S(1)}, bf16[512,512]{1,0:T(8,128)(2,1)S(1)}, u32[]{:S(2)}, u32[]{:S(2)}) collective-permute-start(bf16[512,512]{1,0:T(8,128)(2,1)S(1)} %collective-permute-done.26.refs_1_), channel_id=1, source_target_pairs={{0,32},{1,33},{2,34},{3,35},{4,36},{5,37},{6,38},{7,39},{8,40},{9,... | collective-permute-start | bytes 1572872 | tf_op jit(solution)/shard_map/ppermute | solution.py:53
  147.1 2.9 %collective-permute-done.27.refs_2_ = bf16[512,512]{1,0:T(8,128)(2,1)S(1)} collective-permute-done((bf16[512,512]{1,0:T(8,128)(2,1)S(1)}, bf16[512,512]{1,0:T(8,128)(2,1)S(1)}, u32[]{:S(2)}, u32[]{:S(2)}) %collective-permute-start.27) | collective-permute-done | bytes 524320 | tf_op jit(solution)/shard_map/ppermute | solution.py:53
  150.0 4.1 %collective-permute-start.31 = (bf16[512,512]{1,0:T(8,128)(2,1)S(1)}, bf16[512,512]{1,0:T(8,128)(2,1)S(1)}, u32[]{:S(2)}, u32[]{:S(2)}) collective-permute-start(bf16[512,512]{1,0:T(8,128)(2,1)S(1)} %collective-permute-done.27.refs_2_), channel_id=1, source_target_pairs={{0,32},{1,33},{2,34},{3,35},{4,36},{5,37},{6,38},{7,39},{8,40},{9,... | collective-permute-start | bytes 1572872 | tf_op jit(solution)/shard_map/ppermute | solution.py:53
  154.2 3.1 %collective-permute-start.32 = (bf16[512,512]{1,0:T(8,128)(2,1)S(1)}, bf16[512,512]{1,0:T(8,128)(2,1)S(1)}, u32[]{:S(2)}, u32[]{:S(2)}) collective-permute-start(bf16[512,512]{1,0:T(8,128)(2,1)S(1)} %collective-permute-done.28.refs_3_), channel_id=1, source_target_pairs={{0,32},{1,33},{2,34},{3,35},{4,36},{5,37},{6,38},{7,39},{8,40},{9,... | collective-permute-start | bytes 1572872 | tf_op jit(solution)/shard_map/ppermute | solution.py:53
  157.4 1.5 collective-permute-done.33.refs_9_
  158.9 2.9 %shard_map.219 = (bf16[512,512]{1,0:T(8,128)(2,1)}, bf16[512,512]{1,0:T(8,128)(2,1)}, bf16[512,512]{1,0:T(8,128)(2,1)}, bf16[512,512]{1,0:T(8,128)(2,1)}, bf16[5...) custom-call(s32[3]{0:T(128)S(1)} %pad_add_fusion.where_ref, ...), custom_call_target="tpu_custom_call" | custom-call | tf_op jit(solution)/shard_map/pallas_call | solution.py:375
  (74 shorter events, 15.1 us)
Async XLA Ops:
  0.7 7.7 %collective-permute-start = (bf16[128,512]{1,0:T(8,128)(2,1)}, bf16[128,512]{1,0:T(8,128)(2,1)S(1)}, u32[]{:S(2)}, u32[]{:S(2)}) collective-permute-start(bf16[128,512]{1,0:T(8,128)(2,1)} %bitcast.22), channel_id=1, source_target_pairs={{0,0},{1,1},{2,2},{3,3},{4,32},{5,33},{6,34},{7,35},{8,8},{9,9},{1... | collective-permute-start | bytes 393224 | tf_op jit(solution)/shard_map/ppermute | solution.py:53
  8.4 6.7 %collective-permute-start.1 = (bf16[128,512]{1,0:T(8,128)(2,1)S(1)}, bf16[128,512]{1,0:T(8,128)(2,1)S(1)}, u32[]{:S(2)}, u32[]{:S(2)}) collective-permute-start(bf16[128,512]{1,0:T(8,128)(2,1)S(1)} %collective-permute-done), channel_id=1, source_target_pairs={{0,1},{1,0},{2,3},{3,2},{4,5},{5,4},{6,7},{7,6},{8,9},{9,8},{10,11... | collective-permute-start | bytes 393224 | tf_op jit(solution)/shard_map/ppermute | solution.py:53
  10.1 7.1 %collective-permute-start.2 = (bf16[128,512]{1,0:T(8,128)(2,1)S(1)}, bf16[128,512]{1,0:T(8,128)(2,1)S(1)}, u32[]{:S(2)}, u32[]{:S(2)}) collective-permute-start(bf16[128,512]{1,0:T(8,128)(2,1)S(1)} %collective-permute-done), channel_id=1, source_target_pairs={{0,2},{1,3},{2,0},{3,1},{4,6},{5,7},{6,4},{7,5},{8,10},{9,11},{10,... | collective-permute-start | bytes 393224 | tf_op jit(solution)/shard_map/ppermute | solution.py:53
  13.4 5.2 %collective-permute-start.3 = (bf16[128,512]{1,0:T(8,128)(2,1)S(1)}, bf16[128,512]{1,0:T(8,128)(2,1)S(1)}, u32[]{:S(2)}, u32[]{:S(2)}) collective-permute-start(bf16[128,512]{1,0:T(8,128)(2,1)S(1)} %collective-permute-done), channel_id=1, source_target_pairs={{0,3},{1,2},{2,1},{3,0},{4,7},{5,6},{6,5},{7,4},{8,11},{9,10},{10,... | collective-permute-start | bytes 393224 | tf_op jit(solution)/shard_map/ppermute | solution.py:53
  18.6 17.0 %collective-permute-start.6 = (bf16[512,512]{1,0:T(8,128)(2,1)S(1)}, bf16[512,512]{1,0:T(8,128)(2,1)S(1)}, u32[]{:S(2)}, u32[]{:S(2)}) collective-permute-start(bf16[512,512]{1,0:T(8,128)(2,1)S(1)} %pad_maximum_fusion.refs_0_), channel_id=1, source_target_pairs={{0,16},{1,17},{2,18},{3,19},{4,20},{5,21},{6,22},{7,23},{8,24},{9,... | collective-permute-start | bytes 1572872 | tf_op jit(solution)/shard_map/ppermute | solution.py:53
  28.9 12.3 %collective-permute-start.7 = (bf16[512,512]{1,0:T(8,128)(2,1)S(1)}, bf16[512,512]{1,0:T(8,128)(2,1)}, u32[]{:S(2)}, u32[]{:S(2)}) collective-permute-start(bf16[512,512]{1,0:T(8,128)(2,1)S(1)} %pad_maximum_fusion.refs_0_), channel_id=1, source_target_pairs={{0,24},{1,25},{2,26},{3,27},{4,28},{5,29},{6,30},{7,31},{8,16},{9,... | collective-permute-start | bytes 1572872 | tf_op jit(solution)/shard_map/ppermute | solution.py:53
  29.3 12.2 %collective-permute-start.5 = (bf16[512,512]{1,0:T(8,128)(2,1)S(1)}, bf16[512,512]{1,0:T(8,128)(2,1)}, u32[]{:S(2)}, u32[]{:S(2)}) collective-permute-start(bf16[512,512]{1,0:T(8,128)(2,1)S(1)} %pad_maximum_fusion.refs_0_), channel_id=1, source_target_pairs={{0,8},{1,9},{2,10},{3,11},{4,12},{5,13},{6,14},{7,15},{8,0},{9,1},... | collective-permute-start | bytes 1572872 | tf_op jit(solution)/shard_map/ppermute | solution.py:53
  29.3 12.4 %collective-permute-start.4 = (bf16[272,512]{1,0:T(8,128)(2,1)S(1)}, bf16[272,512]{1,0:T(8,128)(2,1)S(1)}, u32[]{:S(2)}, u32[]{:S(2)}) collective-permute-start(bf16[272,512]{1,0:T(8,128)(2,1)S(1)} %fusion.1), channel_id=1, source_target_pairs={{0,0},{1,1},{2,2},{3,3},{4,32},{5,33},{6,34},{7,35},{8,8},{9,9},{1... | collective-permute-start | bytes 835592 | tf_op jit(solution)/shard_map/ppermute | solution.py:53
  34.9 7.8 %collective-permute-start.8 = (bf16[512,512]{1,0:T(8,128)(2,1)S(1)}, bf16[512,512]{1,0:T(8,128)(2,1)}, u32[]{:S(2)}, u32[]{:S(2)}) collective-permute-start(bf16[512,512]{1,0:T(8,128)(2,1)S(1)} %pad_maximum_fusion.refs_0_), channel_id=1, source_target_pairs={{0,32},{1,33},{2,34},{3,35},{4,36},{5,37},{6,38},{7,39},{8,40},{9,... | collective-permute-start | bytes 1572872 | tf_op jit(solution)/shard_map/ppermute | solution.py:53
  35.6 7.1 %collective-permute-start.10 = (bf16[512,512]{1,0:T(8,128)(2,1)S(1)}, bf16[512,512]{1,0:T(8,128)(2,1)}, u32[]{:S(2)}, u32[]{:S(2)}) collective-permute-start(bf16[512,512]{1,0:T(8,128)(2,1)S(1)} %collective-permute-done.6.refs_2_), channel_id=1, source_target_pairs={{0,32},{1,33},{2,34},{3,35},{4,36},{5,37},{6,38},{7,39},{8,40},{9,... | collective-permute-start | bytes 1572872 | tf_op jit(solution)/shard_map/ppermute | solution.py:53
  41.5 2.7 %collective-permute-start.9 = (bf16[512,512]{1,0:T(8,128)(2,1)}, bf16[512,512]{1,0:T(8,128)(2,1)}, u32[]{:S(2)}, u32[]{:S(2)}) collective-permute-start(bf16[512,512]{1,0:T(8,128)(2,1)} %collective-permute-done.5.refs_1_), channel_id=1, source_target_pairs={{0,32},{1,33},{2,34},{3,35},{4,36},{5,37},{6,38},{7,39},{8,40},{9,... | collective-permute-start | bytes 1572872 | tf_op jit(solution)/shard_map/ppermute | solution.py:53
  73.8 4.5 %collective-permute-start.13 = (bf16[2064,512]{1,0:T(8,128)(2,1)}, bf16[2064,512]{1,0:T(8,128)(2,1)S(1)}, u32[]{:S(2)}, u32[]{:S(2)}) collective-permute-start(bf16[2064,512]{1,0:T(8,128)(2,1)} %get-tuple-element.43), channel_id=1, source_target_pairs={{0,32},{1,33},{2,34},{3,35},{4,36},{5,37},{6,38},{7,39},{8,40},{9,... | collective-permute-start | bytes 6340616 | tf_op jit(solution)/shard_map/ppermute | solution.py:53
  81.8 8.7 %collective-permute-start.14 = (bf16[528,512]{1,0:T(8,128)(2,1)}, bf16[528,512]{1,0:T(8,128)(2,1)S(1)}, u32[]{:S(2)}, u32[]{:S(2)}) collective-permute-start(bf16[528,512]{1,0:T(8,128)(2,1)} %get-tuple-element.46), channel_id=1, source_target_pairs={{0,1},{1,0},{2,3},{3,2},{4,5},{5,4},{6,7},{7,6},{8,9},{9,8},{10,11... | collective-permute-start | bytes 1622024 | tf_op jit(solution)/shard_map/ppermute | solution.py:53
  81.8 13.4 %collective-permute-start.15 = (bf16[528,512]{1,0:T(8,128)(2,1)}, bf16[528,512]{1,0:T(8,128)(2,1)S(1)}, u32[]{:S(2)}, u32[]{:S(2)}) collective-permute-start(bf16[528,512]{1,0:T(8,128)(2,1)} %get-tuple-element.47), channel_id=1, source_target_pairs={{0,2},{1,3},{2,0},{3,1},{4,6},{5,7},{6,4},{7,5},{8,10},{9,11},{10,... | collective-permute-start | bytes 1622024 | tf_op jit(solution)/shard_map/ppermute | solution.py:53
  82.1 16.6 %collective-permute-start.16 = (bf16[528,512]{1,0:T(8,128)(2,1)}, bf16[528,512]{1,0:T(8,128)(2,1)S(1)}, u32[]{:S(2)}, u32[]{:S(2)}) collective-permute-start(bf16[528,512]{1,0:T(8,128)(2,1)} %get-tuple-element.48), channel_id=1, source_target_pairs={{0,3},{1,2},{2,1},{3,0},{4,7},{5,6},{6,5},{7,4},{8,11},{9,10},{10,... | collective-permute-start | bytes 1622024 | tf_op jit(solution)/shard_map/ppermute | solution.py:53
  98.9 15.3 %collective-permute-start.17 = (bf16[144,512]{1,0:T(8,128)(2,1)S(1)}, bf16[144,512]{1,0:T(8,128)(2,1)S(1)}, u32[]{:S(2)}, u32[]{:S(2)}) collective-permute-start(bf16[144,512]{1,0:T(8,128)(2,1)S(1)} %get-tuple-element.49), channel_id=1, source_target_pairs={{0,8},{1,9},{2,10},{3,11},{4,12},{5,13},{6,14},{7,15},{8,0},{9,1},... | collective-permute-start | bytes 442376 | tf_op jit(solution)/shard_map/ppermute | solution.py:53
  99.7 14.6 %collective-permute-start.18 = (bf16[144,512]{1,0:T(8,128)(2,1)S(1)}, bf16[144,512]{1,0:T(8,128)(2,1)S(1)}, u32[]{:S(2)}, u32[]{:S(2)}) collective-permute-start(bf16[144,512]{1,0:T(8,128)(2,1)S(1)} %get-tuple-element.50), channel_id=1, source_target_pairs={{0,16},{1,17},{2,18},{3,19},{4,20},{5,21},{6,22},{7,23},{8,24},{9,... | collective-permute-start | bytes 442376 | tf_op jit(solution)/shard_map/ppermute | solution.py:53
  102.8 11.4 %collective-permute-start.19 = (bf16[144,512]{1,0:T(8,128)(2,1)S(1)}, bf16[144,512]{1,0:T(8,128)(2,1)S(1)}, u32[]{:S(2)}, u32[]{:S(2)}) collective-permute-start(bf16[144,512]{1,0:T(8,128)(2,1)S(1)} %get-tuple-element.51), channel_id=1, source_target_pairs={{0,24},{1,25},{2,26},{3,27},{4,28},{5,29},{6,30},{7,31},{8,16},{9,... | collective-permute-start | bytes 442376 | tf_op jit(solution)/shard_map/ppermute | solution.py:53
  102.9 11.4 %collective-permute-start.12 = (bf16[128,512]{1,0:T(8,128)(2,1)S(1)}, bf16[128,512]{1,0:T(8,128)(2,1)S(1)}, u32[]{:S(2)}, u32[]{:S(2)}) collective-permute-start(bf16[128,512]{1,0:T(8,128)(2,1)S(1)} %get-tuple-element.40), channel_id=1, source_target_pairs={{0,0},{1,1},{2,2},{3,3},{4,32},{5,33},{6,34},{7,35},{8,8},{9,9},{1... | collective-permute-start | bytes 393224 | tf_op jit(solution)/shard_map/ppermute | solution.py:53
  114.3 5.6 %collective-permute-start.20 = (bf16[144,512]{1,0:T(8,128)(2,1)S(1)}, bf16[144,512]{1,0:T(8,128)(2,1)S(1)}, u32[]{:S(2)}, u32[]{:S(2)}) collective-permute-start(bf16[144,512]{1,0:T(8,128)(2,1)S(1)} %shard_map.217.own_ref), channel_id=1, source_target_pairs={{0,4},{1,5},{2,6},{3,7},{4,0},{5,1},{6,2},{7,3},{8,12},{9,13},{10,... | collective-permute-start | bytes 442376 | tf_op jit(solution)/shard_map/ppermute | solution.py:53
  114.4 7.5 %collective-permute-start.21 = (bf16[144,512]{1,0:T(8,128)(2,1)S(1)}, bf16[144,512]{1,0:T(8,128)(2,1)S(1)}, u32[]{:S(2)}, u32[]{:S(2)}) collective-permute-start(bf16[144,512]{1,0:T(8,128)(2,1)S(1)} %shard_map.217.own_ref), channel_id=1, source_target_pairs={{0,64},{1,65},{2,66},{3,67},{4,68},{5,69},{6,70},{7,71},{8,72},{9,... | collective-permute-start | bytes 442376 | tf_op jit(solution)/shard_map/ppermute | solution.py:53
  117.0 7.8 %collective-permute-start.22 = (bf16[144,512]{1,0:T(8,128)(2,1)S(1)}, bf16[144,512]{1,0:T(8,128)(2,1)S(1)}, u32[]{:S(2)}, u32[]{:S(2)}) collective-permute-start(bf16[144,512]{1,0:T(8,128)(2,1)S(1)} %shard_map.217.own_ref), channel_id=1, source_target_pairs={{0,68},{1,69},{2,70},{3,71},{4,64},{5,65},{6,66},{7,67},{8,76},{9,... | collective-permute-start | bytes 442376 | tf_op jit(solution)/shard_map/ppermute | solution.py:53
  124.9 4.0 %collective-permute-start.23 = (bf16[128,512]{1,0:T(8,128)(2,1)S(1)}, bf16[128,512]{1,0:T(8,128)(2,1)S(1)}, u32[]{:S(2)}, u32[]{:S(2)}) collective-permute-start(bf16[128,512]{1,0:T(8,128)(2,1)S(1)} %get-tuple-element.58), channel_id=1, source_target_pairs={{0,8},{1,9},{2,10},{3,11},{4,12},{5,13},{6,14},{7,15},{8,0},{9,1},... | collective-permute-start | bytes 393224 | tf_op jit(solution)/shard_map/ppermute | solution.py:53
  125.0 6.6 %collective-permute-start.24 = (bf16[128,512]{1,0:T(8,128)(2,1)S(1)}, bf16[128,512]{1,0:T(8,128)(2,1)S(1)}, u32[]{:S(2)}, u32[]{:S(2)}) collective-permute-start(bf16[128,512]{1,0:T(8,128)(2,1)S(1)} %get-tuple-element.58), channel_id=1, source_target_pairs={{0,16},{1,17},{2,18},{3,19},{4,20},{5,21},{6,22},{7,23},{8,24},{9,... | collective-permute-start | bytes 393224 | tf_op jit(solution)/shard_map/ppermute | solution.py:53
  127.8 5.1 %collective-permute-start.25 = (bf16[128,512]{1,0:T(8,128)(2,1)S(1)}, bf16[128,512]{1,0:T(8,128)(2,1)S(1)}, u32[]{:S(2)}, u32[]{:S(2)}) collective-permute-start(bf16[128,512]{1,0:T(8,128)(2,1)S(1)} %get-tuple-element.58), channel_id=1, source_target_pairs={{0,24},{1,25},{2,26},{3,27},{4,28},{5,29},{6,30},{7,31},{8,16},{9,... | collective-permute-start | bytes 393224 | tf_op jit(solution)/shard_map/ppermute | solution.py:53
  132.9 9.7 %collective-permute-start.26 = (bf16[512,512]{1,0:T(8,128)(2,1)S(1)}, bf16[512,512]{1,0:T(8,128)(2,1)S(1)}, u32[]{:S(2)}, u32[]{:S(2)}) collective-permute-start(bf16[512,512]{1,0:T(8,128)(2,1)S(1)} %constant_dynamic-update-slice_fusion.refs_0_), channel_id=1, source_target_pairs={{0,1},{1,0},{2,3},{3,2},{4,5},{5,4},{6,7},{7,6},{8,9},{9,8},{10,11... | collective-permute-start | bytes 1572872 | tf_op jit(solution)/shard_map/ppermute | solution.py:53
  133.0 17.0 %collective-permute-start.27 = (bf16[512,512]{1,0:T(8,128)(2,1)S(1)}, bf16[512,512]{1,0:T(8,128)(2,1)S(1)}, u32[]{:S(2)}, u32[]{:S(2)}) collective-permute-start(bf16[512,512]{1,0:T(8,128)(2,1)S(1)} %constant_dynamic-update-slice_fusion.refs_0_), channel_id=1, source_target_pairs={{0,2},{1,3},{2,0},{3,1},{4,6},{5,7},{6,4},{7,5},{8,10},{9,11},{10,... | collective-permute-start | bytes 1572872 | tf_op jit(solution)/shard_map/ppermute | solution.py:53
  137.5 16.7 %collective-permute-start.28 = (bf16[512,512]{1,0:T(8,128)(2,1)S(1)}, bf16[512,512]{1,0:T(8,128)(2,1)S(1)}, u32[]{:S(2)}, u32[]{:S(2)}) collective-permute-start(bf16[512,512]{1,0:T(8,128)(2,1)S(1)} %constant_dynamic-update-slice_fusion.refs_0_), channel_id=1, source_target_pairs={{0,3},{1,2},{2,1},{3,0},{4,7},{5,6},{6,5},{7,4},{8,11},{9,10},{10,... | collective-permute-start | bytes 1572872 | tf_op jit(solution)/shard_map/ppermute | solution.py:53
  137.5 21.4 %collective-permute-start.29 = (bf16[512,512]{1,0:T(8,128)(2,1)S(1)}, bf16[512,512]{1,0:T(8,128)(2,1)S(1)}, u32[]{:S(2)}, u32[]{:S(2)}) collective-permute-start(bf16[512,512]{1,0:T(8,128)(2,1)S(1)} %constant_dynamic-update-slice_fusion.refs_0_), channel_id=1, source_target_pairs={{0,32},{1,33},{2,34},{3,35},{4,36},{5,37},{6,38},{7,39},{8,40},{9,... | collective-permute-start | bytes 1572872 | tf_op jit(solution)/shard_map/ppermute | solution.py:53
  142.6 16.2 %collective-permute-start.30 = (bf16[512,512]{1,0:T(8,128)(2,1)S(1)}, bf16[512,512]{1,0:T(8,128)(2,1)S(1)}, u32[]{:S(2)}, u32[]{:S(2)}) collective-permute-start(bf16[512,512]{1,0:T(8,128)(2,1)S(1)} %collective-permute-done.26.refs_1_), channel_id=1, source_target_pairs={{0,32},{1,33},{2,34},{3,35},{4,36},{5,37},{6,38},{7,39},{8,40},{9,... | collective-permute-start | bytes 1572872 | tf_op jit(solution)/shard_map/ppermute | solution.py:53
  150.0 8.8 %collective-permute-start.31 = (bf16[512,512]{1,0:T(8,128)(2,1)S(1)}, bf16[512,512]{1,0:T(8,128)(2,1)S(1)}, u32[]{:S(2)}, u32[]{:S(2)}) collective-permute-start(bf16[512,512]{1,0:T(8,128)(2,1)S(1)} %collective-permute-done.27.refs_2_), channel_id=1, source_target_pairs={{0,32},{1,33},{2,34},{3,35},{4,36},{5,37},{6,38},{7,39},{8,40},{9,... | collective-permute-start | bytes 1572872 | tf_op jit(solution)/shard_map/ppermute | solution.py:53
  154.2 4.7 %collective-permute-start.32 = (bf16[512,512]{1,0:T(8,128)(2,1)S(1)}, bf16[512,512]{1,0:T(8,128)(2,1)S(1)}, u32[]{:S(2)}, u32[]{:S(2)}) collective-permute-start(bf16[512,512]{1,0:T(8,128)(2,1)S(1)} %collective-permute-done.28.refs_3_), channel_id=1, source_target_pairs={{0,32},{1,33},{2,34},{3,35},{4,36},{5,37},{6,38},{7,39},{8,40},{9,... | collective-permute-start | bytes 1572872 | tf_op jit(solution)/shard_map/ppermute | solution.py:53
  (9 other events, 256.1 us)

commit v4 on v3

--- a/solution.py
+++ b/solution.py
@@ -37,6 +37,11 @@
     return pairs_of(
         lambda xh, c, z, xl, y: (xh, c, z, xl, y ^ mask) if c == 0 else (xh, c, z ^ mask, xl, y)
     )
+
+
+def first_swapped(mask):
+    after = dict(first(mask))
+    return [(source, after[target]) for source, target in SWAP]
 
 
 def second(mask):
@@ -118,42 +123,47 @@
     normed_b = normed.astype(b16)
     query_rows = mult(normed_b, w_query[...]).astype(b16)
 
+    blank = jnp.zeros((BLK, head), b16)
+    query_pairs = jnp.concatenate(
+        [
+            jnp.concatenate(
+                [query_rows[:, c] if h % 2 == side else blank for side in range(2)], axis=1
+            )
+            for h, c in enumerate(cols)
+        ],
+        axis=0,
+    )
+    pair_rows = [slice(0, 2 * BLK), slice(2 * BLK, 4 * BLK)]
+    pair_cols = [slice(0, 2 * head), slice(2 * head, 4 * head)]
+
     stat[...] = jnp.full_like(stat, -1e30)
 
-    for copy in copies:
-        copy.wait()
-
-    def score(p, carry):
+    for p in range(PARTS):
+        copies[p].wait()
         key_rows = mult(feats[p], w_key[...]).astype(b16)
-        allowed = seen[pl.ds(p, 1), :] > 0
-        for r, c in zip(heads, cols):
-            part = mult_nt(query_rows[:, c], key_rows[:, c]) * factor
+        allowed = seen[p : p + 1, :] > 0
+        for r, c in zip(pair_rows, pair_cols):
+            part = mult_nt(query_pairs[r, :], key_rows[:, c]) * factor
             part = jnp.where(allowed, part, -1e30)
             scores[p, r, :] = part
             stat[r, :] = jnp.maximum(stat[r, :], lanes(part, jnp.maximum))
-        return carry
-
-    lax.fori_loop(0, PARTS, score, 0)
+
     highest = jnp.max(stat[...], axis=-1, keepdims=True)
     stat[...] = jnp.zeros_like(stat)
 
-    def expo(p, carry):
+    for p in range(PARTS):
         part = jnp.exp(scores[p] - highest)
         scores[p] = part
         stat[...] += lanes(part, jnp.add)
-        return carry
-
-    lax.fori_loop(0, PARTS, expo, 0)
+
     inverse_sum = 1.0 / jnp.sum(stat[...], axis=-1, keepdims=True)
     sums[...] = jnp.zeros_like(sums)
 
-    def attend(p, carry):
+    for p in range(PARTS):
         part = scores[p] * inverse_sum
         scores[p] = part
         sums[...] += mult(part.astype(b16), feats[p])
-        return carry
-
-    lax.fori_loop(0, PARTS, attend, 0)
+
     u_high, u_low = two_parts(sums[...])
     context = jnp.concatenate(
         [mult(u_high[r], w_value[:, c]) + mult(u_low[r], w_value[:, c]) for r, c in zip(heads, cols)],
@@ -166,7 +176,7 @@
     def store(at, rows, grad):
         middle = grad.shape[0] // 2
         low, high = grad[:middle], grad[middle:]
-        mine = jnp.where(core == 0, low, high)
+        mine = jnp.where(core == 0, low, high).astype(b16)
         yours = jnp.where(core == 0, high, low).astype(b16)
         for i in range(half):
             keep[i * CHUNK + at : i * CHUNK + at + rows, :] = mine[i * rows : (i + 1) * rows]
@@ -210,22 +220,18 @@
     ).astype(b16)
     stat[...] = jnp.zeros_like(stat)
 
-    def pull(p, carry):
+    for p in range(PARTS):
         part = mult_nt(pulled, feats[p])
         pulls[p] = part
         stat[...] += lanes(part * scores[p], jnp.add)
-        return carry
-
-    lax.fori_loop(0, PARTS, pull, 0)
+
     centre = jnp.sum(stat[...], axis=-1, keepdims=True)
     sums[...] = jnp.zeros_like(sums)
 
-    def back(p, carry):
+    for p in range(PARTS):
         part = (scores[p] * (pulls[p] - centre) * factor).astype(b16)
         sums[...] += mult(part, feats[p])
-        return carry
-
-    lax.fori_loop(0, PARTS, back, 0)
+
     t_high, t_low = two_parts(sums[...])
     grad_query_rows = jnp.concatenate(
         [mult(t_high[r], w_key[:, c]) + mult(t_low[r], w_key[:, c]) for r, c in zip(heads, cols)],
@@ -257,7 +263,7 @@
         out_shape=[
             jax.ShapeDtypeStruct((BLK, 512), b16),
             jax.ShapeDtypeStruct((2048 + TAIL, 512), b16),
-            jax.ShapeDtypeStruct((2048, 512), f32),
+            jax.ShapeDtypeStruct((2048, 512), b16),
             jax.ShapeDtypeStruct((8, 512), f32),
         ],
         in_specs=[SMEM] + [VMEM] * 10 + [pl.BlockSpec(memory_space=pl.ANY)] * PARTS,
@@ -314,7 +320,7 @@
     total = own_ref.shape[0]
     for mask in range(4):
         at = pl.ds(pl.multiple_of((index ^ mask) * rows, rows), rows)
-        value = own_ref[at, :]
+        value = own_ref[at, :].astype(jnp.float32)
         for ref in arrived:
             value = value + ref[at, :].astype(jnp.float32)
         if mask:
@@ -355,8 +361,8 @@
 
 
 def place_kernel(where_ref, *refs):
-    own, other, gains_own, gains_other = refs[0:4], refs[4:8], refs[8], refs[9]
-    grads, gains_out = refs[10:16], refs[16]
+    own, other, gains_own = refs[0:4], refs[4:8], refs[8]
+    grads, gain_attn, gain_mlp = refs[9:15], refs[15], refs[16]
     core, y, z = where_ref[0], where_ref[1], where_ref[2]
     for side, group in enumerate((own, other)):
         holder = core ^ side
@@ -367,8 +373,9 @@
                 k = holder * 16 + (one ^ m1) * 4 + (two ^ m2)
                 for at, piece in pieces_of(grads, k):
                     piece[...] = group[m1][m2 * CHUNK + at : m2 * CHUNK + at + piece.shape[0], :]
-    gains = jnp.where(core == 0, take_gains(gains_own, 0), take_gains(gains_other, 0))
-    gains_out[...] = gains.astype(jnp.bfloat16)
+    gains = jnp.where(core == 0, take_gains(gains_own, 0), take_gains(other[0], 4 * CHUNK))
+    gain_attn[...] = gains[0].astype(jnp.bfloat16)
+    gain_mlp[...] = gains[1].astype(jnp.bfloat16)
 
 
 def call(kernel, outs, *operands, scalars=0):
@@ -395,27 +402,26 @@
             index, keep, gains, *arrived, scalars=1,
         )
         arrived = [send(give, route(mask)) for mask, give in enumerate(gives, 1)]
-    output, *arrived = lax.optimization_barrier((send(output, SWAP), *arrived))
+        if count == 1:
+            output, *arrived = lax.optimization_barrier((send(output, SWAP), *arrived))
     (give,) = call(chunk_kernel, [((128 + TAIL, 512), b16)], keep, gains, *arrived)
     arrived = [send(give, along_x(mask)) for mask in (1, 2, 3)]
     chunk, gains = call(last_kernel, [((128, 512), b16), ((TAIL, 512), b16)], give, *arrived)
 
     mine = jnp.concatenate([chunk] + [send(chunk, second(mask)) for mask in (1, 2, 3)])
     own = [mine] + [send(mine, first(mask)) for mask in (1, 2, 3)]
-    other = [send(part, CORE) for part in own]
-    gains_other = send(gains, CORE)
+    other = [send(jnp.concatenate([mine, gains]), CORE)] + [send(part, CORE) for part in own[1:]]
     where = jnp.stack([core, y, z]).astype(jnp.int32)
-    *weights, gains = call(
+    placed = call(
         place_kernel,
-        [((512, 512), b16)] * 4 + [((512, 1024), b16), ((1024, 512), b16), ((8, 512), b16)],
-        where, *own, *other, gains, gains_other, scalars=1,
-    )
-    return (output[None], *weights, gains[0], gains[1])
+        [((512, 512), b16)] * 4 + [((512, 1024), b16), ((1024, 512), b16)] + [((512,), b16)] * 2,
+        where, *own, *other, gains, scalars=1,
+    )
+    return (output[None], *placed)
 
 
 def gather_features(own, others):
-    own = send(own, SWAP)
-    mine = jnp.concatenate([own] + [send(own, first(mask)) for mask in (1, 2, 3)])
+    mine = jnp.concatenate([send(own, first_swapped(mask)) for mask in range(4)])
     mine, others = lax.optimization_barrier((mine, others))
     group = [mine] + [send(mine, second(mask)) for mask in (1, 2, 3)]
     parts = group + [send(part, CORE) for part in group]

time: 163 us -> 144 us (0.88)
  starting transfers between devices: 71.5 us -> 63.3 us
  Pallas kernels: 36.3 us -> 29 us
  waiting for transfers between devices: 49.7 us -> 43.9 us
  local copies, waits for them, and re-layouts: 2.26 us -> 4.65 us
    ppermute x34 -> x33, starting transfers between devices: 71.5 us -> 63.3 us  [send(): return lax.ppermute(value, AXES, pairs)]
    pallas_call x1, Pallas kernels: 29.5 us -> 22.8 us  [device_step(): pl.pallas_call(step_kernel, out_shape=[jax.ShapeDtypeStruct((BLK, 512), b...]
    ppermute x34 -> x33, waiting for transfers between devices: 49.7 us -> 43.9 us  [send(): return lax.ppermute(value, AXES, pairs)]
    unnamed x18 -> x23, local copies, waits for them, and re-layouts: 0.71 us -> 3.69 us
  transfers between devices with their start and end apart: 34 -> 33, of which waited for: 20 -> 19; matrix products, arithmetic and copies ran while one was open for 2% -> 2% of each run, Pallas kernels for 0% -> 0%
where the time goes in v4:
time: 144 us
  starting transfers between devices  63.3 us (44%)
  waiting for transfers between devices  43.9 us (30%)
  Pallas kernels  29 us (20%)
  local copies, waits for them, and re-layouts  4.65 us (3%)
  other arithmetic  2.47 us (2%)
    ppermute x33, starting transfers between devices, send(): return lax.ppermute(value, AXES, pairs)  63.3 us
    ppermute x33, waiting for transfers between devices, send(): return lax.ppermute(value, AXES, pairs)  43.9 us
    pallas_call x1, Pallas kernels, device_step(): pl.pallas_call(step_kernel, out_shape=[jax.ShapeDtypeStruct((BLK, 512), b...  22.8 us
    pallas_call x5, Pallas kernels, call(): pl.pallas_call(kernel, out_shape=[jax.ShapeDtypeStruct(shape, dtype) for...  6.17 us
    unnamed x23, local copies, waits for them, and re-layouts  3.69 us
  transfers between devices with their start and end apart: 33, of which 19 were waited for; matrix products, arithmetic and copies ran while one was open for 2% of the time, Pallas kernels for 0%

profile of v4, /device:TPU:1, one launch (start us, length us, event | category | flops | bytes accessed | tf_op | source)
XLA Modules:
  0.0 144.1 jit_solution(16885914755628235116)
XLA Ops:
  0.7 4.6 %collective-permute-start = (bf16[128,512]{1,0:T(8,128)(2,1)}, bf16[128,512]{1,0:T(8,128)(2,1)S(1)}, u32[]{:S(2)}, u32[]{:S(2)}) collective-permute-start(bf16[128,512]{1,0:T(8,128)(2,1)} %bitcast.22), channel_id=1, source_target_pairs={{0,0},{1,1},{2,2},{3,3},{4,32},{5,33},{6,34},{7,35},{8,8},{9,9},{1... | collective-permute-start | bytes 393224 | tf_op jit(solution)/shard_map/ppermute | solution.py:58
  6.4 4.7 %collective-permute-start.2 = (bf16[128,512]{1,0:T(8,128)(2,1)}, bf16[128,512]{1,0:T(8,128)(2,1)S(1)}, u32[]{:S(2)}, u32[]{:S(2)}) collective-permute-start(bf16[128,512]{1,0:T(8,128)(2,1)} %bitcast.24), channel_id=1, source_target_pairs={{0,2},{1,3},{2,0},{3,1},{4,48},{5,49},{6,50},{7,51},{8,10},{9,11},... | collective-permute-start | bytes 393224 | tf_op jit(solution)/shard_map/ppermute | solution.py:58
  11.1 2.0 %collective-permute-start.3 = (bf16[128,512]{1,0:T(8,128)(2,1)}, bf16[128,512]{1,0:T(8,128)(2,1)S(1)}, u32[]{:S(2)}, u32[]{:S(2)}) collective-permute-start(bf16[128,512]{1,0:T(8,128)(2,1)} %bitcast.25), channel_id=1, source_target_pairs={{0,3},{1,2},{2,1},{3,0},{4,56},{5,57},{6,58},{7,59},{8,11},{9,10},... | collective-permute-start | bytes 393224 | tf_op jit(solution)/shard_map/ppermute | solution.py:58
  15.8 2.1 %collective-permute-done.3 = bf16[128,512]{1,0:T(8,128)(2,1)S(1)} collective-permute-done((bf16[128,512]{1,0:T(8,128)(2,1)}, bf16[128,512]{1,0:T(8,128)(2,1)S(1)}, u32[]{:S(2)}, u32[]{:S(2)}) %collective-permute-start.3) | collective-permute-done | bytes 131104 | tf_op jit(solution)/shard_map/ppermute | solution.py:58
  17.9 2.3 %collective-permute-start.6 = (bf16[512,512]{1,0:T(8,128)(2,1)S(1)}, bf16[512,512]{1,0:T(8,128)(2,1)S(1)}, u32[]{:S(2)}, u32[]{:S(2)}) collective-permute-start(bf16[512,512]{1,0:T(8,128)(2,1)S(1)} %pad_maximum_fusion.refs_0_), channel_id=1, source_target_pairs={{0,16},{1,17},{2,18},{3,19},{4,20},{5,21},{6,22},{7,23},{8,24},{9,... | collective-permute-start | bytes 1572872 | tf_op jit(solution)/shard_map/ppermute | solution.py:58
  21.0 3.4 %collective-permute-start.4 = (bf16[272,512]{1,0:T(8,128)(2,1)S(1)}, bf16[272,512]{1,0:T(8,128)(2,1)S(1)}, u32[]{:S(2)}, u32[]{:S(2)}) collective-permute-start(bf16[272,512]{1,0:T(8,128)(2,1)S(1)} %fusion.1), channel_id=1, source_target_pairs={{0,0},{1,1},{2,2},{3,3},{4,32},{5,33},{6,34},{7,35},{8,8},{9,9},{1... | collective-permute-start | bytes 835592 | tf_op jit(solution)/shard_map/ppermute | solution.py:58
  25.2 2.4 %collective-permute-done.6.refs_2_ = bf16[512,512]{1,0:T(8,128)(2,1)S(1)} collective-permute-done((bf16[512,512]{1,0:T(8,128)(2,1)S(1)}, bf16[512,512]{1,0:T(8,128)(2,1)S(1)}, u32[]{:S(2)}, u32[]{:S(2)}) %collective-permute-start.6) | collective-permute-done | bytes 524320 | tf_op jit(solution)/shard_map/ppermute | solution.py:58
  27.6 5.6 %collective-permute-done.7.refs_3_ = bf16[512,512]{1,0:T(8,128)(2,1)} collective-permute-done((bf16[512,512]{1,0:T(8,128)(2,1)S(1)}, bf16[512,512]{1,0:T(8,128)(2,1)}, u32[]{:S(2)}, u32[]{:S(2)}) %collective-permute-start.7) | collective-permute-done | bytes 524320 | tf_op jit(solution)/shard_map/ppermute | solution.py:58
  36.3 22.8 %shard_map.214 = (bf16[128,512]{1,0:T(8,128)(2,1)S(1)}, bf16[2064,512]{1,0:T(8,128)(2,1)}, bf16[2048,512]{1,0:T(8,128)(2,1)}, f32[8,512]{1,0:T(8,128)S(1)}) custom-call(s32[1]{0:T(128)} %bitcast.core_ref, bf16[272,512]{1,0:T(8,128)(2,1)S(1)} %collective-permute-done.4.moved, f32[8,512]{1,0:T(8,128)S(1)} %broadcast_bitcast_fusion.seen, ...), custom_call_target="tpu_custom_call" | custom-call | flops 12000000000 | bytes 18000000 | tf_op jit(solution)/shard_map/pallas_call | solution.py:261
  59.3 4.3 %collective-permute-done.13.refs_3_ = bf16[2064,512]{1,0:T(8,128)(2,1)S(1)} collective-permute-done((bf16[2064,512]{1,0:T(8,128)(2,1)}, bf16[2064,512]{1,0:T(8,128)(2,1)S(1)}, u32[]{:S(2)}, u32[]{:S(2)}) %collective-permute-start.13) | collective-permute-done | bytes 2113568 | tf_op jit(solution)/shard_map/ppermute | solution.py:58
  64.9 1.6 %copy-done = bf16[2048,512]{1,0:T(8,128)(2,1)S(1)} copy-done((bf16[2048,512]{1,0:T(8,128)(2,1)S(1)}, bf16[2048,512]{1,0:T(8,128)(2,1)}, u32[]{:S(2)}) %copy-start) | copy-done | bytes 2097176
  66.5 2.9 %shard_map.215 = (bf16[528,512]{1,0:T(8,128)(2,1)}, bf16[528,512]{1,0:T(8,128)(2,1)}, bf16[528,512]{1,0:T(8,128)(2,1)S(1)}, f32[512,512]{1,0:T(8,128)S(1)}, f32[8,512]{1,0:T(8,128)S(1)}) custom-call(s32[1]{0:T(128)} %bitcast.9.refs_0_, bf16[2048,512]{1,0:T(8,128)(2,1)S(1)} %copy-done, f32[8,512]{1,0:T(8,128)S(1)} %get-tuple-element.43.refs_2_, ...), custom_call_target="tpu_custom_call" | custom-call | tf_op jit(solution)/shard_map/pallas_call | solution.py:382
  69.4 3.4 %collective-permute-start.15 = (bf16[528,512]{1,0:T(8,128)(2,1)}, bf16[528,512]{1,0:T(8,128)(2,1)S(1)}, u32[]{:S(2)}, u32[]{:S(2)}) collective-permute-start(bf16[528,512]{1,0:T(8,128)(2,1)} %get-tuple-element.46), channel_id=1, source_target_pairs={{0,2},{1,3},{2,0},{3,1},{4,6},{5,7},{6,4},{7,5},{8,10},{9,11},{10,... | collective-permute-start | bytes 1622024 | tf_op jit(solution)/shard_map/ppermute | solution.py:58
  73.3 4.8 %collective-permute-start.12 = (bf16[128,512]{1,0:T(8,128)(2,1)S(1)}, bf16[128,512]{1,0:T(8,128)(2,1)S(1)}, u32[]{:S(2)}, u32[]{:S(2)}) collective-permute-start(bf16[128,512]{1,0:T(8,128)(2,1)S(1)} %get-tuple-element.41), channel_id=1, source_target_pairs={{0,0},{1,1},{2,2},{3,3},{4,32},{5,33},{6,34},{7,35},{8,8},{9,9},{1... | collective-permute-start | bytes 393224 | tf_op jit(solution)/shard_map/ppermute | solution.py:58
  78.1 2.9 %collective-permute-done.12 = bf16[128,512]{1,0:T(8,128)(2,1)S(1)} collective-permute-done((bf16[128,512]{1,0:T(8,128)(2,1)S(1)}, bf16[128,512]{1,0:T(8,128)(2,1)S(1)}, u32[]{:S(2)}, u32[]{:S(2)}) %collective-permute-start.12) | collective-permute-done | bytes 131104 | tf_op jit(solution)/shard_map/ppermute | solution.py:58
  81.1 4.9 %collective-permute-done.15.refs_4_ = bf16[528,512]{1,0:T(8,128)(2,1)S(1)} collective-permute-done((bf16[528,512]{1,0:T(8,128)(2,1)}, bf16[528,512]{1,0:T(8,128)(2,1)S(1)}, u32[]{:S(2)}, u32[]{:S(2)}) %collective-permute-start.15) | collective-permute-done | bytes 540704 | tf_op jit(solution)/shard_map/ppermute | solution.py:58
  85.9 2.4 %collective-permute-done.16.refs_5_ = bf16[528,512]{1,0:T(8,128)(2,1)S(1)} collective-permute-done((bf16[528,512]{1,0:T(8,128)(2,1)S(1)}, bf16[528,512]{1,0:T(8,128)(2,1)S(1)}, u32[]{:S(2)}, u32[]{:S(2)}) %collective-permute-start.16) | collective-permute-done | bytes 540704 | tf_op jit(solution)/shard_map/ppermute | solution.py:58
  88.7 2.0 %collective-permute-start.18 = (bf16[144,512]{1,0:T(8,128)(2,1)S(1)}, bf16[144,512]{1,0:T(8,128)(2,1)S(1)}, u32[]{:S(2)}, u32[]{:S(2)}) collective-permute-start(bf16[144,512]{1,0:T(8,128)(2,1)S(1)} %get-tuple-element.57), channel_id=1, source_target_pairs={{0,16},{1,17},{2,18},{3,19},{4,20},{5,21},{6,22},{7,23},{8,24},{9,... | collective-permute-start | bytes 442376 | tf_op jit(solution)/shard_map/ppermute | solution.py:58
  90.6 1.9 %collective-permute-start.19 = (bf16[144,512]{1,0:T(8,128)(2,1)S(1)}, bf16[144,512]{1,0:T(8,128)(2,1)S(1)}, u32[]{:S(2)}, u32[]{:S(2)}) collective-permute-start(bf16[144,512]{1,0:T(8,128)(2,1)S(1)} %get-tuple-element.58), channel_id=1, source_target_pairs={{0,24},{1,25},{2,26},{3,27},{4,28},{5,29},{6,30},{7,31},{8,16},{9,... | collective-permute-start | bytes 442376 | tf_op jit(solution)/shard_map/ppermute | solution.py:58
  92.7 2.1 %collective-permute-done.18.refs_1_ = bf16[144,512]{1,0:T(8,128)(2,1)S(1)} collective-permute-done((bf16[144,512]{1,0:T(8,128)(2,1)S(1)}, bf16[144,512]{1,0:T(8,128)(2,1)S(1)}, u32[]{:S(2)}, u32[]{:S(2)}) %collective-permute-start.18) | collective-permute-done | bytes 147488 | tf_op jit(solution)/shard_map/ppermute | solution.py:58
  94.8 1.8 %collective-permute-done.19.refs_2_ = bf16[144,512]{1,0:T(8,128)(2,1)S(1)} collective-permute-done((bf16[144,512]{1,0:T(8,128)(2,1)S(1)}, bf16[144,512]{1,0:T(8,128)(2,1)S(1)}, u32[]{:S(2)}, u32[]{:S(2)}) %collective-permute-start.19) | collective-permute-done | bytes 147488 | tf_op jit(solution)/shard_map/ppermute | solution.py:58
  96.7 2.0 %collective-permute-start.20 = (bf16[144,512]{1,0:T(8,128)(2,1)S(1)}, bf16[144,512]{1,0:T(8,128)(2,1)S(1)}, u32[]{:S(2)}, u32[]{:S(2)}) collective-permute-start(bf16[144,512]{1,0:T(8,128)(2,1)S(1)} %shard_map.217.own_ref), channel_id=1, source_target_pairs={{0,4},{1,5},{2,6},{3,7},{4,0},{5,1},{6,2},{7,3},{8,12},{9,13},{10,... | collective-permute-start | bytes 442376 | tf_op jit(solution)/shard_map/ppermute | solution.py:58
  98.7 2.4 %collective-permute-start.21 = (bf16[144,512]{1,0:T(8,128)(2,1)S(1)}, bf16[144,512]{1,0:T(8,128)(2,1)S(1)}, u32[]{:S(2)}, u32[]{:S(2)}) collective-permute-start(bf16[144,512]{1,0:T(8,128)(2,1)S(1)} %shard_map.217.own_ref), channel_id=1, source_target_pairs={{0,64},{1,65},{2,66},{3,67},{4,68},{5,69},{6,70},{7,71},{8,72},{9,... | collective-permute-start | bytes 442376 | tf_op jit(solution)/shard_map/ppermute | solution.py:58
  101.2 4.1 %collective-permute-done.21.refs_1_ = bf16[144,512]{1,0:T(8,128)(2,1)S(1)} collective-permute-done((bf16[144,512]{1,0:T(8,128)(2,1)S(1)}, bf16[144,512]{1,0:T(8,128)(2,1)S(1)}, u32[]{:S(2)}, u32[]{:S(2)}) %collective-permute-start.21) | collective-permute-done | bytes 147488 | tf_op jit(solution)/shard_map/ppermute | solution.py:58
  108.4 2.0 %collective-permute-start.24 = (bf16[128,512]{1,0:T(8,128)(2,1)S(1)}, bf16[128,512]{1,0:T(8,128)(2,1)S(1)}, u32[]{:S(2)}, u32[]{:S(2)}) collective-permute-start(bf16[128,512]{1,0:T(8,128)(2,1)S(1)} %get-tuple-element.59), channel_id=1, source_target_pairs={{0,16},{1,17},{2,18},{3,19},{4,20},{5,21},{6,22},{7,23},{8,24},{9,... | collective-permute-start | bytes 393224 | tf_op jit(solution)/shard_map/ppermute | solution.py:58
  111.0 3.0 %collective-permute-done.24 = bf16[128,512]{1,0:T(8,128)(2,1)S(1)} collective-permute-done((bf16[128,512]{1,0:T(8,128)(2,1)S(1)}, bf16[128,512]{1,0:T(8,128)(2,1)S(1)}, u32[]{:S(2)}, u32[]{:S(2)}) %collective-permute-start.24) | collective-permute-done | bytes 131104 | tf_op jit(solution)/shard_map/ppermute | solution.py:58
  115.6 2.5 %collective-permute-start.27 = (bf16[512,512]{1,0:T(8,128)(2,1)S(1)}, bf16[512,512]{1,0:T(8,128)(2,1)S(1)}, u32[]{:S(2)}, u32[]{:S(2)}) collective-permute-start(bf16[512,512]{1,0:T(8,128)(2,1)S(1)} %get-tuple-element.70.refs_0_), channel_id=1, source_target_pairs={{0,2},{1,3},{2,0},{3,1},{4,6},{5,7},{6,4},{7,5},{8,10},{9,11},{10,... | collective-permute-start | bytes 1572872 | tf_op jit(solution)/shard_map/ppermute | solution.py:58
  119.4 5.5 %collective-permute-start.29 = (bf16[528,512]{1,0:T(8,128)(2,1)S(1)}, bf16[528,512]{1,0:T(8,128)(2,1)S(1)}, u32[]{:S(2)}, u32[]{:S(2)}) collective-permute-start(bf16[528,512]{1,0:T(8,128)(2,1)S(1)} %constant_dynamic-update-slice_fusion.4), channel_id=1, source_target_pairs={{0,32},{1,33},{2,34},{3,35},{4,36},{5,37},{6,38},{7,39},{8,40},{9,... | collective-permute-start | bytes 1622024 | tf_op jit(solution)/shard_map/ppermute | solution.py:58
  125.0 4.5 %collective-permute-start.30 = (bf16[512,512]{1,0:T(8,128)(2,1)S(1)}, bf16[512,512]{1,0:T(8,128)(2,1)S(1)}, u32[]{:S(2)}, u32[]{:S(2)}) collective-permute-start(bf16[512,512]{1,0:T(8,128)(2,1)S(1)} %collective-permute-done.26.refs_1_), channel_id=1, source_target_pairs={{0,32},{1,33},{2,34},{3,35},{4,36},{5,37},{6,38},{7,39},{8,40},{9,... | collective-permute-start | bytes 1572872 | tf_op jit(solution)/shard_map/ppermute | solution.py:58
  130.6 5.4 %collective-permute-start.31 = (bf16[512,512]{1,0:T(8,128)(2,1)S(1)}, bf16[512,512]{1,0:T(8,128)(2,1)S(1)}, u32[]{:S(2)}, u32[]{:S(2)}) collective-permute-start(bf16[512,512]{1,0:T(8,128)(2,1)S(1)} %collective-permute-done.27.refs_2_), channel_id=1, source_target_pairs={{0,32},{1,33},{2,34},{3,35},{4,36},{5,37},{6,38},{7,39},{8,40},{9,... | collective-permute-start | bytes 1572872 | tf_op jit(solution)/shard_map/ppermute | solution.py:58
  136.0 3.1 %collective-permute-start.32 = (bf16[512,512]{1,0:T(8,128)(2,1)S(1)}, bf16[512,512]{1,0:T(8,128)(2,1)S(1)}, u32[]{:S(2)}, u32[]{:S(2)}) collective-permute-start(bf16[512,512]{1,0:T(8,128)(2,1)S(1)} %collective-permute-done.28.refs_3_), channel_id=1, source_target_pairs={{0,32},{1,33},{2,34},{3,35},{4,36},{5,37},{6,38},{7,39},{8,40},{9,... | collective-permute-start | bytes 1572872 | tf_op jit(solution)/shard_map/ppermute | solution.py:58
  140.6 2.9 %shard_map.219 = (bf16[512,512]{1,0:T(8,128)(2,1)}, bf16[512,512]{1,0:T(8,128)(2,1)}, bf16[512,512]{1,0:T(8,128)(2,1)}, bf16[512,512]{1,0:T(8,128)(2,1)}, bf16[5...) custom-call(s32[3]{0:T(128)S(1)} %pad_add_fusion.where_ref, ...), custom_call_target="tpu_custom_call" | custom-call | tf_op jit(solution)/shard_map/pallas_call | solution.py:382
  (76 shorter events, 21.0 us)
Async XLA Ops:
  0.7 14.1 %collective-permute-start = (bf16[128,512]{1,0:T(8,128)(2,1)}, bf16[128,512]{1,0:T(8,128)(2,1)S(1)}, u32[]{:S(2)}, u32[]{:S(2)}) collective-permute-start(bf16[128,512]{1,0:T(8,128)(2,1)} %bitcast.22), channel_id=1, source_target_pairs={{0,0},{1,1},{2,2},{3,3},{4,32},{5,33},{6,34},{7,35},{8,8},{9,9},{1... | collective-permute-start | bytes 393224 | tf_op jit(solution)/shard_map/ppermute | solution.py:58
  5.3 9.4 %collective-permute-start.1 = (bf16[128,512]{1,0:T(8,128)(2,1)}, bf16[128,512]{1,0:T(8,128)(2,1)S(1)}, u32[]{:S(2)}, u32[]{:S(2)}) collective-permute-start(bf16[128,512]{1,0:T(8,128)(2,1)} %bitcast.23), channel_id=1, source_target_pairs={{0,1},{1,0},{2,3},{3,2},{4,40},{5,41},{6,42},{7,43},{8,9},{9,8},{1... | collective-permute-start | bytes 393224 | tf_op jit(solution)/shard_map/ppermute | solution.py:58
  6.4 9.4 %collective-permute-start.2 = (bf16[128,512]{1,0:T(8,128)(2,1)}, bf16[128,512]{1,0:T(8,128)(2,1)S(1)}, u32[]{:S(2)}, u32[]{:S(2)}) collective-permute-start(bf16[128,512]{1,0:T(8,128)(2,1)} %bitcast.24), channel_id=1, source_target_pairs={{0,2},{1,3},{2,0},{3,1},{4,48},{5,49},{6,50},{7,51},{8,10},{9,11},... | collective-permute-start | bytes 393224 | tf_op jit(solution)/shard_map/ppermute | solution.py:58
  11.1 6.7 %collective-permute-start.3 = (bf16[128,512]{1,0:T(8,128)(2,1)}, bf16[128,512]{1,0:T(8,128)(2,1)S(1)}, u32[]{:S(2)}, u32[]{:S(2)}) collective-permute-start(bf16[128,512]{1,0:T(8,128)(2,1)} %bitcast.25), channel_id=1, source_target_pairs={{0,3},{1,2},{2,1},{3,0},{4,56},{5,57},{6,58},{7,59},{8,11},{9,10},... | collective-permute-start | bytes 393224 | tf_op jit(solution)/shard_map/ppermute | solution.py:58
  17.9 9.7 %collective-permute-start.6 = (bf16[512,512]{1,0:T(8,128)(2,1)S(1)}, bf16[512,512]{1,0:T(8,128)(2,1)S(1)}, u32[]{:S(2)}, u32[]{:S(2)}) collective-permute-start(bf16[512,512]{1,0:T(8,128)(2,1)S(1)} %pad_maximum_fusion.refs_0_), channel_id=1, source_target_pairs={{0,16},{1,17},{2,18},{3,19},{4,20},{5,21},{6,22},{7,23},{8,24},{9,... | collective-permute-start | bytes 1572872 | tf_op jit(solution)/shard_map/ppermute | solution.py:58
  20.2 13.0 %collective-permute-start.7 = (bf16[512,512]{1,0:T(8,128)(2,1)S(1)}, bf16[512,512]{1,0:T(8,128)(2,1)}, u32[]{:S(2)}, u32[]{:S(2)}) collective-permute-start(bf16[512,512]{1,0:T(8,128)(2,1)S(1)} %pad_maximum_fusion.refs_0_), channel_id=1, source_target_pairs={{0,24},{1,25},{2,26},{3,27},{4,28},{5,29},{6,30},{7,31},{8,16},{9,... | collective-permute-start | bytes 1572872 | tf_op jit(solution)/shard_map/ppermute | solution.py:58
  21.0 12.2 %collective-permute-start.5 = (bf16[512,512]{1,0:T(8,128)(2,1)S(1)}, bf16[512,512]{1,0:T(8,128)(2,1)}, u32[]{:S(2)}, u32[]{:S(2)}) collective-permute-start(bf16[512,512]{1,0:T(8,128)(2,1)S(1)} %pad_maximum_fusion.refs_0_), channel_id=1, source_target_pairs={{0,8},{1,9},{2,10},{3,11},{4,12},{5,13},{6,14},{7,15},{8,0},{9,1},... | collective-permute-start | bytes 1572872 | tf_op jit(solution)/shard_map/ppermute | solution.py:58
  21.0 12.7 %collective-permute-start.4 = (bf16[272,512]{1,0:T(8,128)(2,1)S(1)}, bf16[272,512]{1,0:T(8,128)(2,1)S(1)}, u32[]{:S(2)}, u32[]{:S(2)}) collective-permute-start(bf16[272,512]{1,0:T(8,128)(2,1)S(1)} %fusion.1), channel_id=1, source_target_pairs={{0,0},{1,1},{2,2},{3,3},{4,32},{5,33},{6,34},{7,35},{8,8},{9,9},{1... | collective-permute-start | bytes 835592 | tf_op jit(solution)/shard_map/ppermute | solution.py:58
  25.1 9.6 %collective-permute-start.8 = (bf16[512,512]{1,0:T(8,128)(2,1)S(1)}, bf16[512,512]{1,0:T(8,128)(2,1)}, u32[]{:S(2)}, u32[]{:S(2)}) collective-permute-start(bf16[512,512]{1,0:T(8,128)(2,1)S(1)} %pad_maximum_fusion.refs_0_), channel_id=1, source_target_pairs={{0,32},{1,33},{2,34},{3,35},{4,36},{5,37},{6,38},{7,39},{8,40},{9,... | collective-permute-start | bytes 1572872 | tf_op jit(solution)/shard_map/ppermute | solution.py:58
  27.6 7.1 %collective-permute-start.10 = (bf16[512,512]{1,0:T(8,128)(2,1)S(1)}, bf16[512,512]{1,0:T(8,128)(2,1)}, u32[]{:S(2)}, u32[]{:S(2)}) collective-permute-start(bf16[512,512]{1,0:T(8,128)(2,1)S(1)} %collective-permute-done.6.refs_2_), channel_id=1, source_target_pairs={{0,32},{1,33},{2,34},{3,35},{4,36},{5,37},{6,38},{7,39},{8,40},{9,... | collective-permute-start | bytes 1572872 | tf_op jit(solution)/shard_map/ppermute | solution.py:58
  33.3 3.0 %collective-permute-start.9 = (bf16[512,512]{1,0:T(8,128)(2,1)}, bf16[512,512]{1,0:T(8,128)(2,1)}, u32[]{:S(2)}, u32[]{:S(2)}) collective-permute-start(bf16[512,512]{1,0:T(8,128)(2,1)} %collective-permute-done.5.refs_1_), channel_id=1, source_target_pairs={{0,32},{1,33},{2,34},{3,35},{4,36},{5,37},{6,38},{7,39},{8,40},{9,... | collective-permute-start | bytes 1572872 | tf_op jit(solution)/shard_map/ppermute | solution.py:58
  59.1 4.5 %collective-permute-start.13 = (bf16[2064,512]{1,0:T(8,128)(2,1)}, bf16[2064,512]{1,0:T(8,128)(2,1)S(1)}, u32[]{:S(2)}, u32[]{:S(2)}) collective-permute-start(bf16[2064,512]{1,0:T(8,128)(2,1)} %get-tuple-element.44), channel_id=1, source_target_pairs={{0,32},{1,33},{2,34},{3,35},{4,36},{5,37},{6,38},{7,39},{8,40},{9,... | collective-permute-start | bytes 6340616 | tf_op jit(solution)/shard_map/ppermute | solution.py:58
  69.4 11.6 %collective-permute-start.14 = (bf16[528,512]{1,0:T(8,128)(2,1)}, bf16[528,512]{1,0:T(8,128)(2,1)S(1)}, u32[]{:S(2)}, u32[]{:S(2)}) collective-permute-start(bf16[528,512]{1,0:T(8,128)(2,1)} %get-tuple-element.45), channel_id=1, source_target_pairs={{0,1},{1,0},{2,3},{3,2},{4,5},{5,4},{6,7},{7,6},{8,9},{9,8},{10,11... | collective-permute-start | bytes 1622024 | tf_op jit(solution)/shard_map/ppermute | solution.py:58
  69.4 16.5 %collective-permute-start.15 = (bf16[528,512]{1,0:T(8,128)(2,1)}, bf16[528,512]{1,0:T(8,128)(2,1)S(1)}, u32[]{:S(2)}, u32[]{:S(2)}) collective-permute-start(bf16[528,512]{1,0:T(8,128)(2,1)} %get-tuple-element.46), channel_id=1, source_target_pairs={{0,2},{1,3},{2,0},{3,1},{4,6},{5,7},{6,4},{7,5},{8,10},{9,11},{10,... | collective-permute-start | bytes 1622024 | tf_op jit(solution)/shard_map/ppermute | solution.py:58
  72.8 15.5 %collective-permute-start.16 = (bf16[528,512]{1,0:T(8,128)(2,1)S(1)}, bf16[528,512]{1,0:T(8,128)(2,1)S(1)}, u32[]{:S(2)}, u32[]{:S(2)}) collective-permute-start(bf16[528,512]{1,0:T(8,128)(2,1)S(1)} %get-tuple-element.47), channel_id=1, source_target_pairs={{0,3},{1,2},{2,1},{3,0},{4,7},{5,6},{6,5},{7,4},{8,11},{9,10},{10,... | collective-permute-start | bytes 1622024 | tf_op jit(solution)/shard_map/ppermute | solution.py:58
  73.3 7.8 %collective-permute-start.12 = (bf16[128,512]{1,0:T(8,128)(2,1)S(1)}, bf16[128,512]{1,0:T(8,128)(2,1)S(1)}, u32[]{:S(2)}, u32[]{:S(2)}) collective-permute-start(bf16[128,512]{1,0:T(8,128)(2,1)S(1)} %get-tuple-element.41), channel_id=1, source_target_pairs={{0,0},{1,1},{2,2},{3,3},{4,32},{5,33},{6,34},{7,35},{8,8},{9,9},{1... | collective-permute-start | bytes 393224 | tf_op jit(solution)/shard_map/ppermute | solution.py:58
  88.6 4.1 %collective-permute-start.17 = (bf16[144,512]{1,0:T(8,128)(2,1)S(1)}, bf16[144,512]{1,0:T(8,128)(2,1)S(1)}, u32[]{:S(2)}, u32[]{:S(2)}) collective-permute-start(bf16[144,512]{1,0:T(8,128)(2,1)S(1)} %get-tuple-element.56), channel_id=1, source_target_pairs={{0,8},{1,9},{2,10},{3,11},{4,12},{5,13},{6,14},{7,15},{8,0},{9,1},... | collective-permute-start | bytes 442376 | tf_op jit(solution)/shard_map/ppermute | solution.py:58
  88.7 6.1 %collective-permute-start.18 = (bf16[144,512]{1,0:T(8,128)(2,1)S(1)}, bf16[144,512]{1,0:T(8,128)(2,1)S(1)}, u32[]{:S(2)}, u32[]{:S(2)}) collective-permute-start(bf16[144,512]{1,0:T(8,128)(2,1)S(1)} %get-tuple-element.57), channel_id=1, source_target_pairs={{0,16},{1,17},{2,18},{3,19},{4,20},{5,21},{6,22},{7,23},{8,24},{9,... | collective-permute-start | bytes 442376 | tf_op jit(solution)/shard_map/ppermute | solution.py:58
  90.6 6.0 %collective-permute-start.19 = (bf16[144,512]{1,0:T(8,128)(2,1)S(1)}, bf16[144,512]{1,0:T(8,128)(2,1)S(1)}, u32[]{:S(2)}, u32[]{:S(2)}) collective-permute-start(bf16[144,512]{1,0:T(8,128)(2,1)S(1)} %get-tuple-element.58), channel_id=1, source_target_pairs={{0,24},{1,25},{2,26},{3,27},{4,28},{5,29},{6,30},{7,31},{8,16},{9,... | collective-permute-start | bytes 442376 | tf_op jit(solution)/shard_map/ppermute | solution.py:58
  96.7 4.5 %collective-permute-start.20 = (bf16[144,512]{1,0:T(8,128)(2,1)S(1)}, bf16[144,512]{1,0:T(8,128)(2,1)S(1)}, u32[]{:S(2)}, u32[]{:S(2)}) collective-permute-start(bf16[144,512]{1,0:T(8,128)(2,1)S(1)} %shard_map.217.own_ref), channel_id=1, source_target_pairs={{0,4},{1,5},{2,6},{3,7},{4,0},{5,1},{6,2},{7,3},{8,12},{9,13},{10,... | collective-permute-start | bytes 442376 | tf_op jit(solution)/shard_map/ppermute | solution.py:58
  98.7 6.6 %collective-permute-start.21 = (bf16[144,512]{1,0:T(8,128)(2,1)S(1)}, bf16[144,512]{1,0:T(8,128)(2,1)S(1)}, u32[]{:S(2)}, u32[]{:S(2)}) collective-permute-start(bf16[144,512]{1,0:T(8,128)(2,1)S(1)} %shard_map.217.own_ref), channel_id=1, source_target_pairs={{0,64},{1,65},{2,66},{3,67},{4,68},{5,69},{6,70},{7,71},{8,72},{9,... | collective-permute-start | bytes 442376 | tf_op jit(solution)/shard_map/ppermute | solution.py:58
  101.1 5.7 %collective-permute-start.22 = (bf16[144,512]{1,0:T(8,128)(2,1)S(1)}, bf16[144,512]{1,0:T(8,128)(2,1)S(1)}, u32[]{:S(2)}, u32[]{:S(2)}) collective-permute-start(bf16[144,512]{1,0:T(8,128)(2,1)S(1)} %shard_map.217.own_ref), channel_id=1, source_target_pairs={{0,68},{1,69},{2,70},{3,71},{4,64},{5,65},{6,66},{7,67},{8,76},{9,... | collective-permute-start | bytes 442376 | tf_op jit(solution)/shard_map/ppermute | solution.py:58
  106.9 4.1 %collective-permute-start.23 = (bf16[128,512]{1,0:T(8,128)(2,1)S(1)}, bf16[128,512]{1,0:T(8,128)(2,1)S(1)}, u32[]{:S(2)}, u32[]{:S(2)}) collective-permute-start(bf16[128,512]{1,0:T(8,128)(2,1)S(1)} %get-tuple-element.59), channel_id=1, source_target_pairs={{0,8},{1,9},{2,10},{3,11},{4,12},{5,13},{6,14},{7,15},{8,0},{9,1},... | collective-permute-start | bytes 393224 | tf_op jit(solution)/shard_map/ppermute | solution.py:58
  108.4 5.6 %collective-permute-start.24 = (bf16[128,512]{1,0:T(8,128)(2,1)S(1)}, bf16[128,512]{1,0:T(8,128)(2,1)S(1)}, u32[]{:S(2)}, u32[]{:S(2)}) collective-permute-start(bf16[128,512]{1,0:T(8,128)(2,1)S(1)} %get-tuple-element.59), channel_id=1, source_target_pairs={{0,16},{1,17},{2,18},{3,19},{4,20},{5,21},{6,22},{7,23},{8,24},{9,... | collective-permute-start | bytes 393224 | tf_op jit(solution)/shard_map/ppermute | solution.py:58
  110.4 5.1 %collective-permute-start.25 = (bf16[128,512]{1,0:T(8,128)(2,1)S(1)}, bf16[128,512]{1,0:T(8,128)(2,1)S(1)}, u32[]{:S(2)}, u32[]{:S(2)}) collective-permute-start(bf16[128,512]{1,0:T(8,128)(2,1)S(1)} %get-tuple-element.59), channel_id=1, source_target_pairs={{0,24},{1,25},{2,26},{3,27},{4,28},{5,29},{6,30},{7,31},{8,16},{9,... | collective-permute-start | bytes 393224 | tf_op jit(solution)/shard_map/ppermute | solution.py:58
  115.5 9.5 %collective-permute-start.26 = (bf16[512,512]{1,0:T(8,128)(2,1)S(1)}, bf16[512,512]{1,0:T(8,128)(2,1)S(1)}, u32[]{:S(2)}, u32[]{:S(2)}) collective-permute-start(bf16[512,512]{1,0:T(8,128)(2,1)S(1)} %get-tuple-element.70.refs_0_), channel_id=1, source_target_pairs={{0,1},{1,0},{2,3},{3,2},{4,5},{5,4},{6,7},{7,6},{8,9},{9,8},{10,11... | collective-permute-start | bytes 1572872 | tf_op jit(solution)/shard_map/ppermute | solution.py:58
  115.6 15.0 %collective-permute-start.27 = (bf16[512,512]{1,0:T(8,128)(2,1)S(1)}, bf16[512,512]{1,0:T(8,128)(2,1)S(1)}, u32[]{:S(2)}, u32[]{:S(2)}) collective-permute-start(bf16[512,512]{1,0:T(8,128)(2,1)S(1)} %get-tuple-element.70.refs_0_), channel_id=1, source_target_pairs={{0,2},{1,3},{2,0},{3,1},{4,6},{5,7},{6,4},{7,5},{8,10},{9,11},{10,... | collective-permute-start | bytes 1572872 | tf_op jit(solution)/shard_map/ppermute | solution.py:58
  118.0 17.9 %collective-permute-start.28 = (bf16[512,512]{1,0:T(8,128)(2,1)S(1)}, bf16[512,512]{1,0:T(8,128)(2,1)S(1)}, u32[]{:S(2)}, u32[]{:S(2)}) collective-permute-start(bf16[512,512]{1,0:T(8,128)(2,1)S(1)} %get-tuple-element.70.refs_0_), channel_id=1, source_target_pairs={{0,3},{1,2},{2,1},{3,0},{4,7},{5,6},{6,5},{7,4},{8,11},{9,10},{10,... | collective-permute-start | bytes 1572872 | tf_op jit(solution)/shard_map/ppermute | solution.py:58
  119.4 19.7 %collective-permute-start.29 = (bf16[528,512]{1,0:T(8,128)(2,1)S(1)}, bf16[528,512]{1,0:T(8,128)(2,1)S(1)}, u32[]{:S(2)}, u32[]{:S(2)}) collective-permute-start(bf16[528,512]{1,0:T(8,128)(2,1)S(1)} %constant_dynamic-update-slice_fusion.4), channel_id=1, source_target_pairs={{0,32},{1,33},{2,34},{3,35},{4,36},{5,37},{6,38},{7,39},{8,40},{9,... | collective-permute-start | bytes 1622024 | tf_op jit(solution)/shard_map/ppermute | solution.py:58
  125.0 14.2 %collective-permute-start.30 = (bf16[512,512]{1,0:T(8,128)(2,1)S(1)}, bf16[512,512]{1,0:T(8,128)(2,1)S(1)}, u32[]{:S(2)}, u32[]{:S(2)}) collective-permute-start(bf16[512,512]{1,0:T(8,128)(2,1)S(1)} %collective-permute-done.26.refs_1_), channel_id=1, source_target_pairs={{0,32},{1,33},{2,34},{3,35},{4,36},{5,37},{6,38},{7,39},{8,40},{9,... | collective-permute-start | bytes 1572872 | tf_op jit(solution)/shard_map/ppermute | solution.py:58
  130.6 8.6 %collective-permute-start.31 = (bf16[512,512]{1,0:T(8,128)(2,1)S(1)}, bf16[512,512]{1,0:T(8,128)(2,1)S(1)}, u32[]{:S(2)}, u32[]{:S(2)}) collective-permute-start(bf16[512,512]{1,0:T(8,128)(2,1)S(1)} %collective-permute-done.27.refs_2_), channel_id=1, source_target_pairs={{0,32},{1,33},{2,34},{3,35},{4,36},{5,37},{6,38},{7,39},{8,40},{9,... | collective-permute-start | bytes 1572872 | tf_op jit(solution)/shard_map/ppermute | solution.py:58
  136.0 4.7 %collective-permute-start.32 = (bf16[512,512]{1,0:T(8,128)(2,1)S(1)}, bf16[512,512]{1,0:T(8,128)(2,1)S(1)}, u32[]{:S(2)}, u32[]{:S(2)}) collective-permute-start(bf16[512,512]{1,0:T(8,128)(2,1)S(1)} %collective-permute-done.28.refs_3_), channel_id=1, source_target_pairs={{0,32},{1,33},{2,34},{3,35},{4,36},{5,37},{6,38},{7,39},{8,40},{9,... | collective-permute-start | bytes 1572872 | tf_op jit(solution)/shard_map/ppermute | solution.py:58
  (10 other events, 210.2 us)

commit v5 on v4

--- a/solution.py
+++ b/solution.py
@@ -19,6 +19,9 @@
 GEOM = ("z", "x_lo", "y")
 VMEM = pl.BlockSpec(memory_space=pltpu.VMEM)
 SMEM = pl.BlockSpec(memory_space=pltpu.SMEM)
+ANY = pl.BlockSpec(memory_space=pl.ANY)
+FAR = 2
+ORDER = (2, 1, 3)
 
 
 def pairs_of(move):
@@ -98,6 +101,12 @@
 
 
 PARTS = 8
+PIECES = 32
+CHUNK = 128
+TAIL = 16
+LAYOUT = ((0, 16), (16, 16), (32, 16), (48, 16), (64, 16), (80, 16), (96, 32))
+
+
 def lanes(value, combine):
     out = value[:, 0:BLK]
     for at in range(BLK, value.shape[1], BLK):
@@ -105,9 +114,10 @@
     return out
 
 
-def step_kernel(core_ref, moved, seen, w_query, w_key, w_value, w_out, w_up, w_down, gain_attn, gain_mlp, *refs):
-    parts, (output, give, keep, gains_out) = refs[:PARTS], refs[PARTS : PARTS + 4]
-    feats, scores, pulls, sums, stat, sems = refs[PARTS + 4 :]
+def step_kernel(where, moved, seen, w_query, w_key, w_value, w_out, w_up, w_down, gain_attn, gain_mlp, *refs):
+    parts, (output, gains_out), refs = refs[:PARTS], refs[PARTS : PARTS + 2], refs[PARTS + 2 :]
+    gives, keeps, refs = refs[:4], refs[4:8], refs[8:]
+    feats, scores, pulls, sums, stat, give, keep, tail, sems, out_sems = refs
     f32, b16 = jnp.float32, jnp.bfloat16
     copies = [pltpu.make_async_copy(parts[p], feats.at[p], sems.at[p]) for p in range(PARTS)]
     for copy in copies:
@@ -170,7 +180,7 @@
         axis=1,
     ).astype(b16)
 
-    core = core_ref[0]
+    core = where[0]
     half = PIECES // 2
 
     def store(at, rows, grad):
@@ -179,8 +189,9 @@
         mine = jnp.where(core == 0, low, high).astype(b16)
         yours = jnp.where(core == 0, high, low).astype(b16)
         for i in range(half):
-            keep[i * CHUNK + at : i * CHUNK + at + rows, :] = mine[i * rows : (i + 1) * rows]
-            give[i * CHUNK + at : i * CHUNK + at + rows, :] = yours[i * rows : (i + 1) * rows]
+            row = i % 4 * CHUNK + at
+            keep[i // 4, row : row + rows, :] = mine[i * rows : (i + 1) * rows]
+            give[i // 4, row : row + rows, :] = yours[i * rows : (i + 1) * rows]
 
     mixed = inputs + mult(context, w_out[...])
     scaled_two, inverse_two, normed_two = normalize(mixed, gain_mlp[...])
@@ -252,54 +263,57 @@
     grad_normed = mult_nt(grad_query_rows, w_query[...])
     grad_gain_attn = jnp.sum(grad_normed * scaled_one, axis=0, keepdims=True)
     gains = jnp.concatenate([grad_gain_attn, grad_gain_mlp, jnp.zeros((6, width), f32)], axis=0)
-    put_gains(give, half * CHUNK, gains)
+    put_gains(tail, 0, gains)
     gains_out[...] = gains
-
-
-def device_step(core_at, moved, seen, parts, weights):
+    one, two = where[1], where[2]
+    copies = [
+        pltpu.make_async_copy(tail, gives[FAR].at[pl.ds(4 * CHUNK, TAIL)], out_sems.at[8])
+    ]
+    for i, mask in enumerate(ORDER + (0,)):
+        for j, (held, outs, index) in enumerate(((give, gives, two), (keep, keeps, one))):
+            copies.append(
+                pltpu.make_async_copy(
+                    held.at[index ^ mask],
+                    outs[mask].at[pl.ds(0, 4 * CHUNK)],
+                    out_sems.at[2 * i + j],
+                )
+            )
+    for copy in copies:
+        copy.start()
+    for copy in copies:
+        copy.wait()
+
+
+def device_step(where, moved, seen, parts, weights):
     f32, b16 = jnp.float32, jnp.bfloat16
+    quarters = [(4 * CHUNK + (TAIL if mask == FAR else 0), 512) for mask in range(4)]
     return pl.pallas_call(
         step_kernel,
         out_shape=[
             jax.ShapeDtypeStruct((BLK, 512), b16),
-            jax.ShapeDtypeStruct((2048 + TAIL, 512), b16),
-            jax.ShapeDtypeStruct((2048, 512), b16),
             jax.ShapeDtypeStruct((8, 512), f32),
-        ],
-        in_specs=[SMEM] + [VMEM] * 10 + [pl.BlockSpec(memory_space=pl.ANY)] * PARTS,
-        out_specs=[VMEM] * 4,
+        ]
+        + [jax.ShapeDtypeStruct(shape, b16) for shape in quarters]
+        + [jax.ShapeDtypeStruct((4 * CHUNK, 512), b16)] * 4,
+        in_specs=[SMEM] + [VMEM] * 10 + [ANY] * PARTS,
+        out_specs=[VMEM] * 2 + [ANY] * 8,
         scratch_shapes=[
             pltpu.VMEM((PARTS, 512, 512), b16),
             pltpu.VMEM((PARTS, 512, 512), f32),
             pltpu.VMEM((PARTS, 512, 512), f32),
             pltpu.VMEM((512, 512), f32),
             pltpu.VMEM((512, BLK), f32),
+            pltpu.VMEM((4, 4 * CHUNK, 512), b16),
+            pltpu.VMEM((4, 4 * CHUNK, 512), b16),
+            pltpu.VMEM((TAIL, 512), b16),
             pltpu.SemaphoreType.DMA((PARTS,)),
+            pltpu.SemaphoreType.DMA((9,)),
         ],
         compiler_params=pltpu.CompilerParams(vmem_limit_bytes=52 << 20),
         cost_estimate=pl.CostEstimate(
             flops=12 * 10**9, bytes_accessed=18 * 10**6, transcendentals=3 * 10**6
         ),
-    )(core_at, moved, seen, *weights, *parts)
-
-
-PIECES = 32
-CHUNK = 128
-TAIL = 16
-
-
-def pieces_of(refs, k):
-    query, key, value, out, up, down = refs
-    rows = pl.ds(pl.multiple_of(k * 16, 16), 16)
-    return (
-        (0, query.at[rows, :]),
-        (16, key.at[rows, :]),
-        (32, value.at[rows, :]),
-        (48, out.at[rows, :]),
-        (64, up.at[rows, pl.ds(0, 512)]),
-        (80, up.at[rows, pl.ds(512, 512)]),
-        (96, down.at[pl.ds(pl.multiple_of(k * 32, 32), 32), :]),
-    )
+    )(where, moved, seen, *weights, *parts)
 
 
 def put_gains(ref, at, gains):
@@ -313,23 +327,36 @@
     return tail[: TAIL // 2] + tail[TAIL // 2 :]
 
 
-def quarters_kernel(many, index_ref, own_ref, gains_ref, *refs):
-    arrived, gives, keep, gains_out = refs[:many], refs[many : many + 3], refs[many + 3], refs[many + 4]
-    index = index_ref[0]
+def lift_far_kernel(keep, arrived, gains_ref, give, gains_out):
     rows = keep.shape[0]
-    total = own_ref.shape[0]
+    total = keep[...].astype(jnp.float32) + arrived[0:rows, :].astype(jnp.float32)
+    give[0:rows, :] = total.astype(jnp.bfloat16)
+    gains = add_gains(gains_ref[...], [take_gains(arrived, rows)])
+    put_gains(give, rows, gains)
+    gains_out[...] = gains
+
+
+def lift_kernel(keep, arrived, gains_ref, give):
+    rows = keep.shape[0]
+    total = keep[...].astype(jnp.float32) + arrived[...].astype(jnp.float32)
+    give[0:rows, :] = total.astype(jnp.bfloat16)
+    put_gains(give, rows, gains_ref[...])
+
+
+def quarters_kernel(where, keep, across, gains_ref, *refs):
+    arrived, gives, own, gains_out = refs[:3], refs[3:6], refs[6], refs[7]
     for mask in range(4):
-        at = pl.ds(pl.multiple_of((index ^ mask) * rows, rows), rows)
-        value = own_ref[at, :].astype(jnp.float32)
+        at = pl.ds(pl.multiple_of((where[2] ^ mask) * CHUNK, CHUNK), CHUNK)
+        value = keep[at, :].astype(jnp.float32) + across[at, :].astype(jnp.float32)
         for ref in arrived:
             value = value + ref[at, :].astype(jnp.float32)
         if mask:
-            gives[mask - 1][0:rows, :] = value.astype(jnp.bfloat16)
+            gives[mask - 1][0:CHUNK, :] = value.astype(jnp.bfloat16)
         else:
-            keep[...] = value
-    gains = add_gains(gains_ref[...], [take_gains(ref, total) for ref in arrived])
+            own[...] = value
+    gains = add_gains(gains_ref[...], [take_gains(ref, 4 * CHUNK) for ref in arrived])
     for give in gives:
-        put_gains(give, rows, gains)
+        put_gains(give, CHUNK, gains)
     gains_out[...] = gains
 
 
@@ -360,20 +387,50 @@
     put_gains(gains, 0, (a + b) + (c + d))
 
 
-def place_kernel(where_ref, *refs):
-    own, other, gains_own = refs[0:4], refs[4:8], refs[8]
-    grads, gain_attn, gain_mlp = refs[9:15], refs[15], refs[16]
-    core, y, z = where_ref[0], where_ref[1], where_ref[2]
-    for side, group in enumerate((own, other)):
-        holder = core ^ side
-        one = jnp.where(holder == 0, y, z)
-        two = jnp.where(holder == 0, z, y)
-        for m1 in range(4):
-            for m2 in range(4):
-                k = holder * 16 + (one ^ m1) * 4 + (two ^ m2)
-                for at, piece in pieces_of(grads, k):
-                    piece[...] = group[m1][m2 * CHUNK + at : m2 * CHUNK + at + piece.shape[0], :]
-    gains = jnp.where(core == 0, take_gains(gains_own, 0), take_gains(other[0], 4 * CHUNK))
+def arrange_kernel(where, gains, *refs):
+    chunks, out = refs[:4], refs[4]
+    for mask, chunk in enumerate(chunks):
+        for at, rows in LAYOUT:
+            to = pl.multiple_of(at * 4 + (where[2] ^ mask) * rows, 16)
+            out[pl.ds(to, rows), :] = chunk[at : at + rows, :]
+    out[4 * CHUNK :, :] = gains[...]
+
+
+def place_kernel(which, where, *refs):
+    count = len(which)
+    arranged, grads, sems = refs[:count], refs[-7:-1], refs[-1]
+    copies = []
+    for i, (side, mask) in enumerate(which):
+        holder = where[0] ^ side
+        part = holder * 4 + (where[1 + side] ^ mask)
+        for j, (at, rows) in enumerate(LAYOUT):
+            to = pl.ds(pl.multiple_of(part * (4 * rows), 64), 4 * rows)
+            grad = grads[min(j, 4 if j < 6 else 5)]
+            target = grad.at[to, pl.ds(512 * (j - 4), 512)] if j in (4, 5) else grad.at[to, :]
+            copies.append(
+                pltpu.make_async_copy(arranged[i].at[pl.ds(at * 4, 4 * rows)], target, sems.at[i, j])
+            )
+    for copy in copies:
+        copy.start()
+    for copy in copies:
+        copy.wait()
+
+
+def place(which, where, arranged, grads):
+    shapes = [(512, 512)] * 4 + [(512, 1024), (1024, 512)]
+    count = len(which)
+    return pl.pallas_call(
+        lambda *refs: place_kernel(which, *refs),
+        out_shape=[jax.ShapeDtypeStruct(shape, jnp.bfloat16) for shape in shapes],
+        in_specs=[SMEM] + [ANY] * (count + len(grads)),
+        out_specs=[ANY] * 6,
+        scratch_shapes=[pltpu.SemaphoreType.DMA((count, len(LAYOUT)))],
+        input_output_aliases={1 + count + i: i for i in range(len(grads))},
+    )(where, *arranged, *grads)
+
+
+def gains_kernel(where, own, other, gain_attn, gain_mlp):
+    gains = jnp.where(where[0] == 0, take_gains(own, 4 * CHUNK), take_gains(other, 4 * CHUNK))
     gain_attn[...] = gains[0].astype(jnp.bfloat16)
     gain_mlp[...] = gains[1].astype(jnp.bfloat16)
 
@@ -384,46 +441,60 @@
         out_shape=[jax.ShapeDtypeStruct(shape, dtype) for shape, dtype in outs],
         in_specs=[SMEM] * scalars + [VMEM] * (len(operands) - scalars),
         out_specs=[VMEM] * len(outs),
-        compiler_params=pltpu.CompilerParams(vmem_limit_bytes=48 << 20),
+        compiler_params=pltpu.CompilerParams(vmem_limit_bytes=24 << 20),
     )(*operands)
 
 
-def sum_everywhere(output, give, keep, gains):
-    core, y, z = (lax.axis_index(name) for name in ("core", "y", "z"))
-    one_at = jnp.where(core == 0, y, z).astype(jnp.int32).reshape(1)
-    two_at = jnp.where(core == 0, z, y).astype(jnp.int32).reshape(1)
+def to_peers(give_of, route):
+    return dict(sorted((mask, send(give_of(mask), route(mask))) for mask in ORDER))
+
+
+def sum_everywhere(where, output, gains, *quarters):
+    gives, keeps = quarters[:4], quarters[4:]
     b16, f32 = jnp.bfloat16, jnp.float32
-
-    arrived = [send(give, CORE)]
-    for rows, index, route, count in ((512, one_at, first, 1), (128, two_at, second, 3)):
-        *gives, keep, gains = call(
-            lambda *refs, count=count: quarters_kernel(count, *refs),
-            [((rows + TAIL, 512), b16)] * 3 + [((rows, 512), f32), ((8, 512), f32)],
-            index, keep, gains, *arrived, scalars=1,
-        )
-        arrived = [send(give, route(mask)) for mask, give in enumerate(gives, 1)]
-        if count == 1:
-            output, *arrived = lax.optimization_barrier((send(output, SWAP), *arrived))
-    (give,) = call(chunk_kernel, [((128 + TAIL, 512), b16)], keep, gains, *arrived)
-    arrived = [send(give, along_x(mask)) for mask in (1, 2, 3)]
-    chunk, gains = call(last_kernel, [((128, 512), b16), ((TAIL, 512), b16)], give, *arrived)
-
-    mine = jnp.concatenate([chunk] + [send(chunk, second(mask)) for mask in (1, 2, 3)])
-    own = [mine] + [send(mine, first(mask)) for mask in (1, 2, 3)]
-    other = [send(jnp.concatenate([mine, gains]), CORE)] + [send(part, CORE) for part in own[1:]]
-    where = jnp.stack([core, y, z]).astype(jnp.int32)
-    placed = call(
-        place_kernel,
-        [((512, 512), b16)] * 4 + [((512, 1024), b16), ((1024, 512), b16)] + [((512,), b16)] * 2,
-        where, *own, *other, gains, scalars=1,
-    )
-    return (output[None], *placed)
+    message = ((4 * CHUNK + TAIL, 512), b16)
+
+    across = {mask: send(gives[mask], CORE) for mask in ORDER + (0,)}
+    far, gains = call(lift_far_kernel, [message, ((8, 512), f32)], keeps[FAR], across[FAR], gains)
+
+    def lifted(mask):
+        if mask == FAR:
+            return far
+        return call(lift_kernel, [message], keeps[mask], across[mask], gains)[0]
+
+    arrived = to_peers(lifted, first).values()
+    output, *arrived = lax.optimization_barrier((send(output, SWAP), *arrived))
+    small = ((CHUNK + TAIL, 512), b16)
+    *gives, own, gains = call(
+        quarters_kernel,
+        [small] * 3 + [((CHUNK, 512), f32), ((8, 512), f32)],
+        where, keeps[0], across[0], gains, *arrived, scalars=1,
+    )
+    arrived = to_peers(lambda mask: gives[mask - 1], second).values()
+    (give,) = call(chunk_kernel, [small], own, gains, *arrived)
+    arrived = to_peers(lambda mask: give, along_x).values()
+    chunk, gains = call(last_kernel, [((CHUNK, 512), b16), ((TAIL, 512), b16)], give, *arrived)
+
+    chunks = [chunk, *to_peers(lambda mask: chunk, second).values()]
+    (mine,) = call(arrange_kernel, [message], where, gains, *chunks, scalars=1)
+    own = {0: mine, **to_peers(lambda mask: mine, first)}
+    other = {mask: send(own[mask], CORE) for mask in (0,) + ORDER}
+    early = [(side, mask) for mask in (0,) + ORDER[:2] for side in range(2)]
+    held = [(own, other)[side][mask] for side, mask in early]
+    *held, last = lax.optimization_barrier((*held, own[ORDER[2]]))
+    grads = place(early, where, held, ())
+    grads = place([(0, ORDER[2]), (1, ORDER[2])], where, [last, other[ORDER[2]]], grads)
+    gains = call(
+        gains_kernel, [((512,), b16)] * 2, where, held[0], held[1], scalars=1
+    )
+    return (output[None], *grads, *gains)
 
 
 def gather_features(own, others):
-    mine = jnp.concatenate([send(own, first_swapped(mask)) for mask in range(4)])
+    near = {mask: send(own, first_swapped(mask)) for mask in (0,) + ORDER}
+    mine = jnp.concatenate([near[mask] for mask in range(4)])
     mine, others = lax.optimization_barrier((mine, others))
-    group = [mine] + [send(mine, second(mask)) for mask in (1, 2, 3)]
+    group = [mine, *to_peers(lambda mask: mine, second).values()]
     parts = group + [send(part, CORE) for part in group]
     core, y, z = (lax.axis_index(name) for name in ("core", "y", "z"))
     side, two, one = (jnp.asarray(i) for i in np.unravel_index(np.arange(32), (2, 4, 4)))
@@ -452,10 +523,12 @@
         features[0], jnp.concatenate([queries[0], cotangent[0], seen])
     )
     seen = jnp.take(moved[2 * BLK].astype(jnp.float32), blocks)
-    core_at = lax.axis_index("core").astype(jnp.int32).reshape(1)
+    core, y, z = (lax.axis_index(name).astype(jnp.int32) for name in ("core", "y", "z"))
+    where = jnp.stack([core, jnp.where(core == 0, y, z), jnp.where(core == 0, z, y)])
     return sum_everywhere(
+        where,
         *device_step(
-            core_at,
+            where,
             moved,
             jnp.repeat(seen, BLK).reshape(PARTS, 512),
             parts,

time: 144 us -> 262 us (1.82)
  Pallas kernels: 29 us -> 157 us
  waiting for transfers between devices: 43.9 us -> 35.9 us
    pallas_call x0 -> x2, Pallas kernels: none -> 131 us  [place(): pl.pallas_call(lambda *refs: place_kernel(which, *refs), out_shape=[jax.S...]
    ppermute x33 -> x36, waiting for transfers between devices: 43.9 us -> 35.9 us  [send(): return lax.ppermute(value, AXES, pairs)]
    pallas_call x5 -> x8, Pallas kernels: 6.17 us -> 3.18 us  [call(): pl.pallas_call(kernel, out_shape=[jax.ShapeDtypeStruct(shape, dtype) for...]
    ppermute x33 -> x36, starting transfers between devices: 63.3 us -> 63.2 us  [send(): return lax.ppermute(value, AXES, pairs)]
  transfers between devices with their start and end apart: 33 -> 36, of which waited for: 19 -> 19; matrix products, arithmetic and copies ran while one was open for 2% -> 1% of each run, Pallas kernels for 0% -> 38%
where the time goes in v5:
time: 262 us
  Pallas kernels  157 us (60%)
  starting transfers between devices  63.2 us (24%)
  waiting for transfers between devices  35.9 us (14%)
  local copies, waits for them, and re-layouts  3.25 us (1%)
    pallas_call x2, Pallas kernels, place(): pl.pallas_call(lambda *refs: place_kernel(which, *refs), out_shape=[jax.S...  131 us
    ppermute x36, starting transfers between devices, send(): return lax.ppermute(value, AXES, pairs)  63.2 us
    ppermute x36, waiting for transfers between devices, send(): return lax.ppermute(value, AXES, pairs)  35.9 us
    pallas_call x1, Pallas kernels, device_step(): pl.pallas_call(step_kernel, out_shape=[jax.ShapeDtypeStruct((BLK, 512), b...  22.9 us
  transfers between devices with their start and end apart: 36, of which 19 were waited for; matrix products, arithmetic and copies ran while one was open for 1% of the time, Pallas kernels for 38%

profile of v5, /device:TPU:1, one launch (start us, length us, event | category | flops | bytes accessed | tf_op | source)
XLA Modules:
  0.0 261.6 jit_solution(13427118301817926519)
XLA Ops:
  0.7 5.1 %collective-permute-start.3 = (bf16[128,512]{1,0:T(8,128)(2,1)}, bf16[128,512]{1,0:T(8,128)(2,1)S(1)}, u32[]{:S(2)}, u32[]{:S(2)}) collective-permute-start(bf16[128,512]{1,0:T(8,128)(2,1)} %bitcast.20), channel_id=1, source_target_pairs={{0,3},{1,2},{2,1},{3,0},{4,56},{5,57},{6,58},{7,59},{8,11},{9,10},... | collective-permute-start | bytes 393224 | tf_op jit(solution)/shard_map/ppermute | solution.py:61
  5.8 3.6 %collective-permute-start.2 = (bf16[128,512]{1,0:T(8,128)(2,1)}, bf16[128,512]{1,0:T(8,128)(2,1)S(1)}, u32[]{:S(2)}, u32[]{:S(2)}) collective-permute-start(bf16[128,512]{1,0:T(8,128)(2,1)} %bitcast.21), channel_id=1, source_target_pairs={{0,2},{1,3},{2,0},{3,1},{4,48},{5,49},{6,50},{7,51},{8,10},{9,11},... | collective-permute-start | bytes 393224 | tf_op jit(solution)/shard_map/ppermute | solution.py:61
  10.4 2.3 collective-permute-start
  13.8 1.8 collective-permute-done.1
  15.5 1.3 collective-permute-done
  17.8 2.9 %collective-permute-start.6 = (bf16[512,512]{1,0:T(8,128)(2,1)S(1)}, bf16[512,512]{1,0:T(8,128)(2,1)S(1)}, u32[]{:S(2)}, u32[]{:S(2)}) collective-permute-start(bf16[512,512]{1,0:T(8,128)(2,1)S(1)} %pad_maximum_fusion.refs_0_), channel_id=1, source_target_pairs={{0,16},{1,17},{2,18},{3,19},{4,20},{5,21},{6,22},{7,23},{8,24},{9,... | collective-permute-start | bytes 1572872 | tf_op jit(solution)/shard_map/ppermute | solution.py:61
  20.7 2.9 %collective-permute-start.4 = (bf16[272,512]{1,0:T(8,128)(2,1)S(1)}, bf16[272,512]{1,0:T(8,128)(2,1)S(1)}, u32[]{:S(2)}, u32[]{:S(2)}) collective-permute-start(bf16[272,512]{1,0:T(8,128)(2,1)S(1)} %fusion.1), channel_id=1, source_target_pairs={{0,0},{1,1},{2,2},{3,3},{4,32},{5,33},{6,34},{7,35},{8,8},{9,9},{1... | collective-permute-start | bytes 835592 | tf_op jit(solution)/shard_map/ppermute | solution.py:61
  23.8 8.1 %collective-permute-done.7.refs_3_ = bf16[512,512]{1,0:T(8,128)(2,1)S(1)} collective-permute-done((bf16[512,512]{1,0:T(8,128)(2,1)S(1)}, bf16[512,512]{1,0:T(8,128)(2,1)S(1)}, u32[]{:S(2)}, u32[]{:S(2)}) %collective-permute-start.7) | collective-permute-done | bytes 524320 | tf_op jit(solution)/shard_map/ppermute | solution.py:61
  35.5 22.9 %shard_map.214 = (bf16[128,512]{1,0:T(8,128)(2,1)S(1)}, f32[8,512]{1,0:T(8,128)S(1)}, bf16[512,512]{1,0:T(8,128)(2,1)S(1)}, bf16[512,512]{1,0:T(8,128)(2,1)S(1)}...) custom-call(s32[3]{0:T(128)S(1)} %pad_add_fusion.where.refs_0_, ...), custom_call_target="tpu_custom_call" | custom-call | flops 12000000000 | bytes 18000000 | tf_op jit(solution)/shard_map/pallas_call | solution.py:290
  59.1 1.5 collective-permute-done.14.arrived
  64.1 2.5 collective-permute-start.18
  67.3 3.5 %collective-permute-start.12 = (bf16[128,512]{1,0:T(8,128)(2,1)S(1)}, bf16[128,512]{1,0:T(8,128)(2,1)S(1)}, u32[]{:S(2)}, u32[]{:S(2)}) collective-permute-start(bf16[128,512]{1,0:T(8,128)(2,1)S(1)} %get-tuple-element.57), channel_id=1, source_target_pairs={{0,0},{1,1},{2,2},{3,3},{4,32},{5,33},{6,34},{7,35},{8,8},{9,9},{1... | collective-permute-start | bytes 393224 | tf_op jit(solution)/shard_map/ppermute | solution.py:61
  70.8 3.1 %collective-permute-done.12 = bf16[128,512]{1,0:T(8,128)(2,1)S(1)} collective-permute-done((bf16[128,512]{1,0:T(8,128)(2,1)S(1)}, bf16[128,512]{1,0:T(8,128)(2,1)S(1)}, u32[]{:S(2)}, u32[]{:S(2)}) %collective-permute-start.12) | collective-permute-done | bytes 131104 | tf_op jit(solution)/shard_map/ppermute | solution.py:61
  73.9 1.9 collective-permute-done.15.refs_0_
  75.8 1.9 collective-permute-done.18.refs_2_
  80.6 1.9 collective-permute-start.22
  82.9 2.1 collective-permute-done.21.refs_1_
  85.0 1.8 collective-permute-done.22.refs_2_
  86.9 2.8 %collective-permute-start.25 = (bf16[144,512]{1,0:T(8,128)(2,1)S(1)}, bf16[144,512]{1,0:T(8,128)(2,1)S(1)}, u32[]{:S(2)}, u32[]{:S(2)}) collective-permute-start(bf16[144,512]{1,0:T(8,128)(2,1)S(1)} %shard_map.219.own_ref), channel_id=1, source_target_pairs={{0,68},{1,69},{2,70},{3,71},{4,64},{5,65},{6,66},{7,67},{8,76},{9,... | collective-permute-start | bytes 442376 | tf_op jit(solution)/shard_map/ppermute | solution.py:61
  90.4 3.0 %collective-permute-done.25.refs_2_ = bf16[144,512]{1,0:T(8,128)(2,1)S(1)} collective-permute-done((bf16[144,512]{1,0:T(8,128)(2,1)S(1)}, bf16[144,512]{1,0:T(8,128)(2,1)S(1)}, u32[]{:S(2)}, u32[]{:S(2)}) %collective-permute-start.25) | collective-permute-done | bytes 147488 | tf_op jit(solution)/shard_map/ppermute | solution.py:61
  93.4 1.9 collective-permute-done.24.refs_1_
  95.4 2.0 collective-permute-start.28
  98.7 2.0 collective-permute-done.28.refs_3_
  100.8 2.0 collective-permute-done.27.refs_2_
  103.4 2.1 collective-permute-start.32
  105.7 2.3 collective-permute-start.34
  107.9 6.1 %collective-permute-start.29 = (bf16[528,512]{1,0:T(8,128)(2,1)S(1)}, bf16[528,512]{1,0:T(8,128)(2,1)S(1)}, u32[]{:S(2)}, u32[]{:S(2)}) collective-permute-start(bf16[528,512]{1,0:T(8,128)(2,1)S(1)} %shard_map.221.refs_1_.own), channel_id=1, source_target_pairs={{0,32},{1,33},{2,34},{3,35},{4,36},{5,37},{6,38},{7,39},{8,40},{9,... | collective-permute-start | bytes 1622024 | tf_op jit(solution)/shard_map/ppermute | solution.py:61
  114.0 4.7 %collective-permute-start.33 = (bf16[528,512]{1,0:T(8,128)(2,1)S(1)}, bf16[528,512]{1,0:T(8,128)(2,1)S(1)}, u32[]{:S(2)}, u32[]{:S(2)}) collective-permute-start(bf16[528,512]{1,0:T(8,128)(2,1)S(1)} %collective-permute-done.32.refs_5_), channel_id=1, source_target_pairs={{0,32},{1,33},{2,34},{3,35},{4,36},{5,37},{6,38},{7,39},{8,40},{9,... | collective-permute-start | bytes 1622024 | tf_op jit(solution)/shard_map/ppermute | solution.py:61
  119.9 5.5 %collective-permute-start.31 = (bf16[528,512]{1,0:T(8,128)(2,1)S(1)}, bf16[528,512]{1,0:T(8,128)(2,1)S(1)}, u32[]{:S(2)}, u32[]{:S(2)}) collective-permute-start(bf16[528,512]{1,0:T(8,128)(2,1)S(1)} %collective-permute-done.30.refs_3_), channel_id=1, source_target_pairs={{0,32},{1,33},{2,34},{3,35},{4,36},{5,37},{6,38},{7,39},{8,40},{9,... | collective-permute-start | bytes 1622024 | tf_op jit(solution)/shard_map/ppermute | solution.py:61
  125.4 3.2 %collective-permute-start.35 = (bf16[528,512]{1,0:T(8,128)(2,1)}, bf16[528,512]{1,0:T(8,128)(2,1)}, u32[]{:S(2)}, u32[]{:S(2)}) collective-permute-start(bf16[528,512]{1,0:T(8,128)(2,1)} %collective-permute-done.34.refs_1_), channel_id=1, source_target_pairs={{0,32},{1,33},{2,34},{3,35},{4,36},{5,37},{6,38},{7,39},{8,40},{9,... | collective-permute-start | bytes 1622024 | tf_op jit(solution)/shard_map/ppermute | solution.py:61
  129.8 97.4 %shard_map.222 = (bf16[512,512]{1,0:T(8,128)(2,1)}, bf16[512,512]{1,0:T(8,128)(2,1)}, bf16[512,512]{1,0:T(8,128)(2,1)}, bf16[512,512]{1,0:T(8,128)(2,1)}, bf16[5...) custom-call(s32[3]{0:T(128)} %copy-done.6, bf16[528,512]{1,0:T(8,128)(2,1)} %copy-done, bf16[528,512]{1,0:T(8,128)(2,1)} %copy-done.1, ...), custom_call_target="tpu_custom_call" | custom-call | tf_op jit(solution)/shard_map/pallas_call | solution.py:422
  227.3 33.7 %shard_map.223 = (bf16[512,512]{1,0:T(8,128)(2,1)}, bf16[512,512]{1,0:T(8,128)(2,1)}, bf16[512,512]{1,0:T(8,128)(2,1)}, bf16[512,512]{1,0:T(8,128)(2,1)}, bf16[5...) custom-call(s32[3]{0:T(128)} %copy-done.6, ...), custom_call_target="tpu_custom_call", output_to_operand_aliasing={{0}: (3, {}), {1}: (4, {}), {2}: (5, {}), {3}: (6, {}), {4}... | custom-call | tf_op jit(solution)/shard_map/pallas_call | solution.py:422
  (106 shorter events, 21.0 us)
Async XLA Ops:
  0.7 13.1 %collective-permute-start.3 = (bf16[128,512]{1,0:T(8,128)(2,1)}, bf16[128,512]{1,0:T(8,128)(2,1)S(1)}, u32[]{:S(2)}, u32[]{:S(2)}) collective-permute-start(bf16[128,512]{1,0:T(8,128)(2,1)} %bitcast.20), channel_id=1, source_target_pairs={{0,3},{1,2},{2,1},{3,0},{4,56},{5,57},{6,58},{7,59},{8,11},{9,10},... | collective-permute-start | bytes 393224 | tf_op jit(solution)/shard_map/ppermute | solution.py:61
  5.8 8.0 %collective-permute-start.2 = (bf16[128,512]{1,0:T(8,128)(2,1)}, bf16[128,512]{1,0:T(8,128)(2,1)S(1)}, u32[]{:S(2)}, u32[]{:S(2)}) collective-permute-start(bf16[128,512]{1,0:T(8,128)(2,1)} %bitcast.21), channel_id=1, source_target_pairs={{0,2},{1,3},{2,0},{3,1},{4,48},{5,49},{6,50},{7,51},{8,10},{9,11},... | collective-permute-start | bytes 393224 | tf_op jit(solution)/shard_map/ppermute | solution.py:61
  9.4 6.1 %collective-permute-start.1 = (bf16[128,512]{1,0:T(8,128)(2,1)}, bf16[128,512]{1,0:T(8,128)(2,1)S(1)}, u32[]{:S(2)}, u32[]{:S(2)}) collective-permute-start(bf16[128,512]{1,0:T(8,128)(2,1)} %bitcast.22), channel_id=1, source_target_pairs={{0,1},{1,0},{2,3},{3,2},{4,40},{5,41},{6,42},{7,43},{8,9},{9,8},{1... | collective-permute-start | bytes 393224 | tf_op jit(solution)/shard_map/ppermute | solution.py:61
  10.4 6.5 %collective-permute-start = (bf16[128,512]{1,0:T(8,128)(2,1)}, bf16[128,512]{1,0:T(8,128)(2,1)S(1)}, u32[]{:S(2)}, u32[]{:S(2)}) collective-permute-start(bf16[128,512]{1,0:T(8,128)(2,1)} %bitcast.23), channel_id=1, source_target_pairs={{0,0},{1,1},{2,2},{3,3},{4,32},{5,33},{6,34},{7,35},{8,8},{9,9},{1... | collective-permute-start | bytes 393224 | tf_op jit(solution)/shard_map/ppermute | solution.py:61
  16.9 14.9 %collective-permute-start.7 = (bf16[512,512]{1,0:T(8,128)(2,1)S(1)}, bf16[512,512]{1,0:T(8,128)(2,1)S(1)}, u32[]{:S(2)}, u32[]{:S(2)}) collective-permute-start(bf16[512,512]{1,0:T(8,128)(2,1)S(1)} %pad_maximum_fusion.refs_0_), channel_id=1, source_target_pairs={{0,24},{1,25},{2,26},{3,27},{4,28},{5,29},{6,30},{7,31},{8,16},{9,... | collective-permute-start | bytes 1572872 | tf_op jit(solution)/shard_map/ppermute | solution.py:61
  17.8 14.1 %collective-permute-start.6 = (bf16[512,512]{1,0:T(8,128)(2,1)S(1)}, bf16[512,512]{1,0:T(8,128)(2,1)S(1)}, u32[]{:S(2)}, u32[]{:S(2)}) collective-permute-start(bf16[512,512]{1,0:T(8,128)(2,1)S(1)} %pad_maximum_fusion.refs_0_), channel_id=1, source_target_pairs={{0,16},{1,17},{2,18},{3,19},{4,20},{5,21},{6,22},{7,23},{8,24},{9,... | collective-permute-start | bytes 1572872 | tf_op jit(solution)/shard_map/ppermute | solution.py:61
  20.7 11.8 %collective-permute-start.5 = (bf16[512,512]{1,0:T(8,128)(2,1)S(1)}, bf16[512,512]{1,0:T(8,128)(2,1)S(1)}, u32[]{:S(2)}, u32[]{:S(2)}) collective-permute-start(bf16[512,512]{1,0:T(8,128)(2,1)S(1)} %pad_maximum_fusion.refs_0_), channel_id=1, source_target_pairs={{0,8},{1,9},{2,10},{3,11},{4,12},{5,13},{6,14},{7,15},{8,0},{9,1},... | collective-permute-start | bytes 1572872 | tf_op jit(solution)/shard_map/ppermute | solution.py:61
  20.7 12.0 %collective-permute-start.4 = (bf16[272,512]{1,0:T(8,128)(2,1)S(1)}, bf16[272,512]{1,0:T(8,128)(2,1)S(1)}, u32[]{:S(2)}, u32[]{:S(2)}) collective-permute-start(bf16[272,512]{1,0:T(8,128)(2,1)S(1)} %fusion.1), channel_id=1, source_target_pairs={{0,0},{1,1},{2,2},{3,3},{4,32},{5,33},{6,34},{7,35},{8,8},{9,9},{1... | collective-permute-start | bytes 835592 | tf_op jit(solution)/shard_map/ppermute | solution.py:61
  23.7 9.9 %collective-permute-start.8 = (bf16[512,512]{1,0:T(8,128)(2,1)S(1)}, bf16[512,512]{1,0:T(8,128)(2,1)}, u32[]{:S(2)}, u32[]{:S(2)}) collective-permute-start(bf16[512,512]{1,0:T(8,128)(2,1)S(1)} %pad_maximum_fusion.refs_0_), channel_id=1, source_target_pairs={{0,32},{1,33},{2,34},{3,35},{4,36},{5,37},{6,38},{7,39},{8,40},{9,... | collective-permute-start | bytes 1572872 | tf_op jit(solution)/shard_map/ppermute | solution.py:61
  58.6 3.5 %collective-permute-start.13 = (bf16[512,512]{1,0:T(8,128)(2,1)S(1)}, bf16[512,512]{1,0:T(8,128)(2,1)S(1)}, u32[]{:S(2)}, u32[]{:S(2)}) collective-permute-start(bf16[512,512]{1,0:T(8,128)(2,1)S(1)} %get-tuple-element.59), channel_id=1, source_target_pairs={{0,32},{1,33},{2,34},{3,35},{4,36},{5,37},{6,38},{7,39},{8,40},{9,... | collective-permute-start | bytes 1572872 | tf_op jit(solution)/shard_map/ppermute | solution.py:61
  59.0 5.0 %collective-permute-start.17 = (bf16[512,512]{1,0:T(8,128)(2,1)S(1)}, bf16[512,512]{1,0:T(8,128)(2,1)S(1)}, u32[]{:S(2)}, u32[]{:S(2)}) collective-permute-start(bf16[512,512]{1,0:T(8,128)(2,1)S(1)} %get-tuple-element.66), channel_id=1, source_target_pairs={{0,32},{1,33},{2,34},{3,35},{4,36},{5,37},{6,38},{7,39},{8,40},{9,... | collective-permute-start | bytes 1572872 | tf_op jit(solution)/shard_map/ppermute | solution.py:61
  61.8 12.1 %collective-permute-start.16 = (bf16[528,512]{1,0:T(8,128)(2,1)S(1)}, bf16[528,512]{1,0:T(8,128)(2,1)S(1)}, u32[]{:S(2)}, u32[]{:S(2)}) collective-permute-start(bf16[528,512]{1,0:T(8,128)(2,1)S(1)} %get-tuple-element.64), channel_id=1, source_target_pairs={{0,2},{1,3},{2,0},{3,1},{4,6},{5,7},{6,4},{7,5},{8,10},{9,11},{10,... | collective-permute-start | bytes 1622024 | tf_op jit(solution)/shard_map/ppermute | solution.py:61
  62.8 12.9 %collective-permute-start.15 = (bf16[528,512]{1,0:T(8,128)(2,1)S(1)}, bf16[528,512]{1,0:T(8,128)(2,1)S(1)}, u32[]{:S(2)}, u32[]{:S(2)}) collective-permute-start(bf16[528,512]{1,0:T(8,128)(2,1)S(1)} %shard_map.216), channel_id=1, source_target_pairs={{0,1},{1,0},{2,3},{3,2},{4,5},{5,4},{6,7},{7,6},{8,9},{9,8},{10,11... | collective-permute-start | bytes 1622024 | tf_op jit(solution)/shard_map/ppermute | solution.py:61
  64.1 13.6 %collective-permute-start.18 = (bf16[528,512]{1,0:T(8,128)(2,1)S(1)}, bf16[528,512]{1,0:T(8,128)(2,1)S(1)}, u32[]{:S(2)}, u32[]{:S(2)}) collective-permute-start(bf16[528,512]{1,0:T(8,128)(2,1)S(1)} %shard_map.217), channel_id=1, source_target_pairs={{0,3},{1,2},{2,1},{3,0},{4,7},{5,6},{6,5},{7,4},{8,11},{9,10},{10,... | collective-permute-start | bytes 1622024 | tf_op jit(solution)/shard_map/ppermute | solution.py:61
  66.5 11.1 %collective-permute-start.19 = (bf16[512,512]{1,0:T(8,128)(2,1)S(1)}, bf16[512,512]{1,0:T(8,128)(2,1)S(1)}, u32[]{:S(2)}, u32[]{:S(2)}) collective-permute-start(bf16[512,512]{1,0:T(8,128)(2,1)S(1)} %get-tuple-element.69), channel_id=1, source_target_pairs={{0,32},{1,33},{2,34},{3,35},{4,36},{5,37},{6,38},{7,39},{8,40},{9,... | collective-permute-start | bytes 1572872 | tf_op jit(solution)/shard_map/ppermute | solution.py:61
  67.3 6.6 %collective-permute-start.12 = (bf16[128,512]{1,0:T(8,128)(2,1)S(1)}, bf16[128,512]{1,0:T(8,128)(2,1)S(1)}, u32[]{:S(2)}, u32[]{:S(2)}) collective-permute-start(bf16[128,512]{1,0:T(8,128)(2,1)S(1)} %get-tuple-element.57), channel_id=1, source_target_pairs={{0,0},{1,1},{2,2},{3,3},{4,32},{5,33},{6,34},{7,35},{8,8},{9,9},{1... | collective-permute-start | bytes 393224 | tf_op jit(solution)/shard_map/ppermute | solution.py:61
  78.6 4.4 %collective-permute-start.20 = (bf16[144,512]{1,0:T(8,128)(2,1)S(1)}, bf16[144,512]{1,0:T(8,128)(2,1)S(1)}, u32[]{:S(2)}, u32[]{:S(2)}) collective-permute-start(bf16[144,512]{1,0:T(8,128)(2,1)S(1)} %get-tuple-element.75), channel_id=1, source_target_pairs={{0,8},{1,9},{2,10},{3,11},{4,12},{5,13},{6,14},{7,15},{8,0},{9,1},... | collective-permute-start | bytes 442376 | tf_op jit(solution)/shard_map/ppermute | solution.py:61
  79.4 5.6 %collective-permute-start.21 = (bf16[144,512]{1,0:T(8,128)(2,1)S(1)}, bf16[144,512]{1,0:T(8,128)(2,1)S(1)}, u32[]{:S(2)}, u32[]{:S(2)}) collective-permute-start(bf16[144,512]{1,0:T(8,128)(2,1)S(1)} %get-tuple-element.76), channel_id=1, source_target_pairs={{0,16},{1,17},{2,18},{3,19},{4,20},{5,21},{6,22},{7,23},{8,24},{9,... | collective-permute-start | bytes 442376 | tf_op jit(solution)/shard_map/ppermute | solution.py:61
  80.6 6.2 %collective-permute-start.22 = (bf16[144,512]{1,0:T(8,128)(2,1)S(1)}, bf16[144,512]{1,0:T(8,128)(2,1)S(1)}, u32[]{:S(2)}, u32[]{:S(2)}) collective-permute-start(bf16[144,512]{1,0:T(8,128)(2,1)S(1)} %get-tuple-element.77), channel_id=1, source_target_pairs={{0,24},{1,25},{2,26},{3,27},{4,28},{5,29},{6,30},{7,31},{8,16},{9,... | collective-permute-start | bytes 442376 | tf_op jit(solution)/shard_map/ppermute | solution.py:61
  86.9 6.5 %collective-permute-start.25 = (bf16[144,512]{1,0:T(8,128)(2,1)S(1)}, bf16[144,512]{1,0:T(8,128)(2,1)S(1)}, u32[]{:S(2)}, u32[]{:S(2)}) collective-permute-start(bf16[144,512]{1,0:T(8,128)(2,1)S(1)} %shard_map.219.own_ref), channel_id=1, source_target_pairs={{0,68},{1,69},{2,70},{3,71},{4,64},{5,65},{6,66},{7,67},{8,76},{9,... | collective-permute-start | bytes 442376 | tf_op jit(solution)/shard_map/ppermute | solution.py:61
  89.7 5.6 %collective-permute-start.24 = (bf16[144,512]{1,0:T(8,128)(2,1)S(1)}, bf16[144,512]{1,0:T(8,128)(2,1)S(1)}, u32[]{:S(2)}, u32[]{:S(2)}) collective-permute-start(bf16[144,512]{1,0:T(8,128)(2,1)S(1)} %shard_map.219.own_ref), channel_id=1, source_target_pairs={{0,64},{1,65},{2,66},{3,67},{4,68},{5,69},{6,70},{7,71},{8,72},{9,... | collective-permute-start | bytes 442376 | tf_op jit(solution)/shard_map/ppermute | solution.py:61
  90.2 5.1 %collective-permute-start.23 = (bf16[144,512]{1,0:T(8,128)(2,1)S(1)}, bf16[144,512]{1,0:T(8,128)(2,1)S(1)}, u32[]{:S(2)}, u32[]{:S(2)}) collective-permute-start(bf16[144,512]{1,0:T(8,128)(2,1)S(1)} %shard_map.219.own_ref), channel_id=1, source_target_pairs={{0,4},{1,5},{2,6},{3,7},{4,0},{5,1},{6,2},{7,3},{8,12},{9,13},{10,... | collective-permute-start | bytes 442376 | tf_op jit(solution)/shard_map/ppermute | solution.py:61
  95.4 5.4 %collective-permute-start.28 = (bf16[128,512]{1,0:T(8,128)(2,1)S(1)}, bf16[128,512]{1,0:T(8,128)(2,1)S(1)}, u32[]{:S(2)}, u32[]{:S(2)}) collective-permute-start(bf16[128,512]{1,0:T(8,128)(2,1)S(1)} %get-tuple-element.79.refs_0_), channel_id=1, source_target_pairs={{0,24},{1,25},{2,26},{3,27},{4,28},{5,29},{6,30},{7,31},{8,16},{9,... | collective-permute-start | bytes 393224 | tf_op jit(solution)/shard_map/ppermute | solution.py:61
  97.4 5.3 %collective-permute-start.27 = (bf16[128,512]{1,0:T(8,128)(2,1)S(1)}, bf16[128,512]{1,0:T(8,128)(2,1)S(1)}, u32[]{:S(2)}, u32[]{:S(2)}) collective-permute-start(bf16[128,512]{1,0:T(8,128)(2,1)S(1)} %get-tuple-element.79.refs_0_), channel_id=1, source_target_pairs={{0,16},{1,17},{2,18},{3,19},{4,20},{5,21},{6,22},{7,23},{8,24},{9,... | collective-permute-start | bytes 393224 | tf_op jit(solution)/shard_map/ppermute | solution.py:61
  97.4 5.3 %collective-permute-start.26 = (bf16[128,512]{1,0:T(8,128)(2,1)S(1)}, bf16[128,512]{1,0:T(8,128)(2,1)S(1)}, u32[]{:S(2)}, u32[]{:S(2)}) collective-permute-start(bf16[128,512]{1,0:T(8,128)(2,1)S(1)} %get-tuple-element.79.refs_0_), channel_id=1, source_target_pairs={{0,8},{1,9},{2,10},{3,11},{4,12},{5,13},{6,14},{7,15},{8,0},{9,1},... | collective-permute-start | bytes 393224 | tf_op jit(solution)/shard_map/ppermute | solution.py:61
  103.4 10.7 %collective-permute-start.32 = (bf16[528,512]{1,0:T(8,128)(2,1)S(1)}, bf16[528,512]{1,0:T(8,128)(2,1)S(1)}, u32[]{:S(2)}, u32[]{:S(2)}) collective-permute-start(bf16[528,512]{1,0:T(8,128)(2,1)S(1)} %shard_map.221.refs_1_.own), channel_id=1, source_target_pairs={{0,1},{1,0},{2,3},{3,2},{4,5},{5,4},{6,7},{7,6},{8,9},{9,8},{10,11... | collective-permute-start | bytes 1622024 | tf_op jit(solution)/shard_map/ppermute | solution.py:61
  105.4 14.5 %collective-permute-start.30 = (bf16[528,512]{1,0:T(8,128)(2,1)S(1)}, bf16[528,512]{1,0:T(8,128)(2,1)S(1)}, u32[]{:S(2)}, u32[]{:S(2)}) collective-permute-start(bf16[528,512]{1,0:T(8,128)(2,1)S(1)} %shard_map.221.refs_1_.own), channel_id=1, source_target_pairs={{0,2},{1,3},{2,0},{3,1},{4,6},{5,7},{6,4},{7,5},{8,10},{9,11},{10,... | collective-permute-start | bytes 1622024 | tf_op jit(solution)/shard_map/ppermute | solution.py:61
  105.7 19.7 %collective-permute-start.34 = (bf16[528,512]{1,0:T(8,128)(2,1)S(1)}, bf16[528,512]{1,0:T(8,128)(2,1)}, u32[]{:S(2)}, u32[]{:S(2)}) collective-permute-start(bf16[528,512]{1,0:T(8,128)(2,1)S(1)} %shard_map.221.refs_1_.own), channel_id=1, source_target_pairs={{0,3},{1,2},{2,1},{3,0},{4,7},{5,6},{6,5},{7,4},{8,11},{9,10},{10,... | collective-permute-start | bytes 1622024 | tf_op jit(solution)/shard_map/ppermute | solution.py:61
  107.9 20.7 %collective-permute-start.29 = (bf16[528,512]{1,0:T(8,128)(2,1)S(1)}, bf16[528,512]{1,0:T(8,128)(2,1)S(1)}, u32[]{:S(2)}, u32[]{:S(2)}) collective-permute-start(bf16[528,512]{1,0:T(8,128)(2,1)S(1)} %shard_map.221.refs_1_.own), channel_id=1, source_target_pairs={{0,32},{1,33},{2,34},{3,35},{4,36},{5,37},{6,38},{7,39},{8,40},{9,... | collective-permute-start | bytes 1622024 | tf_op jit(solution)/shard_map/ppermute | solution.py:61
  114.0 14.6 %collective-permute-start.33 = (bf16[528,512]{1,0:T(8,128)(2,1)S(1)}, bf16[528,512]{1,0:T(8,128)(2,1)S(1)}, u32[]{:S(2)}, u32[]{:S(2)}) collective-permute-start(bf16[528,512]{1,0:T(8,128)(2,1)S(1)} %collective-permute-done.32.refs_5_), channel_id=1, source_target_pairs={{0,32},{1,33},{2,34},{3,35},{4,36},{5,37},{6,38},{7,39},{8,40},{9,... | collective-permute-start | bytes 1622024 | tf_op jit(solution)/shard_map/ppermute | solution.py:61
  119.9 8.7 %collective-permute-start.31 = (bf16[528,512]{1,0:T(8,128)(2,1)S(1)}, bf16[528,512]{1,0:T(8,128)(2,1)S(1)}, u32[]{:S(2)}, u32[]{:S(2)}) collective-permute-start(bf16[528,512]{1,0:T(8,128)(2,1)S(1)} %collective-permute-done.30.refs_3_), channel_id=1, source_target_pairs={{0,32},{1,33},{2,34},{3,35},{4,36},{5,37},{6,38},{7,39},{8,40},{9,... | collective-permute-start | bytes 1622024 | tf_op jit(solution)/shard_map/ppermute | solution.py:61
  125.4 101.9 %collective-permute-start.35 = (bf16[528,512]{1,0:T(8,128)(2,1)}, bf16[528,512]{1,0:T(8,128)(2,1)}, u32[]{:S(2)}, u32[]{:S(2)}) collective-permute-start(bf16[528,512]{1,0:T(8,128)(2,1)} %collective-permute-done.34.refs_1_), channel_id=1, source_target_pairs={{0,32},{1,33},{2,34},{3,35},{4,36},{5,37},{6,38},{7,39},{8,40},{9,... | collective-permute-start | bytes 1622024 | tf_op jit(solution)/shard_map/ppermute | solution.py:61
  (25 other events, 240.5 us)

commit v6 on v5

--- a/solution.py
+++ b/solution.py
@@ -114,16 +114,13 @@
     return out
 
 
-def step_kernel(where, moved, seen, w_query, w_key, w_value, w_out, w_up, w_down, gain_attn, gain_mlp, *refs):
+def step_kernel(where, moved, seen, packed, w_up, w_down, gain_attn, gain_mlp, *refs):
     parts, (output, gains_out), refs = refs[:PARTS], refs[PARTS : PARTS + 2], refs[PARTS + 2 :]
     gives, keeps, refs = refs[:4], refs[4:8], refs[8:]
-    feats, scores, pulls, sums, stat, give, keep, tail, sems, out_sems = refs
+    scores, pulls, sums, stat, give, keep, tail, out_sems = refs
     f32, b16 = jnp.float32, jnp.bfloat16
-    copies = [pltpu.make_async_copy(parts[p], feats.at[p], sems.at[p]) for p in range(PARTS)]
-    for copy in copies:
-        copy.start()
-
-    width = w_query.shape[0]
+    width = w_up.shape[0]
+    w_query, w_key, w_value, w_out = (packed.at[pl.ds(i * width, width)] for i in range(4))
     head = width // HEADS
     factor = 1.0 / math.sqrt(head)
     cols = [slice(h * head, (h + 1) * head) for h in range(HEADS)]
@@ -149,8 +146,7 @@
     stat[...] = jnp.full_like(stat, -1e30)
 
     for p in range(PARTS):
-        copies[p].wait()
-        key_rows = mult(feats[p], w_key[...]).astype(b16)
+        key_rows = mult(parts[p][...], w_key[...]).astype(b16)
         allowed = seen[p : p + 1, :] > 0
         for r, c in zip(pair_rows, pair_cols):
             part = mult_nt(query_pairs[r, :], key_rows[:, c]) * factor
@@ -172,7 +168,7 @@
     for p in range(PARTS):
         part = scores[p] * inverse_sum
         scores[p] = part
-        sums[...] += mult(part.astype(b16), feats[p])
+        sums[...] += mult(part.astype(b16), parts[p][...])
 
     u_high, u_low = two_parts(sums[...])
     context = jnp.concatenate(
@@ -232,7 +228,7 @@
     stat[...] = jnp.zeros_like(stat)
 
     for p in range(PARTS):
-        part = mult_nt(pulled, feats[p])
+        part = mult_nt(pulled, parts[p][...])
         pulls[p] = part
         stat[...] += lanes(part * scores[p], jnp.add)
 
@@ -241,7 +237,7 @@
 
     for p in range(PARTS):
         part = (scores[p] * (pulls[p] - centre) * factor).astype(b16)
-        sums[...] += mult(part, feats[p])
+        sums[...] += mult(part, parts[p][...])
 
     t_high, t_low = two_parts(sums[...])
     grad_query_rows = jnp.concatenate(
@@ -295,10 +291,9 @@
         ]
         + [jax.ShapeDtypeStruct(shape, b16) for shape in quarters]
         + [jax.ShapeDtypeStruct((4 * CHUNK, 512), b16)] * 4,
-        in_specs=[SMEM] + [VMEM] * 10 + [ANY] * PARTS,
+        in_specs=[SMEM] + [VMEM] * (7 + PARTS),
         out_specs=[VMEM] * 2 + [ANY] * 8,
         scratch_shapes=[
-            pltpu.VMEM((PARTS, 512, 512), b16),
             pltpu.VMEM((PARTS, 512, 512), f32),
             pltpu.VMEM((PARTS, 512, 512), f32),
             pltpu.VMEM((512, 512), f32),
@@ -306,10 +301,9 @@
             pltpu.VMEM((4, 4 * CHUNK, 512), b16),
             pltpu.VMEM((4, 4 * CHUNK, 512), b16),
             pltpu.VMEM((TAIL, 512), b16),
-            pltpu.SemaphoreType.DMA((PARTS,)),
             pltpu.SemaphoreType.DMA((9,)),
         ],
-        compiler_params=pltpu.CompilerParams(vmem_limit_bytes=52 << 20),
+        compiler_params=pltpu.CompilerParams(vmem_limit_bytes=38 << 20),
         cost_estimate=pl.CostEstimate(
             flops=12 * 10**9, bytes_accessed=18 * 10**6, transcendentals=3 * 10**6
         ),
@@ -396,43 +390,23 @@
     out[4 * CHUNK :, :] = gains[...]
 
 
-def place_kernel(which, where, *refs):
-    count = len(which)
-    arranged, grads, sems = refs[:count], refs[-7:-1], refs[-1]
-    copies = []
-    for i, (side, mask) in enumerate(which):
+def place_kernel(where, *refs):
+    groups, grads, gain_attn, gain_mlp = (refs[0:4], refs[4:8]), refs[8:14], refs[14], refs[15]
+    for side, group in enumerate(groups):
         holder = where[0] ^ side
-        part = holder * 4 + (where[1 + side] ^ mask)
-        for j, (at, rows) in enumerate(LAYOUT):
-            to = pl.ds(pl.multiple_of(part * (4 * rows), 64), 4 * rows)
-            grad = grads[min(j, 4 if j < 6 else 5)]
-            target = grad.at[to, pl.ds(512 * (j - 4), 512)] if j in (4, 5) else grad.at[to, :]
-            copies.append(
-                pltpu.make_async_copy(arranged[i].at[pl.ds(at * 4, 4 * rows)], target, sems.at[i, j])
-            )
-    for copy in copies:
-        copy.start()
-    for copy in copies:
-        copy.wait()
-
-
-def place(which, where, arranged, grads):
-    shapes = [(512, 512)] * 4 + [(512, 1024), (1024, 512)]
-    count = len(which)
-    return pl.pallas_call(
-        lambda *refs: place_kernel(which, *refs),
-        out_shape=[jax.ShapeDtypeStruct(shape, jnp.bfloat16) for shape in shapes],
-        in_specs=[SMEM] + [ANY] * (count + len(grads)),
-        out_specs=[ANY] * 6,
-        scratch_shapes=[pltpu.SemaphoreType.DMA((count, len(LAYOUT)))],
-        input_output_aliases={1 + count + i: i for i in range(len(grads))},
-    )(where, *arranged, *grads)
-
-
-def gains_kernel(where, own, other, gain_attn, gain_mlp):
-    gains = jnp.where(where[0] == 0, take_gains(own, 4 * CHUNK), take_gains(other, 4 * CHUNK))
-    gain_attn[...] = gains[0].astype(jnp.bfloat16)
-    gain_mlp[...] = gains[1].astype(jnp.bfloat16)
+        for mask, arranged in enumerate(group):
+            part = holder * 4 + (where[1 + side] ^ mask)
+            for j, (at, rows) in enumerate(LAYOUT):
+                to = pl.ds(pl.multiple_of(part * (4 * rows), 64), 4 * rows)
+                piece = arranged[at * 4 : (at + rows) * 4, :]
+                if j in (4, 5):
+                    grads[4][to, 512 * (j - 4) : 512 * (j - 3)] = piece
+                else:
+                    grads[min(j, 5)][to, :] = piece
+    own, other = (take_gains(group[0], 4 * CHUNK) for group in groups)
+    gains = jnp.where(where[0] == 0, own, other).astype(jnp.bfloat16)
+    gain_attn[...] = gains[0]
+    gain_mlp[...] = gains[1]
 
 
 def call(kernel, outs, *operands, scalars=0):
@@ -479,21 +453,18 @@
     (mine,) = call(arrange_kernel, [message], where, gains, *chunks, scalars=1)
     own = {0: mine, **to_peers(lambda mask: mine, first)}
     other = {mask: send(own[mask], CORE) for mask in (0,) + ORDER}
-    early = [(side, mask) for mask in (0,) + ORDER[:2] for side in range(2)]
-    held = [(own, other)[side][mask] for side, mask in early]
-    *held, last = lax.optimization_barrier((*held, own[ORDER[2]]))
-    grads = place(early, where, held, ())
-    grads = place([(0, ORDER[2]), (1, ORDER[2])], where, [last, other[ORDER[2]]], grads)
-    gains = call(
-        gains_kernel, [((512,), b16)] * 2, where, held[0], held[1], scalars=1
-    )
-    return (output[None], *grads, *gains)
-
-
-def gather_features(own, others):
+    placed = call(
+        place_kernel,
+        [((512, 512), b16)] * 4 + [((512, 1024), b16), ((1024, 512), b16)] + [((512,), b16)] * 2,
+        where, *(own[mask] for mask in range(4)), *(other[mask] for mask in range(4)), scalars=1,
+    )
+    return (output[None], *placed)
+
+
+def gather_features(own, others, weights):
     near = {mask: send(own, first_swapped(mask)) for mask in (0,) + ORDER}
     mine = jnp.concatenate([near[mask] for mask in range(4)])
-    mine, others = lax.optimization_barrier((mine, others))
+    mine, others, weights = lax.optimization_barrier((mine, others, weights))
     group = [mine, *to_peers(lambda mask: mine, second).values()]
     parts = group + [send(part, CORE) for part in group]
     core, y, z = (lax.axis_index(name) for name in ("core", "y", "z"))
@@ -501,7 +472,7 @@
     holder = core ^ side
     block_y = jnp.where(holder == 0, y ^ one, y ^ two)
     block_z = jnp.where(holder == 0, z ^ two, z ^ one)
-    return parts, block_z * 8 + holder * 4 + block_y, send(others, SWAP)
+    return parts, block_z * 8 + holder * 4 + block_y, send(others, SWAP), jnp.concatenate(weights)
 
 
 def local(
@@ -519,8 +490,10 @@
     gain_mlp,
 ):
     seen = jnp.pad(visible[0].astype(jnp.bfloat16), ((0, 15), (0, 512 - visible.shape[-1])))
-    parts, blocks, moved = gather_features(
-        features[0], jnp.concatenate([queries[0], cotangent[0], seen])
+    parts, blocks, moved, packed = gather_features(
+        features[0],
+        jnp.concatenate([queries[0], cotangent[0], seen]),
+        (w_query, w_key, w_value, w_out),
     )
     seen = jnp.take(moved[2 * BLK].astype(jnp.float32), blocks)
     core, y, z = (lax.axis_index(name).astype(jnp.int32) for name in ("core", "y", "z"))
@@ -532,7 +505,7 @@
             moved,
             jnp.repeat(seen, BLK).reshape(PARTS, 512),
             parts,
-            (w_query, w_key, w_value, w_out, w_up, w_down, gain_attn[None], gain_mlp[None]),
+            (packed, w_up, w_down, gain_attn[None], gain_mlp[None]),
         )
     )
 

time: 262 us -> 130 us (0.50)
  Pallas kernels: 157 us -> 24.5 us
  starting transfers between devices: 63.2 us -> 55 us
  waiting for transfers between devices: 35.9 us -> 40.5 us
  other arithmetic: 1.13 us -> 4.84 us
    pallas_call x2 -> x0, Pallas kernels: 131 us -> none  [place(): pl.pallas_call(lambda *refs: place_kernel(which, *refs), out_shape=[jax.S...]
    ppermute x36, starting transfers between devices: 63.2 us -> 55 us  [send(): return lax.ppermute(value, AXES, pairs)]
    ppermute x36, waiting for transfers between devices: 35.9 us -> 40.5 us  [send(): return lax.ppermute(value, AXES, pairs)]
    pallas_call x1, Pallas kernels: 22.9 us -> 19.6 us  [device_step(): pl.pallas_call(step_kernel, out_shape=[jax.ShapeDtypeStruct((BLK, 512), b...]
  transfers between devices with their start and end apart: 36 -> 36, of which waited for: 19 -> 23; matrix products, arithmetic and copies ran while one was open for 1% -> 4% of each run, Pallas kernels for 38% -> 0%
where the time goes in v6:
time: 130 us
  starting transfers between devices  55 us (42%)
  waiting for transfers between devices  40.5 us (31%)
  Pallas kernels  24.5 us (19%)
  other arithmetic  4.84 us (4%)
  local copies, waits for them, and re-layouts  4.06 us (3%)
    ppermute x36, starting transfers between devices, send(): return lax.ppermute(value, AXES, pairs)  55 us
    ppermute x36, waiting for transfers between devices, send(): return lax.ppermute(value, AXES, pairs)  40.5 us
    pallas_call x1, Pallas kernels, device_step(): pl.pallas_call(step_kernel, out_shape=[jax.ShapeDtypeStruct((BLK, 512), b...  19.6 us
    pallas_call x8, Pallas kernels, call(): pl.pallas_call(kernel, out_shape=[jax.ShapeDtypeStruct(shape, dtype) for...  4.84 us
    unnamed x9, local copies, waits for them, and re-layouts  3.11 us
  transfers between devices with their start and end apart: 36, of which 23 were waited for; matrix products, arithmetic and copies ran while one was open for 4% of the time, Pallas kernels for 0%

profile of v6, /device:TPU:1, one launch (start us, length us, event | category | flops | bytes accessed | tf_op | source)
XLA Modules:
  0.0 129.7 jit_solution(10969394986609842847)
XLA Ops:
  0.6 5.1 %collective-permute-start.3 = (bf16[128,512]{1,0:T(8,128)(2,1)}, bf16[128,512]{1,0:T(8,128)(2,1)S(1)}, u32[]{:S(2)}, u32[]{:S(2)}) collective-permute-start(bf16[128,512]{1,0:T(8,128)(2,1)} %bitcast.20), channel_id=1, source_target_pairs={{0,3},{1,2},{2,1},{3,0},{4,56},{5,57},{6,58},{7,59},{8,11},{9,10},... | collective-permute-start | bytes 393224 | tf_op jit(solution)/shard_map/ppermute | solution.py:61
  5.8 3.6 %collective-permute-start.2 = (bf16[128,512]{1,0:T(8,128)(2,1)}, bf16[128,512]{1,0:T(8,128)(2,1)S(1)}, u32[]{:S(2)}, u32[]{:S(2)}) collective-permute-start(bf16[128,512]{1,0:T(8,128)(2,1)} %bitcast.21), channel_id=1, source_target_pairs={{0,2},{1,3},{2,0},{3,1},{4,48},{5,49},{6,50},{7,51},{8,10},{9,11},... | collective-permute-start | bytes 393224 | tf_op jit(solution)/shard_map/ppermute | solution.py:61
  10.4 2.3 %collective-permute-start = (bf16[128,512]{1,0:T(8,128)(2,1)}, bf16[128,512]{1,0:T(8,128)(2,1)S(1)}, u32[]{:S(2)}, u32[]{:S(2)}) collective-permute-start(bf16[128,512]{1,0:T(8,128)(2,1)} %bitcast.23), channel_id=1, source_target_pairs={{0,0},{1,1},{2,2},{3,3},{4,32},{5,33},{6,34},{7,35},{8,8},{9,9},{1... | collective-permute-start | bytes 393224 | tf_op jit(solution)/shard_map/ppermute | solution.py:61
  13.4 1.7 %fusion.1 = bf16[272,512]{1,0:T(8,128)(2,1)} fusion(bf16[1,32]{1,0:T(2,128)(2,1)S(1)} %convert_bitcast_fusion, bf16[128,512]{1,0:T(8,128)(2,1)} %bitcast.17, bf16[128,512]{1,0:T(8,128)(2,1)} %bitcast.18), kind=kLoop, calls=%fused_computation.5 | loop fusion | flops 1114112 | bytes 540736 | tf_op jit(solution)/shard_map/concatenate | solution.py:495
  15.5 1.3 %collective-permute-done = bf16[128,512]{1,0:T(8,128)(2,1)S(1)} collective-permute-done((bf16[128,512]{1,0:T(8,128)(2,1)}, bf16[128,512]{1,0:T(8,128)(2,1)S(1)}, u32[]{:S(2)}, u32[]{:S(2)}) %collective-permute-start) | collective-permute-done | bytes 131104 | tf_op jit(solution)/shard_map/ppermute | solution.py:61
  17.8 2.9 %collective-permute-start.6 = (bf16[512,512]{1,0:T(8,128)(2,1)S(1)}, bf16[512,512]{1,0:T(8,128)(2,1)}, u32[]{:S(2)}, u32[]{:S(2)}) collective-permute-start(bf16[512,512]{1,0:T(8,128)(2,1)S(1)} %pad_maximum_fusion.1.refs_0_), channel_id=1, source_target_pairs={{0,16},{1,17},{2,18},{3,19},{4,20},{5,21},{6,22},{7,23},{8,24},{9,... | collective-permute-start | bytes 1572872 | tf_op jit(solution)/shard_map/ppermute | solution.py:61
  21.4 2.7 %collective-permute-start.4 = (bf16[272,512]{1,0:T(8,128)(2,1)}, bf16[272,512]{1,0:T(8,128)(2,1)S(1)}, u32[]{:S(2)}, u32[]{:S(2)}) collective-permute-start(bf16[272,512]{1,0:T(8,128)(2,1)} %fusion.1), channel_id=1, source_target_pairs={{0,0},{1,1},{2,2},{3,3},{4,32},{5,33},{6,34},{7,35},{8,8},{9,9},{1... | collective-permute-start | bytes 835592 | tf_op jit(solution)/shard_map/ppermute | solution.py:61
  24.3 1.7 %pad_maximum_fusion.packed = bf16[2048,512]{1,0:T(8,128)(2,1)S(1)} fusion(bf16[512,512]{1,0:T(8,128)(2,1)} %param.22, bf16[512,512]{1,0:T(8,128)(2,1)} %param.21, bf16[512,512]{1,0:T(8,128)(2,1)} %param.20, bf16[512,512]{1,0:T(8,128)(2,1)} %param.19), kind=kLoop, calls=%fused_computation.1 | loop fusion | flops 8388608 | bytes 4194304 | tf_op jit(solution)/shard_map/concatenate | solution.py:475
  25.9 5.9 %collective-permute-done.7.refs_3_ = bf16[512,512]{1,0:T(8,128)(2,1)S(1)} collective-permute-done((bf16[512,512]{1,0:T(8,128)(2,1)S(1)}, bf16[512,512]{1,0:T(8,128)(2,1)S(1)}, u32[]{:S(2)}, u32[]{:S(2)}) %collective-permute-start.7) | collective-permute-done | bytes 524320 | tf_op jit(solution)/shard_map/ppermute | solution.py:61
  38.1 19.6 %shard_map.214 = (bf16[128,512]{1,0:T(8,128)(2,1)S(1)}, f32[8,512]{1,0:T(8,128)S(1)}, bf16[512,512]{1,0:T(8,128)(2,1)S(1)}, bf16[512,512]{1,0:T(8,128)(2,1)S(1)}...) custom-call(s32[3]{0:T(128)S(1)} %pad_add_fusion.where, ...), custom_call_target="tpu_custom_call" | custom-call | flops 12000000000 | bytes 18000000 | tf_op jit(solution)/shard_map/pallas_call | solution.py:286
  58.4 1.3 collective-permute-done.14.arrived
  61.9 2.0 %collective-permute-start.18 = (bf16[528,512]{1,0:T(8,128)(2,1)S(1)}, bf16[528,512]{1,0:T(8,128)(2,1)S(1)}, u32[]{:S(2)}, u32[]{:S(2)}) collective-permute-start(bf16[528,512]{1,0:T(8,128)(2,1)S(1)} %shard_map.217), channel_id=1, source_target_pairs={{0,3},{1,2},{2,1},{3,0},{4,7},{5,6},{6,5},{7,4},{8,11},{9,10},{10,... | collective-permute-start | bytes 1622024 | tf_op jit(solution)/shard_map/ppermute | solution.py:61
  64.6 3.4 %collective-permute-start.12 = (bf16[128,512]{1,0:T(8,128)(2,1)S(1)}, bf16[128,512]{1,0:T(8,128)(2,1)S(1)}, u32[]{:S(2)}, u32[]{:S(2)}) collective-permute-start(bf16[128,512]{1,0:T(8,128)(2,1)S(1)} %get-tuple-element.52), channel_id=1, source_target_pairs={{0,0},{1,1},{2,2},{3,3},{4,32},{5,33},{6,34},{7,35},{8,8},{9,9},{1... | collective-permute-start | bytes 393224 | tf_op jit(solution)/shard_map/ppermute | solution.py:61
  68.0 3.2 %collective-permute-done.12 = bf16[128,512]{1,0:T(8,128)(2,1)S(1)} collective-permute-done((bf16[128,512]{1,0:T(8,128)(2,1)S(1)}, bf16[128,512]{1,0:T(8,128)(2,1)S(1)}, u32[]{:S(2)}, u32[]{:S(2)}) %collective-permute-start.12) | collective-permute-done | bytes 131104 | tf_op jit(solution)/shard_map/ppermute | solution.py:61
  71.2 2.7 %collective-permute-done.15.refs_0_ = bf16[528,512]{1,0:T(8,128)(2,1)S(1)} collective-permute-done((bf16[528,512]{1,0:T(8,128)(2,1)S(1)}, bf16[528,512]{1,0:T(8,128)(2,1)S(1)}, u32[]{:S(2)}, u32[]{:S(2)}) %collective-permute-start.15) | collective-permute-done | bytes 540704 | tf_op jit(solution)/shard_map/ppermute | solution.py:61
  73.9 1.9 %collective-permute-done.18.refs_2_ = bf16[528,512]{1,0:T(8,128)(2,1)S(1)} collective-permute-done((bf16[528,512]{1,0:T(8,128)(2,1)S(1)}, bf16[528,512]{1,0:T(8,128)(2,1)S(1)}, u32[]{:S(2)}, u32[]{:S(2)}) %collective-permute-start.18) | collective-permute-done | bytes 540704 | tf_op jit(solution)/shard_map/ppermute | solution.py:61
  78.7 1.9 %collective-permute-start.22 = (bf16[144,512]{1,0:T(8,128)(2,1)S(1)}, bf16[144,512]{1,0:T(8,128)(2,1)S(1)}, u32[]{:S(2)}, u32[]{:S(2)}) collective-permute-start(bf16[144,512]{1,0:T(8,128)(2,1)S(1)} %get-tuple-element.72), channel_id=1, source_target_pairs={{0,24},{1,25},{2,26},{3,27},{4,28},{5,29},{6,30},{7,31},{8,16},{9,... | collective-permute-start | bytes 442376 | tf_op jit(solution)/shard_map/ppermute | solution.py:61
  81.0 2.1 %collective-permute-done.21.refs_1_ = bf16[144,512]{1,0:T(8,128)(2,1)S(1)} collective-permute-done((bf16[144,512]{1,0:T(8,128)(2,1)S(1)}, bf16[144,512]{1,0:T(8,128)(2,1)S(1)}, u32[]{:S(2)}, u32[]{:S(2)}) %collective-permute-start.21) | collective-permute-done | bytes 147488 | tf_op jit(solution)/shard_map/ppermute | solution.py:61
  83.1 1.8 %collective-permute-done.22.refs_2_ = bf16[144,512]{1,0:T(8,128)(2,1)S(1)} collective-permute-done((bf16[144,512]{1,0:T(8,128)(2,1)S(1)}, bf16[144,512]{1,0:T(8,128)(2,1)S(1)}, u32[]{:S(2)}, u32[]{:S(2)}) %collective-permute-start.22) | collective-permute-done | bytes 147488 | tf_op jit(solution)/shard_map/ppermute | solution.py:61
  85.0 2.7 %collective-permute-start.25 = (bf16[144,512]{1,0:T(8,128)(2,1)S(1)}, bf16[144,512]{1,0:T(8,128)(2,1)S(1)}, u32[]{:S(2)}, u32[]{:S(2)}) collective-permute-start(bf16[144,512]{1,0:T(8,128)(2,1)S(1)} %shard_map.219.own_ref), channel_id=1, source_target_pairs={{0,68},{1,69},{2,70},{3,71},{4,64},{5,65},{6,66},{7,67},{8,76},{9,... | collective-permute-start | bytes 442376 | tf_op jit(solution)/shard_map/ppermute | solution.py:61
  88.4 3.0 %collective-permute-done.25.refs_2_ = bf16[144,512]{1,0:T(8,128)(2,1)S(1)} collective-permute-done((bf16[144,512]{1,0:T(8,128)(2,1)S(1)}, bf16[144,512]{1,0:T(8,128)(2,1)S(1)}, u32[]{:S(2)}, u32[]{:S(2)}) %collective-permute-start.25) | collective-permute-done | bytes 147488 | tf_op jit(solution)/shard_map/ppermute | solution.py:61
  91.4 1.9 %collective-permute-done.24.refs_1_ = bf16[144,512]{1,0:T(8,128)(2,1)S(1)} collective-permute-done((bf16[144,512]{1,0:T(8,128)(2,1)S(1)}, bf16[144,512]{1,0:T(8,128)(2,1)S(1)}, u32[]{:S(2)}, u32[]{:S(2)}) %collective-permute-start.24) | collective-permute-done | bytes 147488 | tf_op jit(solution)/shard_map/ppermute | solution.py:61
  93.4 1.9 %collective-permute-start.28 = (bf16[128,512]{1,0:T(8,128)(2,1)S(1)}, bf16[128,512]{1,0:T(8,128)(2,1)S(1)}, u32[]{:S(2)}, u32[]{:S(2)}) collective-permute-start(bf16[128,512]{1,0:T(8,128)(2,1)S(1)} %get-tuple-element.74.refs_0_), channel_id=1, source_target_pairs={{0,24},{1,25},{2,26},{3,27},{4,28},{5,29},{6,30},{7,31},{8,16},{9,... | collective-permute-start | bytes 393224 | tf_op jit(solution)/shard_map/ppermute | solution.py:61
  95.3 1.4 %collective-permute-start.26 = (bf16[128,512]{1,0:T(8,128)(2,1)S(1)}, bf16[128,512]{1,0:T(8,128)(2,1)S(1)}, u32[]{:S(2)}, u32[]{:S(2)}) collective-permute-start(bf16[128,512]{1,0:T(8,128)(2,1)S(1)} %get-tuple-element.74.refs_0_), channel_id=1, source_target_pairs={{0,8},{1,9},{2,10},{3,11},{4,12},{5,13},{6,14},{7,15},{8,0},{9,1},... | collective-permute-start | bytes 393224 | tf_op jit(solution)/shard_map/ppermute | solution.py:61
  96.7 1.8 %collective-permute-done.28.refs_3_ = bf16[128,512]{1,0:T(8,128)(2,1)S(1)} collective-permute-done((bf16[128,512]{1,0:T(8,128)(2,1)S(1)}, bf16[128,512]{1,0:T(8,128)(2,1)S(1)}, u32[]{:S(2)}, u32[]{:S(2)}) %collective-permute-start.28) | collective-permute-done | bytes 131104 | tf_op jit(solution)/shard_map/ppermute | solution.py:61
  98.5 2.1 %collective-permute-done.27.refs_2_ = bf16[128,512]{1,0:T(8,128)(2,1)S(1)} collective-permute-done((bf16[128,512]{1,0:T(8,128)(2,1)S(1)}, bf16[128,512]{1,0:T(8,128)(2,1)S(1)}, u32[]{:S(2)}, u32[]{:S(2)}) %collective-permute-start.27) | collective-permute-done | bytes 131104 | tf_op jit(solution)/shard_map/ppermute | solution.py:61
  101.2 1.3 collective-permute-start.31
  102.5 2.9 %collective-permute-start.30 = (bf16[528,512]{1,0:T(8,128)(2,1)S(1)}, bf16[528,512]{1,0:T(8,128)(2,1)S(1)}, u32[]{:S(2)}, u32[]{:S(2)}) collective-permute-start(bf16[528,512]{1,0:T(8,128)(2,1)S(1)} %shard_map.221.refs_0_), channel_id=1, source_target_pairs={{0,2},{1,3},{2,0},{3,1},{4,6},{5,7},{6,4},{7,5},{8,10},{9,11},{10,... | collective-permute-start | bytes 1622024 | tf_op jit(solution)/shard_map/ppermute | solution.py:61
  105.4 5.4 %collective-permute-start.32 = (bf16[528,512]{1,0:T(8,128)(2,1)S(1)}, bf16[528,512]{1,0:T(8,128)(2,1)S(1)}, u32[]{:S(2)}, u32[]{:S(2)}) collective-permute-start(bf16[528,512]{1,0:T(8,128)(2,1)S(1)} %shard_map.221.refs_0_), channel_id=1, source_target_pairs={{0,32},{1,33},{2,34},{3,35},{4,36},{5,37},{6,38},{7,39},{8,40},{9,... | collective-permute-start | bytes 1622024 | tf_op jit(solution)/shard_map/ppermute | solution.py:61
  110.8 6.0 %collective-permute-done.31.refs_3_ = bf16[528,512]{1,0:T(8,128)(2,1)S(1)} collective-permute-done((bf16[528,512]{1,0:T(8,128)(2,1)S(1)}, bf16[528,512]{1,0:T(8,128)(2,1)S(1)}, u32[]{:S(2)}, u32[]{:S(2)}) %collective-permute-start.31) | collective-permute-done | bytes 540704 | tf_op jit(solution)/shard_map/ppermute | solution.py:61
  116.8 6.3 %collective-permute-start.35 = (bf16[528,512]{1,0:T(8,128)(2,1)S(1)}, bf16[528,512]{1,0:T(8,128)(2,1)S(1)}, u32[]{:S(2)}, u32[]{:S(2)}) collective-permute-start(bf16[528,512]{1,0:T(8,128)(2,1)S(1)} %collective-permute-done.31.refs_3_), channel_id=1, source_target_pairs={{0,32},{1,33},{2,34},{3,35},{4,36},{5,37},{6,38},{7,39},{8,40},{9,... | collective-permute-start | bytes 1622024 | tf_op jit(solution)/shard_map/ppermute | solution.py:61
  126.2 2.8 %shard_map.222 = (bf16[512,512]{1,0:T(8,128)(2,1)}, bf16[512,512]{1,0:T(8,128)(2,1)}, bf16[512,512]{1,0:T(8,128)(2,1)}, bf16[512,512]{1,0:T(8,128)(2,1)}, bf16[5...) custom-call(s32[3]{0:T(128)S(1)} %pad_add_fusion.where, ...), custom_call_target="tpu_custom_call" | custom-call | tf_op jit(solution)/shard_map/pallas_call | solution.py:413
  (71 shorter events, 22.2 us)
Async XLA Ops:
  0.6 14.4 %collective-permute-start.3 = (bf16[128,512]{1,0:T(8,128)(2,1)}, bf16[128,512]{1,0:T(8,128)(2,1)S(1)}, u32[]{:S(2)}, u32[]{:S(2)}) collective-permute-start(bf16[128,512]{1,0:T(8,128)(2,1)} %bitcast.20), channel_id=1, source_target_pairs={{0,3},{1,2},{2,1},{3,0},{4,56},{5,57},{6,58},{7,59},{8,11},{9,10},... | collective-permute-start | bytes 393224 | tf_op jit(solution)/shard_map/ppermute | solution.py:61
  5.8 9.3 %collective-permute-start.2 = (bf16[128,512]{1,0:T(8,128)(2,1)}, bf16[128,512]{1,0:T(8,128)(2,1)S(1)}, u32[]{:S(2)}, u32[]{:S(2)}) collective-permute-start(bf16[128,512]{1,0:T(8,128)(2,1)} %bitcast.21), channel_id=1, source_target_pairs={{0,2},{1,3},{2,0},{3,1},{4,48},{5,49},{6,50},{7,51},{8,10},{9,11},... | collective-permute-start | bytes 393224 | tf_op jit(solution)/shard_map/ppermute | solution.py:61
  9.4 6.1 %collective-permute-start.1 = (bf16[128,512]{1,0:T(8,128)(2,1)}, bf16[128,512]{1,0:T(8,128)(2,1)S(1)}, u32[]{:S(2)}, u32[]{:S(2)}) collective-permute-start(bf16[128,512]{1,0:T(8,128)(2,1)} %bitcast.22), channel_id=1, source_target_pairs={{0,1},{1,0},{2,3},{3,2},{4,40},{5,41},{6,42},{7,43},{8,9},{9,8},{1... | collective-permute-start | bytes 393224 | tf_op jit(solution)/shard_map/ppermute | solution.py:61
  10.4 6.5 %collective-permute-start = (bf16[128,512]{1,0:T(8,128)(2,1)}, bf16[128,512]{1,0:T(8,128)(2,1)S(1)}, u32[]{:S(2)}, u32[]{:S(2)}) collective-permute-start(bf16[128,512]{1,0:T(8,128)(2,1)} %bitcast.23), channel_id=1, source_target_pairs={{0,0},{1,1},{2,2},{3,3},{4,32},{5,33},{6,34},{7,35},{8,8},{9,9},{1... | collective-permute-start | bytes 393224 | tf_op jit(solution)/shard_map/ppermute | solution.py:61
  16.9 14.9 %collective-permute-start.7 = (bf16[512,512]{1,0:T(8,128)(2,1)S(1)}, bf16[512,512]{1,0:T(8,128)(2,1)S(1)}, u32[]{:S(2)}, u32[]{:S(2)}) collective-permute-start(bf16[512,512]{1,0:T(8,128)(2,1)S(1)} %pad_maximum_fusion.1.refs_0_), channel_id=1, source_target_pairs={{0,24},{1,25},{2,26},{3,27},{4,28},{5,29},{6,30},{7,31},{8,16},{9,... | collective-permute-start | bytes 1572872 | tf_op jit(solution)/shard_map/ppermute | solution.py:61
  17.8 14.1 %collective-permute-start.6 = (bf16[512,512]{1,0:T(8,128)(2,1)S(1)}, bf16[512,512]{1,0:T(8,128)(2,1)}, u32[]{:S(2)}, u32[]{:S(2)}) collective-permute-start(bf16[512,512]{1,0:T(8,128)(2,1)S(1)} %pad_maximum_fusion.1.refs_0_), channel_id=1, source_target_pairs={{0,16},{1,17},{2,18},{3,19},{4,20},{5,21},{6,22},{7,23},{8,24},{9,... | collective-permute-start | bytes 1572872 | tf_op jit(solution)/shard_map/ppermute | solution.py:61
  20.7 11.9 %collective-permute-start.5 = (bf16[512,512]{1,0:T(8,128)(2,1)S(1)}, bf16[512,512]{1,0:T(8,128)(2,1)}, u32[]{:S(2)}, u32[]{:S(2)}) collective-permute-start(bf16[512,512]{1,0:T(8,128)(2,1)S(1)} %pad_maximum_fusion.1.refs_0_), channel_id=1, source_target_pairs={{0,8},{1,9},{2,10},{3,11},{4,12},{5,13},{6,14},{7,15},{8,0},{9,1},... | collective-permute-start | bytes 1572872 | tf_op jit(solution)/shard_map/ppermute | solution.py:61
  21.4 11.2 %collective-permute-start.4 = (bf16[272,512]{1,0:T(8,128)(2,1)}, bf16[272,512]{1,0:T(8,128)(2,1)S(1)}, u32[]{:S(2)}, u32[]{:S(2)}) collective-permute-start(bf16[272,512]{1,0:T(8,128)(2,1)} %fusion.1), channel_id=1, source_target_pairs={{0,0},{1,1},{2,2},{3,3},{4,32},{5,33},{6,34},{7,35},{8,8},{9,9},{1... | collective-permute-start | bytes 835592 | tf_op jit(solution)/shard_map/ppermute | solution.py:61
  24.2 9.4 %collective-permute-start.8 = (bf16[512,512]{1,0:T(8,128)(2,1)S(1)}, bf16[512,512]{1,0:T(8,128)(2,1)}, u32[]{:S(2)}, u32[]{:S(2)}) collective-permute-start(bf16[512,512]{1,0:T(8,128)(2,1)S(1)} %pad_maximum_fusion.1.refs_0_), channel_id=1, source_target_pairs={{0,32},{1,33},{2,34},{3,35},{4,36},{5,37},{6,38},{7,39},{8,40},{9,... | collective-permute-start | bytes 1572872 | tf_op jit(solution)/shard_map/ppermute | solution.py:61
  31.9 3.0 %collective-permute-start.10 = (bf16[512,512]{1,0:T(8,128)(2,1)}, bf16[512,512]{1,0:T(8,128)(2,1)}, u32[]{:S(2)}, u32[]{:S(2)}) collective-permute-start(bf16[512,512]{1,0:T(8,128)(2,1)} %collective-permute-done.6.refs_2_), channel_id=1, source_target_pairs={{0,32},{1,33},{2,34},{3,35},{4,36},{5,37},{6,38},{7,39},{8,40},{9,... | collective-permute-start | bytes 1572872 | tf_op jit(solution)/shard_map/ppermute | solution.py:61
  32.6 3.0 %collective-permute-start.9 = (bf16[512,512]{1,0:T(8,128)(2,1)}, bf16[512,512]{1,0:T(8,128)(2,1)}, u32[]{:S(2)}, u32[]{:S(2)}) collective-permute-start(bf16[512,512]{1,0:T(8,128)(2,1)} %collective-permute-done.5.refs_1_), channel_id=1, source_target_pairs={{0,32},{1,33},{2,34},{3,35},{4,36},{5,37},{6,38},{7,39},{8,40},{9,... | collective-permute-start | bytes 1572872 | tf_op jit(solution)/shard_map/ppermute | solution.py:61
  58.3 3.4 %collective-permute-start.17 = (bf16[512,512]{1,0:T(8,128)(2,1)S(1)}, bf16[512,512]{1,0:T(8,128)(2,1)S(1)}, u32[]{:S(2)}, u32[]{:S(2)}) collective-permute-start(bf16[512,512]{1,0:T(8,128)(2,1)S(1)} %get-tuple-element.61), channel_id=1, source_target_pairs={{0,32},{1,33},{2,34},{3,35},{4,36},{5,37},{6,38},{7,39},{8,40},{9,... | collective-permute-start | bytes 1572872 | tf_op jit(solution)/shard_map/ppermute | solution.py:61
  59.9 11.3 %collective-permute-start.16 = (bf16[528,512]{1,0:T(8,128)(2,1)S(1)}, bf16[528,512]{1,0:T(8,128)(2,1)S(1)}, u32[]{:S(2)}, u32[]{:S(2)}) collective-permute-start(bf16[528,512]{1,0:T(8,128)(2,1)S(1)} %get-tuple-element.59), channel_id=1, source_target_pairs={{0,2},{1,3},{2,0},{3,1},{4,6},{5,7},{6,4},{7,5},{8,10},{9,11},{10,... | collective-permute-start | bytes 1622024 | tf_op jit(solution)/shard_map/ppermute | solution.py:61
  60.6 13.3 %collective-permute-start.15 = (bf16[528,512]{1,0:T(8,128)(2,1)S(1)}, bf16[528,512]{1,0:T(8,128)(2,1)S(1)}, u32[]{:S(2)}, u32[]{:S(2)}) collective-permute-start(bf16[528,512]{1,0:T(8,128)(2,1)S(1)} %shard_map.216), channel_id=1, source_target_pairs={{0,1},{1,0},{2,3},{3,2},{4,5},{5,4},{6,7},{7,6},{8,9},{9,8},{10,11... | collective-permute-start | bytes 1622024 | tf_op jit(solution)/shard_map/ppermute | solution.py:61
  61.9 13.9 %collective-permute-start.18 = (bf16[528,512]{1,0:T(8,128)(2,1)S(1)}, bf16[528,512]{1,0:T(8,128)(2,1)S(1)}, u32[]{:S(2)}, u32[]{:S(2)}) collective-permute-start(bf16[528,512]{1,0:T(8,128)(2,1)S(1)} %shard_map.217), channel_id=1, source_target_pairs={{0,3},{1,2},{2,1},{3,0},{4,7},{5,6},{6,5},{7,4},{8,11},{9,10},{10,... | collective-permute-start | bytes 1622024 | tf_op jit(solution)/shard_map/ppermute | solution.py:61
  63.8 11.9 %collective-permute-start.19 = (bf16[512,512]{1,0:T(8,128)(2,1)S(1)}, bf16[512,512]{1,0:T(8,128)(2,1)S(1)}, u32[]{:S(2)}, u32[]{:S(2)}) collective-permute-start(bf16[512,512]{1,0:T(8,128)(2,1)S(1)} %get-tuple-element.64), channel_id=1, source_target_pairs={{0,32},{1,33},{2,34},{3,35},{4,36},{5,37},{6,38},{7,39},{8,40},{9,... | collective-permute-start | bytes 1572872 | tf_op jit(solution)/shard_map/ppermute | solution.py:61
  64.6 6.6 %collective-permute-start.12 = (bf16[128,512]{1,0:T(8,128)(2,1)S(1)}, bf16[128,512]{1,0:T(8,128)(2,1)S(1)}, u32[]{:S(2)}, u32[]{:S(2)}) collective-permute-start(bf16[128,512]{1,0:T(8,128)(2,1)S(1)} %get-tuple-element.52), channel_id=1, source_target_pairs={{0,0},{1,1},{2,2},{3,3},{4,32},{5,33},{6,34},{7,35},{8,8},{9,9},{1... | collective-permute-start | bytes 393224 | tf_op jit(solution)/shard_map/ppermute | solution.py:61
  76.6 4.4 %collective-permute-start.20 = (bf16[144,512]{1,0:T(8,128)(2,1)S(1)}, bf16[144,512]{1,0:T(8,128)(2,1)S(1)}, u32[]{:S(2)}, u32[]{:S(2)}) collective-permute-start(bf16[144,512]{1,0:T(8,128)(2,1)S(1)} %get-tuple-element.70), channel_id=1, source_target_pairs={{0,8},{1,9},{2,10},{3,11},{4,12},{5,13},{6,14},{7,15},{8,0},{9,1},... | collective-permute-start | bytes 442376 | tf_op jit(solution)/shard_map/ppermute | solution.py:61
  77.6 5.6 %collective-permute-start.21 = (bf16[144,512]{1,0:T(8,128)(2,1)S(1)}, bf16[144,512]{1,0:T(8,128)(2,1)S(1)}, u32[]{:S(2)}, u32[]{:S(2)}) collective-permute-start(bf16[144,512]{1,0:T(8,128)(2,1)S(1)} %get-tuple-element.71), channel_id=1, source_target_pairs={{0,16},{1,17},{2,18},{3,19},{4,20},{5,21},{6,22},{7,23},{8,24},{9,... | collective-permute-start | bytes 442376 | tf_op jit(solution)/shard_map/ppermute | solution.py:61
  78.7 6.2 %collective-permute-start.22 = (bf16[144,512]{1,0:T(8,128)(2,1)S(1)}, bf16[144,512]{1,0:T(8,128)(2,1)S(1)}, u32[]{:S(2)}, u32[]{:S(2)}) collective-permute-start(bf16[144,512]{1,0:T(8,128)(2,1)S(1)} %get-tuple-element.72), channel_id=1, source_target_pairs={{0,24},{1,25},{2,26},{3,27},{4,28},{5,29},{6,30},{7,31},{8,16},{9,... | collective-permute-start | bytes 442376 | tf_op jit(solution)/shard_map/ppermute | solution.py:61
  85.0 6.4 %collective-permute-start.25 = (bf16[144,512]{1,0:T(8,128)(2,1)S(1)}, bf16[144,512]{1,0:T(8,128)(2,1)S(1)}, u32[]{:S(2)}, u32[]{:S(2)}) collective-permute-start(bf16[144,512]{1,0:T(8,128)(2,1)S(1)} %shard_map.219.own_ref), channel_id=1, source_target_pairs={{0,68},{1,69},{2,70},{3,71},{4,64},{5,65},{6,66},{7,67},{8,76},{9,... | collective-permute-start | bytes 442376 | tf_op jit(solution)/shard_map/ppermute | solution.py:61
  87.7 5.6 %collective-permute-start.24 = (bf16[144,512]{1,0:T(8,128)(2,1)S(1)}, bf16[144,512]{1,0:T(8,128)(2,1)S(1)}, u32[]{:S(2)}, u32[]{:S(2)}) collective-permute-start(bf16[144,512]{1,0:T(8,128)(2,1)S(1)} %shard_map.219.own_ref), channel_id=1, source_target_pairs={{0,64},{1,65},{2,66},{3,67},{4,68},{5,69},{6,70},{7,71},{8,72},{9,... | collective-permute-start | bytes 442376 | tf_op jit(solution)/shard_map/ppermute | solution.py:61
  88.3 5.1 %collective-permute-start.23 = (bf16[144,512]{1,0:T(8,128)(2,1)S(1)}, bf16[144,512]{1,0:T(8,128)(2,1)S(1)}, u32[]{:S(2)}, u32[]{:S(2)}) collective-permute-start(bf16[144,512]{1,0:T(8,128)(2,1)S(1)} %shard_map.219.own_ref), channel_id=1, source_target_pairs={{0,4},{1,5},{2,6},{3,7},{4,0},{5,1},{6,2},{7,3},{8,12},{9,13},{10,... | collective-permute-start | bytes 442376 | tf_op jit(solution)/shard_map/ppermute | solution.py:61
  93.4 5.1 %collective-permute-start.28 = (bf16[128,512]{1,0:T(8,128)(2,1)S(1)}, bf16[128,512]{1,0:T(8,128)(2,1)S(1)}, u32[]{:S(2)}, u32[]{:S(2)}) collective-permute-start(bf16[128,512]{1,0:T(8,128)(2,1)S(1)} %get-tuple-element.74.refs_0_), channel_id=1, source_target_pairs={{0,24},{1,25},{2,26},{3,27},{4,28},{5,29},{6,30},{7,31},{8,16},{9,... | collective-permute-start | bytes 393224 | tf_op jit(solution)/shard_map/ppermute | solution.py:61
  95.3 5.3 %collective-permute-start.27 = (bf16[128,512]{1,0:T(8,128)(2,1)S(1)}, bf16[128,512]{1,0:T(8,128)(2,1)S(1)}, u32[]{:S(2)}, u32[]{:S(2)}) collective-permute-start(bf16[128,512]{1,0:T(8,128)(2,1)S(1)} %get-tuple-element.74.refs_0_), channel_id=1, source_target_pairs={{0,16},{1,17},{2,18},{3,19},{4,20},{5,21},{6,22},{7,23},{8,24},{9,... | collective-permute-start | bytes 393224 | tf_op jit(solution)/shard_map/ppermute | solution.py:61
  95.3 5.3 %collective-permute-start.26 = (bf16[128,512]{1,0:T(8,128)(2,1)S(1)}, bf16[128,512]{1,0:T(8,128)(2,1)S(1)}, u32[]{:S(2)}, u32[]{:S(2)}) collective-permute-start(bf16[128,512]{1,0:T(8,128)(2,1)S(1)} %get-tuple-element.74.refs_0_), channel_id=1, source_target_pairs={{0,8},{1,9},{2,10},{3,11},{4,12},{5,13},{6,14},{7,15},{8,0},{9,1},... | collective-permute-start | bytes 393224 | tf_op jit(solution)/shard_map/ppermute | solution.py:61
  101.2 15.6 %collective-permute-start.31 = (bf16[528,512]{1,0:T(8,128)(2,1)S(1)}, bf16[528,512]{1,0:T(8,128)(2,1)S(1)}, u32[]{:S(2)}, u32[]{:S(2)}) collective-permute-start(bf16[528,512]{1,0:T(8,128)(2,1)S(1)} %shard_map.221.refs_0_), channel_id=1, source_target_pairs={{0,3},{1,2},{2,1},{3,0},{4,7},{5,6},{6,5},{7,4},{8,11},{9,10},{10,... | collective-permute-start | bytes 1622024 | tf_op jit(solution)/shard_map/ppermute | solution.py:61
  102.5 20.6 %collective-permute-start.30 = (bf16[528,512]{1,0:T(8,128)(2,1)S(1)}, bf16[528,512]{1,0:T(8,128)(2,1)S(1)}, u32[]{:S(2)}, u32[]{:S(2)}) collective-permute-start(bf16[528,512]{1,0:T(8,128)(2,1)S(1)} %shard_map.221.refs_0_), channel_id=1, source_target_pairs={{0,2},{1,3},{2,0},{3,1},{4,6},{5,7},{6,4},{7,5},{8,10},{9,11},{10,... | collective-permute-start | bytes 1622024 | tf_op jit(solution)/shard_map/ppermute | solution.py:61
  105.4 17.7 %collective-permute-start.29 = (bf16[528,512]{1,0:T(8,128)(2,1)S(1)}, bf16[528,512]{1,0:T(8,128)(2,1)S(1)}, u32[]{:S(2)}, u32[]{:S(2)}) collective-permute-start(bf16[528,512]{1,0:T(8,128)(2,1)S(1)} %shard_map.221.refs_0_), channel_id=1, source_target_pairs={{0,1},{1,0},{2,3},{3,2},{4,5},{5,4},{6,7},{7,6},{8,9},{9,8},{10,11... | collective-permute-start | bytes 1622024 | tf_op jit(solution)/shard_map/ppermute | solution.py:61
  105.4 18.6 %collective-permute-start.32 = (bf16[528,512]{1,0:T(8,128)(2,1)S(1)}, bf16[528,512]{1,0:T(8,128)(2,1)S(1)}, u32[]{:S(2)}, u32[]{:S(2)}) collective-permute-start(bf16[528,512]{1,0:T(8,128)(2,1)S(1)} %shard_map.221.refs_0_), channel_id=1, source_target_pairs={{0,32},{1,33},{2,34},{3,35},{4,36},{5,37},{6,38},{7,39},{8,40},{9,... | collective-permute-start | bytes 1622024 | tf_op jit(solution)/shard_map/ppermute | solution.py:61
  116.8 7.8 %collective-permute-start.35 = (bf16[528,512]{1,0:T(8,128)(2,1)S(1)}, bf16[528,512]{1,0:T(8,128)(2,1)S(1)}, u32[]{:S(2)}, u32[]{:S(2)}) collective-permute-start(bf16[528,512]{1,0:T(8,128)(2,1)S(1)} %collective-permute-done.31.refs_3_), channel_id=1, source_target_pairs={{0,32},{1,33},{2,34},{3,35},{4,36},{5,37},{6,38},{7,39},{8,40},{9,... | collective-permute-start | bytes 1622024 | tf_op jit(solution)/shard_map/ppermute | solution.py:61
  123.1 3.1 %collective-permute-start.33 = (bf16[528,512]{1,0:T(8,128)(2,1)S(1)}, bf16[528,512]{1,0:T(8,128)(2,1)S(1)}, u32[]{:S(2)}, u32[]{:S(2)}) collective-permute-start(bf16[528,512]{1,0:T(8,128)(2,1)S(1)} %collective-permute-done.29.refs_1_), channel_id=1, source_target_pairs={{0,32},{1,33},{2,34},{3,35},{4,36},{5,37},{6,38},{7,39},{8,40},{9,... | collective-permute-start | bytes 1622024 | tf_op jit(solution)/shard_map/ppermute | solution.py:61
  (8 other events, 34.8 us)

commit v7 on v6

--- a/solution.py
+++ b/solution.py
@@ -391,7 +391,9 @@
 
 
 def place_kernel(where, *refs):
-    groups, grads, gain_attn, gain_mlp = (refs[0:4], refs[4:8]), refs[8:14], refs[14], refs[15]
+    groups, refs = (refs[0:4], refs[4:8]), refs[8:]
+    output, output_out, grads, gain_attn, gain_mlp = refs[0], refs[1], refs[2:8], refs[8], refs[9]
+    output_out[0] = output[...]
     for side, group in enumerate(groups):
         holder = where[0] ^ side
         for mask, arranged in enumerate(group):
@@ -455,16 +457,19 @@
     other = {mask: send(own[mask], CORE) for mask in (0,) + ORDER}
     placed = call(
         place_kernel,
-        [((512, 512), b16)] * 4 + [((512, 1024), b16), ((1024, 512), b16)] + [((512,), b16)] * 2,
-        where, *(own[mask] for mask in range(4)), *(other[mask] for mask in range(4)), scalars=1,
-    )
-    return (output[None], *placed)
-
-
-def gather_features(own, others, weights):
+        [((1, BLK, 512), b16)]
+        + [((512, 512), b16)] * 4
+        + [((512, 1024), b16), ((1024, 512), b16)]
+        + [((512,), b16)] * 2,
+        where, *(own[mask] for mask in range(4)), *(other[mask] for mask in range(4)), output, scalars=1,
+    )
+    return tuple(placed)
+
+
+def gather_features(own, others, seen, weights):
     near = {mask: send(own, first_swapped(mask)) for mask in (0,) + ORDER}
     mine = jnp.concatenate([near[mask] for mask in range(4)])
-    mine, others, weights = lax.optimization_barrier((mine, others, weights))
+    mine, others, seen, weights = lax.optimization_barrier((mine, others, seen, weights))
     group = [mine, *to_peers(lambda mask: mine, second).values()]
     parts = group + [send(part, CORE) for part in group]
     core, y, z = (lax.axis_index(name) for name in ("core", "y", "z"))
@@ -472,6 +477,7 @@
     holder = core ^ side
     block_y = jnp.where(holder == 0, y ^ one, y ^ two)
     block_z = jnp.where(holder == 0, z ^ two, z ^ one)
+    others = jnp.concatenate([*others, jnp.pad(seen, ((0, 15), (0, 512 - seen.shape[-1])))])
     return parts, block_z * 8 + holder * 4 + block_y, send(others, SWAP), jnp.concatenate(weights)
 
 
@@ -489,10 +495,10 @@
     gain_attn,
     gain_mlp,
 ):
-    seen = jnp.pad(visible[0].astype(jnp.bfloat16), ((0, 15), (0, 512 - visible.shape[-1])))
     parts, blocks, moved, packed = gather_features(
         features[0],
-        jnp.concatenate([queries[0], cotangent[0], seen]),
+        (queries[0], cotangent[0]),
+        visible[0].astype(jnp.bfloat16),
         (w_query, w_key, w_value, w_out),
     )
     seen = jnp.take(moved[2 * BLK].astype(jnp.float32), blocks)

time: 130 us -> 129 us (level)
    unnamed x9 -> x8, local copies, waits for them, and re-layouts: 3.11 us -> 2.46 us
where the time goes in v7:
time: 129 us
  starting transfers between devices  54.9 us (43%)
  waiting for transfers between devices  41.2 us (32%)
  Pallas kernels  24.5 us (19%)
  other arithmetic  4.13 us (3%)
  local copies, waits for them, and re-layouts  3.41 us (3%)
    ppermute x36, starting transfers between devices, send(): return lax.ppermute(value, AXES, pairs)  54.9 us
    ppermute x36, waiting for transfers between devices, send(): return lax.ppermute(value, AXES, pairs)  41.2 us
    pallas_call x1, Pallas kernels, device_step(): pl.pallas_call(step_kernel, out_shape=[jax.ShapeDtypeStruct((BLK, 512), b...  19.6 us
    pallas_call x8, Pallas kernels, call(): pl.pallas_call(kernel, out_shape=[jax.ShapeDtypeStruct(shape, dtype) for...  4.89 us
  transfers between devices with their start and end apart: 36, of which 23 were waited for; matrix products, arithmetic and copies ran while one was open for 4% of the time, Pallas kernels for 0%

profile of v7, /device:TPU:1, one launch (start us, length us, event | category | flops | bytes accessed | tf_op | source)
XLA Modules:
  0.0 129.0 jit_solution(7161328745244619795)
XLA Ops:
  0.6 5.1 %collective-permute-start.3 = (bf16[128,512]{1,0:T(8,128)(2,1)}, bf16[128,512]{1,0:T(8,128)(2,1)S(1)}, u32[]{:S(2)}, u32[]{:S(2)}) collective-permute-start(bf16[128,512]{1,0:T(8,128)(2,1)} %bitcast.18), channel_id=1, source_target_pairs={{0,3},{1,2},{2,1},{3,0},{4,56},{5,57},{6,58},{7,59},{8,11},{9,10},... | collective-permute-start | bytes 393224 | tf_op jit(solution)/shard_map/ppermute | solution.py:61
  5.8 3.6 %collective-permute-start.2 = (bf16[128,512]{1,0:T(8,128)(2,1)}, bf16[128,512]{1,0:T(8,128)(2,1)S(1)}, u32[]{:S(2)}, u32[]{:S(2)}) collective-permute-start(bf16[128,512]{1,0:T(8,128)(2,1)} %bitcast.19), channel_id=1, source_target_pairs={{0,2},{1,3},{2,0},{3,1},{4,48},{5,49},{6,50},{7,51},{8,10},{9,11},... | collective-permute-start | bytes 393224 | tf_op jit(solution)/shard_map/ppermute | solution.py:61
  10.4 2.3 %collective-permute-start = (bf16[128,512]{1,0:T(8,128)(2,1)}, bf16[128,512]{1,0:T(8,128)(2,1)S(1)}, u32[]{:S(2)}, u32[]{:S(2)}) collective-permute-start(bf16[128,512]{1,0:T(8,128)(2,1)} %bitcast.21), channel_id=1, source_target_pairs={{0,0},{1,1},{2,2},{3,3},{4,32},{5,33},{6,34},{7,35},{8,8},{9,9},{1... | collective-permute-start | bytes 393224 | tf_op jit(solution)/shard_map/ppermute | solution.py:61
  14.1 1.4 %collective-permute-done.1 = bf16[128,512]{1,0:T(8,128)(2,1)S(1)} collective-permute-done((bf16[128,512]{1,0:T(8,128)(2,1)}, bf16[128,512]{1,0:T(8,128)(2,1)S(1)}, u32[]{:S(2)}, u32[]{:S(2)}) %collective-permute-start.1) | collective-permute-done | bytes 131104 | tf_op jit(solution)/shard_map/ppermute | solution.py:61
  15.5 1.3 %collective-permute-done = bf16[128,512]{1,0:T(8,128)(2,1)S(1)} collective-permute-done((bf16[128,512]{1,0:T(8,128)(2,1)}, bf16[128,512]{1,0:T(8,128)(2,1)S(1)}, u32[]{:S(2)}, u32[]{:S(2)}) %collective-permute-start) | collective-permute-done | bytes 131104 | tf_op jit(solution)/shard_map/ppermute | solution.py:61
  17.8 2.9 %collective-permute-start.6 = (bf16[512,512]{1,0:T(8,128)(2,1)S(1)}, bf16[512,512]{1,0:T(8,128)(2,1)}, u32[]{:S(2)}, u32[]{:S(2)}) collective-permute-start(bf16[512,512]{1,0:T(8,128)(2,1)S(1)} %pad_maximum_fusion.1.refs_0_), channel_id=1, source_target_pairs={{0,16},{1,17},{2,18},{3,19},{4,20},{5,21},{6,22},{7,23},{8,24},{9,... | collective-permute-start | bytes 1572872 | tf_op jit(solution)/shard_map/ppermute | solution.py:61
  21.7 2.7 %collective-permute-start.4 = (bf16[272,512]{1,0:T(8,128)(2,1)S(1)}, bf16[272,512]{1,0:T(8,128)(2,1)S(1)}, u32[]{:S(2)}, u32[]{:S(2)}) collective-permute-start(bf16[272,512]{1,0:T(8,128)(2,1)S(1)} %fusion.1), channel_id=1, source_target_pairs={{0,0},{1,1},{2,2},{3,3},{4,32},{5,33},{6,34},{7,35},{8,8},{9,9},{1... | collective-permute-start | bytes 835592 | tf_op jit(solution)/shard_map/ppermute | solution.py:61
  24.6 1.7 %pad_maximum_fusion.packed = bf16[2048,512]{1,0:T(8,128)(2,1)S(1)} fusion(bf16[512,512]{1,0:T(8,128)(2,1)} %param.22, bf16[512,512]{1,0:T(8,128)(2,1)} %param.21, bf16[512,512]{1,0:T(8,128)(2,1)} %param.20, bf16[512,512]{1,0:T(8,128)(2,1)} %param.19), kind=kLoop, calls=%fused_computation.1 | loop fusion | flops 8388608 | bytes 4194304 | tf_op jit(solution)/shard_map/concatenate | solution.py:481
  26.2 5.6 %collective-permute-done.7.refs_3_ = bf16[512,512]{1,0:T(8,128)(2,1)S(1)} collective-permute-done((bf16[512,512]{1,0:T(8,128)(2,1)S(1)}, bf16[512,512]{1,0:T(8,128)(2,1)S(1)}, u32[]{:S(2)}, u32[]{:S(2)}) %collective-permute-start.7) | collective-permute-done | bytes 524320 | tf_op jit(solution)/shard_map/ppermute | solution.py:61
  38.1 19.6 %shard_map.214 = (bf16[128,512]{1,0:T(8,128)(2,1)S(1)}, f32[8,512]{1,0:T(8,128)S(1)}, bf16[512,512]{1,0:T(8,128)(2,1)S(1)}, bf16[512,512]{1,0:T(8,128)(2,1)S(1)}...) custom-call(s32[3]{0:T(128)S(1)} %pad_add_fusion.where, ...), custom_call_target="tpu_custom_call" | custom-call | flops 12000000000 | bytes 18000000 | tf_op jit(solution)/shard_map/pallas_call | solution.py:286
  58.4 1.3 collective-permute-done.13.arrived
  61.8 2.0 %collective-permute-start.19 = (bf16[528,512]{1,0:T(8,128)(2,1)S(1)}, bf16[528,512]{1,0:T(8,128)(2,1)S(1)}, u32[]{:S(2)}, u32[]{:S(2)}) collective-permute-start(bf16[528,512]{1,0:T(8,128)(2,1)S(1)} %shard_map.217), channel_id=1, source_target_pairs={{0,3},{1,2},{2,1},{3,0},{4,7},{5,6},{6,5},{7,4},{8,11},{9,10},{10,... | collective-permute-start | bytes 1622024 | tf_op jit(solution)/shard_map/ppermute | solution.py:61
  64.6 3.4 %collective-permute-start.14 = (bf16[128,512]{1,0:T(8,128)(2,1)S(1)}, bf16[128,512]{1,0:T(8,128)(2,1)S(1)}, u32[]{:S(2)}, u32[]{:S(2)}) collective-permute-start(bf16[128,512]{1,0:T(8,128)(2,1)S(1)} %get-tuple-element.54), channel_id=1, source_target_pairs={{0,0},{1,1},{2,2},{3,3},{4,32},{5,33},{6,34},{7,35},{8,8},{9,9},{1... | collective-permute-start | bytes 393224 | tf_op jit(solution)/shard_map/ppermute | solution.py:61
  68.0 3.2 %collective-permute-done.14.refs_8_ = bf16[128,512]{1,0:T(8,128)(2,1)S(1)} collective-permute-done((bf16[128,512]{1,0:T(8,128)(2,1)S(1)}, bf16[128,512]{1,0:T(8,128)(2,1)S(1)}, u32[]{:S(2)}, u32[]{:S(2)}) %collective-permute-start.14) | collective-permute-done | bytes 131104 | tf_op jit(solution)/shard_map/ppermute | solution.py:61
  71.2 2.6 %collective-permute-done.16.refs_0_ = bf16[528,512]{1,0:T(8,128)(2,1)S(1)} collective-permute-done((bf16[528,512]{1,0:T(8,128)(2,1)S(1)}, bf16[528,512]{1,0:T(8,128)(2,1)S(1)}, u32[]{:S(2)}, u32[]{:S(2)}) %collective-permute-start.16) | collective-permute-done | bytes 540704 | tf_op jit(solution)/shard_map/ppermute | solution.py:61
  73.8 1.9 %collective-permute-done.19.refs_2_ = bf16[528,512]{1,0:T(8,128)(2,1)S(1)} collective-permute-done((bf16[528,512]{1,0:T(8,128)(2,1)S(1)}, bf16[528,512]{1,0:T(8,128)(2,1)S(1)}, u32[]{:S(2)}, u32[]{:S(2)}) %collective-permute-start.19) | collective-permute-done | bytes 540704 | tf_op jit(solution)/shard_map/ppermute | solution.py:61
  78.7 1.9 %collective-permute-start.22 = (bf16[144,512]{1,0:T(8,128)(2,1)S(1)}, bf16[144,512]{1,0:T(8,128)(2,1)S(1)}, u32[]{:S(2)}, u32[]{:S(2)}) collective-permute-start(bf16[144,512]{1,0:T(8,128)(2,1)S(1)} %get-tuple-element.67), channel_id=1, source_target_pairs={{0,24},{1,25},{2,26},{3,27},{4,28},{5,29},{6,30},{7,31},{8,16},{9,... | collective-permute-start | bytes 442376 | tf_op jit(solution)/shard_map/ppermute | solution.py:61
  81.0 2.1 %collective-permute-done.21.refs_1_ = bf16[144,512]{1,0:T(8,128)(2,1)S(1)} collective-permute-done((bf16[144,512]{1,0:T(8,128)(2,1)S(1)}, bf16[144,512]{1,0:T(8,128)(2,1)S(1)}, u32[]{:S(2)}, u32[]{:S(2)}) %collective-permute-start.21) | collective-permute-done | bytes 147488 | tf_op jit(solution)/shard_map/ppermute | solution.py:61
  83.1 1.8 %collective-permute-done.22.refs_2_ = bf16[144,512]{1,0:T(8,128)(2,1)S(1)} collective-permute-done((bf16[144,512]{1,0:T(8,128)(2,1)S(1)}, bf16[144,512]{1,0:T(8,128)(2,1)S(1)}, u32[]{:S(2)}, u32[]{:S(2)}) %collective-permute-start.22) | collective-permute-done | bytes 147488 | tf_op jit(solution)/shard_map/ppermute | solution.py:61
  85.0 2.7 %collective-permute-start.25 = (bf16[144,512]{1,0:T(8,128)(2,1)S(1)}, bf16[144,512]{1,0:T(8,128)(2,1)S(1)}, u32[]{:S(2)}, u32[]{:S(2)}) collective-permute-start(bf16[144,512]{1,0:T(8,128)(2,1)S(1)} %shard_map.219.own_ref), channel_id=1, source_target_pairs={{0,68},{1,69},{2,70},{3,71},{4,64},{5,65},{6,66},{7,67},{8,76},{9,... | collective-permute-start | bytes 442376 | tf_op jit(solution)/shard_map/ppermute | solution.py:61
  88.4 3.0 %collective-permute-done.25.refs_2_ = bf16[144,512]{1,0:T(8,128)(2,1)S(1)} collective-permute-done((bf16[144,512]{1,0:T(8,128)(2,1)S(1)}, bf16[144,512]{1,0:T(8,128)(2,1)S(1)}, u32[]{:S(2)}, u32[]{:S(2)}) %collective-permute-start.25) | collective-permute-done | bytes 147488 | tf_op jit(solution)/shard_map/ppermute | solution.py:61
  91.4 1.9 %collective-permute-done.24.refs_1_ = bf16[144,512]{1,0:T(8,128)(2,1)S(1)} collective-permute-done((bf16[144,512]{1,0:T(8,128)(2,1)S(1)}, bf16[144,512]{1,0:T(8,128)(2,1)S(1)}, u32[]{:S(2)}, u32[]{:S(2)}) %collective-permute-start.24) | collective-permute-done | bytes 147488 | tf_op jit(solution)/shard_map/ppermute | solution.py:61
  93.4 1.9 %collective-permute-start.28 = (bf16[128,512]{1,0:T(8,128)(2,1)S(1)}, bf16[128,512]{1,0:T(8,128)(2,1)S(1)}, u32[]{:S(2)}, u32[]{:S(2)}) collective-permute-start(bf16[128,512]{1,0:T(8,128)(2,1)S(1)} %get-tuple-element.69.refs_0_), channel_id=1, source_target_pairs={{0,24},{1,25},{2,26},{3,27},{4,28},{5,29},{6,30},{7,31},{8,16},{9,... | collective-permute-start | bytes 393224 | tf_op jit(solution)/shard_map/ppermute | solution.py:61
  95.3 1.5 %collective-permute-start.26 = (bf16[128,512]{1,0:T(8,128)(2,1)S(1)}, bf16[128,512]{1,0:T(8,128)(2,1)S(1)}, u32[]{:S(2)}, u32[]{:S(2)}) collective-permute-start(bf16[128,512]{1,0:T(8,128)(2,1)S(1)} %get-tuple-element.69.refs_0_), channel_id=1, source_target_pairs={{0,8},{1,9},{2,10},{3,11},{4,12},{5,13},{6,14},{7,15},{8,0},{9,1},... | collective-permute-start | bytes 393224 | tf_op jit(solution)/shard_map/ppermute | solution.py:61
  96.8 1.8 %collective-permute-done.28.refs_3_ = bf16[128,512]{1,0:T(8,128)(2,1)S(1)} collective-permute-done((bf16[128,512]{1,0:T(8,128)(2,1)S(1)}, bf16[128,512]{1,0:T(8,128)(2,1)S(1)}, u32[]{:S(2)}, u32[]{:S(2)}) %collective-permute-start.28) | collective-permute-done | bytes 131104 | tf_op jit(solution)/shard_map/ppermute | solution.py:61
  98.5 2.1 %collective-permute-done.27.refs_2_ = bf16[128,512]{1,0:T(8,128)(2,1)S(1)} collective-permute-done((bf16[128,512]{1,0:T(8,128)(2,1)S(1)}, bf16[128,512]{1,0:T(8,128)(2,1)S(1)}, u32[]{:S(2)}, u32[]{:S(2)}) %collective-permute-start.27) | collective-permute-done | bytes 131104 | tf_op jit(solution)/shard_map/ppermute | solution.py:61
  101.2 1.3 collective-permute-start.31
  102.5 2.9 %collective-permute-start.30 = (bf16[528,512]{1,0:T(8,128)(2,1)S(1)}, bf16[528,512]{1,0:T(8,128)(2,1)S(1)}, u32[]{:S(2)}, u32[]{:S(2)}) collective-permute-start(bf16[528,512]{1,0:T(8,128)(2,1)S(1)} %shard_map.221.refs_0_), channel_id=1, source_target_pairs={{0,2},{1,3},{2,0},{3,1},{4,6},{5,7},{6,4},{7,5},{8,10},{9,11},{10,... | collective-permute-start | bytes 1622024 | tf_op jit(solution)/shard_map/ppermute | solution.py:61
  105.4 5.4 %collective-permute-start.32 = (bf16[528,512]{1,0:T(8,128)(2,1)S(1)}, bf16[528,512]{1,0:T(8,128)(2,1)S(1)}, u32[]{:S(2)}, u32[]{:S(2)}) collective-permute-start(bf16[528,512]{1,0:T(8,128)(2,1)S(1)} %shard_map.221.refs_0_), channel_id=1, source_target_pairs={{0,32},{1,33},{2,34},{3,35},{4,36},{5,37},{6,38},{7,39},{8,40},{9,... | collective-permute-start | bytes 1622024 | tf_op jit(solution)/shard_map/ppermute | solution.py:61
  110.8 6.0 %collective-permute-done.31.refs_3_ = bf16[528,512]{1,0:T(8,128)(2,1)S(1)} collective-permute-done((bf16[528,512]{1,0:T(8,128)(2,1)S(1)}, bf16[528,512]{1,0:T(8,128)(2,1)S(1)}, u32[]{:S(2)}, u32[]{:S(2)}) %collective-permute-start.31) | collective-permute-done | bytes 540704 | tf_op jit(solution)/shard_map/ppermute | solution.py:61
  116.8 6.2 %collective-permute-start.35 = (bf16[528,512]{1,0:T(8,128)(2,1)S(1)}, bf16[528,512]{1,0:T(8,128)(2,1)S(1)}, u32[]{:S(2)}, u32[]{:S(2)}) collective-permute-start(bf16[528,512]{1,0:T(8,128)(2,1)S(1)} %collective-permute-done.31.refs_3_), channel_id=1, source_target_pairs={{0,32},{1,33},{2,34},{3,35},{4,36},{5,37},{6,38},{7,39},{8,40},{9,... | collective-permute-start | bytes 1622024 | tf_op jit(solution)/shard_map/ppermute | solution.py:61
  126.2 2.9 %shard_map.222 = (bf16[1,128,512]{2,1,0:T(8,128)(2,1)}, bf16[512,512]{1,0:T(8,128)(2,1)}, bf16[512,512]{1,0:T(8,128)(2,1)}, bf16[512,512]{1,0:T(8,128)(2,1)}, bf...) custom-call(s32[3]{0:T(128)S(1)} %pad_add_fusion.where, ...), custom_call_target="tpu_custom_call" | custom-call | tf_op jit(solution)/shard_map/pallas_call | solution.py:415
  (70 shorter events, 22.1 us)
Async XLA Ops:
  0.6 13.5 %collective-permute-start.3 = (bf16[128,512]{1,0:T(8,128)(2,1)}, bf16[128,512]{1,0:T(8,128)(2,1)S(1)}, u32[]{:S(2)}, u32[]{:S(2)}) collective-permute-start(bf16[128,512]{1,0:T(8,128)(2,1)} %bitcast.18), channel_id=1, source_target_pairs={{0,3},{1,2},{2,1},{3,0},{4,56},{5,57},{6,58},{7,59},{8,11},{9,10},... | collective-permute-start | bytes 393224 | tf_op jit(solution)/shard_map/ppermute | solution.py:61
  5.8 8.3 %collective-permute-start.2 = (bf16[128,512]{1,0:T(8,128)(2,1)}, bf16[128,512]{1,0:T(8,128)(2,1)S(1)}, u32[]{:S(2)}, u32[]{:S(2)}) collective-permute-start(bf16[128,512]{1,0:T(8,128)(2,1)} %bitcast.19), channel_id=1, source_target_pairs={{0,2},{1,3},{2,0},{3,1},{4,48},{5,49},{6,50},{7,51},{8,10},{9,11},... | collective-permute-start | bytes 393224 | tf_op jit(solution)/shard_map/ppermute | solution.py:61
  9.4 6.1 %collective-permute-start.1 = (bf16[128,512]{1,0:T(8,128)(2,1)}, bf16[128,512]{1,0:T(8,128)(2,1)S(1)}, u32[]{:S(2)}, u32[]{:S(2)}) collective-permute-start(bf16[128,512]{1,0:T(8,128)(2,1)} %bitcast.20), channel_id=1, source_target_pairs={{0,1},{1,0},{2,3},{3,2},{4,40},{5,41},{6,42},{7,43},{8,9},{9,8},{1... | collective-permute-start | bytes 393224 | tf_op jit(solution)/shard_map/ppermute | solution.py:61
  10.4 6.5 %collective-permute-start = (bf16[128,512]{1,0:T(8,128)(2,1)}, bf16[128,512]{1,0:T(8,128)(2,1)S(1)}, u32[]{:S(2)}, u32[]{:S(2)}) collective-permute-start(bf16[128,512]{1,0:T(8,128)(2,1)} %bitcast.21), channel_id=1, source_target_pairs={{0,0},{1,1},{2,2},{3,3},{4,32},{5,33},{6,34},{7,35},{8,8},{9,9},{1... | collective-permute-start | bytes 393224 | tf_op jit(solution)/shard_map/ppermute | solution.py:61
  16.9 14.9 %collective-permute-start.7 = (bf16[512,512]{1,0:T(8,128)(2,1)S(1)}, bf16[512,512]{1,0:T(8,128)(2,1)S(1)}, u32[]{:S(2)}, u32[]{:S(2)}) collective-permute-start(bf16[512,512]{1,0:T(8,128)(2,1)S(1)} %pad_maximum_fusion.1.refs_0_), channel_id=1, source_target_pairs={{0,24},{1,25},{2,26},{3,27},{4,28},{5,29},{6,30},{7,31},{8,16},{9,... | collective-permute-start | bytes 1572872 | tf_op jit(solution)/shard_map/ppermute | solution.py:61
  17.8 14.1 %collective-permute-start.6 = (bf16[512,512]{1,0:T(8,128)(2,1)S(1)}, bf16[512,512]{1,0:T(8,128)(2,1)}, u32[]{:S(2)}, u32[]{:S(2)}) collective-permute-start(bf16[512,512]{1,0:T(8,128)(2,1)S(1)} %pad_maximum_fusion.1.refs_0_), channel_id=1, source_target_pairs={{0,16},{1,17},{2,18},{3,19},{4,20},{5,21},{6,22},{7,23},{8,24},{9,... | collective-permute-start | bytes 1572872 | tf_op jit(solution)/shard_map/ppermute | solution.py:61
  20.7 11.9 %collective-permute-start.5 = (bf16[512,512]{1,0:T(8,128)(2,1)S(1)}, bf16[512,512]{1,0:T(8,128)(2,1)}, u32[]{:S(2)}, u32[]{:S(2)}) collective-permute-start(bf16[512,512]{1,0:T(8,128)(2,1)S(1)} %pad_maximum_fusion.1.refs_0_), channel_id=1, source_target_pairs={{0,8},{1,9},{2,10},{3,11},{4,12},{5,13},{6,14},{7,15},{8,0},{9,1},... | collective-permute-start | bytes 1572872 | tf_op jit(solution)/shard_map/ppermute | solution.py:61
  21.7 10.9 %collective-permute-start.4 = (bf16[272,512]{1,0:T(8,128)(2,1)S(1)}, bf16[272,512]{1,0:T(8,128)(2,1)S(1)}, u32[]{:S(2)}, u32[]{:S(2)}) collective-permute-start(bf16[272,512]{1,0:T(8,128)(2,1)S(1)} %fusion.1), channel_id=1, source_target_pairs={{0,0},{1,1},{2,2},{3,3},{4,32},{5,33},{6,34},{7,35},{8,8},{9,9},{1... | collective-permute-start | bytes 835592 | tf_op jit(solution)/shard_map/ppermute | solution.py:61
  24.5 9.1 %collective-permute-start.8 = (bf16[512,512]{1,0:T(8,128)(2,1)S(1)}, bf16[512,512]{1,0:T(8,128)(2,1)}, u32[]{:S(2)}, u32[]{:S(2)}) collective-permute-start(bf16[512,512]{1,0:T(8,128)(2,1)S(1)} %pad_maximum_fusion.1.refs_0_), channel_id=1, source_target_pairs={{0,32},{1,33},{2,34},{3,35},{4,36},{5,37},{6,38},{7,39},{8,40},{9,... | collective-permute-start | bytes 1572872 | tf_op jit(solution)/shard_map/ppermute | solution.py:61
  31.9 3.0 %collective-permute-start.10 = (bf16[512,512]{1,0:T(8,128)(2,1)}, bf16[512,512]{1,0:T(8,128)(2,1)}, u32[]{:S(2)}, u32[]{:S(2)}) collective-permute-start(bf16[512,512]{1,0:T(8,128)(2,1)} %collective-permute-done.6.refs_2_), channel_id=1, source_target_pairs={{0,32},{1,33},{2,34},{3,35},{4,36},{5,37},{6,38},{7,39},{8,40},{9,... | collective-permute-start | bytes 1572872 | tf_op jit(solution)/shard_map/ppermute | solution.py:61
  32.6 3.0 %collective-permute-start.9 = (bf16[512,512]{1,0:T(8,128)(2,1)}, bf16[512,512]{1,0:T(8,128)(2,1)}, u32[]{:S(2)}, u32[]{:S(2)}) collective-permute-start(bf16[512,512]{1,0:T(8,128)(2,1)} %collective-permute-done.5.refs_1_), channel_id=1, source_target_pairs={{0,32},{1,33},{2,34},{3,35},{4,36},{5,37},{6,38},{7,39},{8,40},{9,... | collective-permute-start | bytes 1572872 | tf_op jit(solution)/shard_map/ppermute | solution.py:61
  58.3 3.4 %collective-permute-start.18 = (bf16[512,512]{1,0:T(8,128)(2,1)S(1)}, bf16[512,512]{1,0:T(8,128)(2,1)S(1)}, u32[]{:S(2)}, u32[]{:S(2)}) collective-permute-start(bf16[512,512]{1,0:T(8,128)(2,1)S(1)} %get-tuple-element.59), channel_id=1, source_target_pairs={{0,32},{1,33},{2,34},{3,35},{4,36},{5,37},{6,38},{7,39},{8,40},{9,... | collective-permute-start | bytes 1572872 | tf_op jit(solution)/shard_map/ppermute | solution.py:61
  59.9 11.3 %collective-permute-start.17 = (bf16[528,512]{1,0:T(8,128)(2,1)S(1)}, bf16[528,512]{1,0:T(8,128)(2,1)S(1)}, u32[]{:S(2)}, u32[]{:S(2)}) collective-permute-start(bf16[528,512]{1,0:T(8,128)(2,1)S(1)} %get-tuple-element.57), channel_id=1, source_target_pairs={{0,2},{1,3},{2,0},{3,1},{4,6},{5,7},{6,4},{7,5},{8,10},{9,11},{10,... | collective-permute-start | bytes 1622024 | tf_op jit(solution)/shard_map/ppermute | solution.py:61
  60.6 13.2 %collective-permute-start.16 = (bf16[528,512]{1,0:T(8,128)(2,1)S(1)}, bf16[528,512]{1,0:T(8,128)(2,1)S(1)}, u32[]{:S(2)}, u32[]{:S(2)}) collective-permute-start(bf16[528,512]{1,0:T(8,128)(2,1)S(1)} %shard_map.216), channel_id=1, source_target_pairs={{0,1},{1,0},{2,3},{3,2},{4,5},{5,4},{6,7},{7,6},{8,9},{9,8},{10,11... | collective-permute-start | bytes 1622024 | tf_op jit(solution)/shard_map/ppermute | solution.py:61
  61.8 13.9 %collective-permute-start.19 = (bf16[528,512]{1,0:T(8,128)(2,1)S(1)}, bf16[528,512]{1,0:T(8,128)(2,1)S(1)}, u32[]{:S(2)}, u32[]{:S(2)}) collective-permute-start(bf16[528,512]{1,0:T(8,128)(2,1)S(1)} %shard_map.217), channel_id=1, source_target_pairs={{0,3},{1,2},{2,1},{3,0},{4,7},{5,6},{6,5},{7,4},{8,11},{9,10},{10,... | collective-permute-start | bytes 1622024 | tf_op jit(solution)/shard_map/ppermute | solution.py:61
  63.8 11.9 %collective-permute-start.12 = (bf16[512,512]{1,0:T(8,128)(2,1)S(1)}, bf16[512,512]{1,0:T(8,128)(2,1)S(1)}, u32[]{:S(2)}, u32[]{:S(2)}) collective-permute-start(bf16[512,512]{1,0:T(8,128)(2,1)S(1)} %get-tuple-element.49), channel_id=1, source_target_pairs={{0,32},{1,33},{2,34},{3,35},{4,36},{5,37},{6,38},{7,39},{8,40},{9,... | collective-permute-start | bytes 1572872 | tf_op jit(solution)/shard_map/ppermute | solution.py:61
  64.6 6.6 %collective-permute-start.14 = (bf16[128,512]{1,0:T(8,128)(2,1)S(1)}, bf16[128,512]{1,0:T(8,128)(2,1)S(1)}, u32[]{:S(2)}, u32[]{:S(2)}) collective-permute-start(bf16[128,512]{1,0:T(8,128)(2,1)S(1)} %get-tuple-element.54), channel_id=1, source_target_pairs={{0,0},{1,1},{2,2},{3,3},{4,32},{5,33},{6,34},{7,35},{8,8},{9,9},{1... | collective-permute-start | bytes 393224 | tf_op jit(solution)/shard_map/ppermute | solution.py:61
  76.6 4.4 %collective-permute-start.20 = (bf16[144,512]{1,0:T(8,128)(2,1)S(1)}, bf16[144,512]{1,0:T(8,128)(2,1)S(1)}, u32[]{:S(2)}, u32[]{:S(2)}) collective-permute-start(bf16[144,512]{1,0:T(8,128)(2,1)S(1)} %get-tuple-element.65), channel_id=1, source_target_pairs={{0,8},{1,9},{2,10},{3,11},{4,12},{5,13},{6,14},{7,15},{8,0},{9,1},... | collective-permute-start | bytes 442376 | tf_op jit(solution)/shard_map/ppermute | solution.py:61
  77.6 5.6 %collective-permute-start.21 = (bf16[144,512]{1,0:T(8,128)(2,1)S(1)}, bf16[144,512]{1,0:T(8,128)(2,1)S(1)}, u32[]{:S(2)}, u32[]{:S(2)}) collective-permute-start(bf16[144,512]{1,0:T(8,128)(2,1)S(1)} %get-tuple-element.66), channel_id=1, source_target_pairs={{0,16},{1,17},{2,18},{3,19},{4,20},{5,21},{6,22},{7,23},{8,24},{9,... | collective-permute-start | bytes 442376 | tf_op jit(solution)/shard_map/ppermute | solution.py:61
  78.7 6.2 %collective-permute-start.22 = (bf16[144,512]{1,0:T(8,128)(2,1)S(1)}, bf16[144,512]{1,0:T(8,128)(2,1)S(1)}, u32[]{:S(2)}, u32[]{:S(2)}) collective-permute-start(bf16[144,512]{1,0:T(8,128)(2,1)S(1)} %get-tuple-element.67), channel_id=1, source_target_pairs={{0,24},{1,25},{2,26},{3,27},{4,28},{5,29},{6,30},{7,31},{8,16},{9,... | collective-permute-start | bytes 442376 | tf_op jit(solution)/shard_map/ppermute | solution.py:61
  85.0 6.4 %collective-permute-start.25 = (bf16[144,512]{1,0:T(8,128)(2,1)S(1)}, bf16[144,512]{1,0:T(8,128)(2,1)S(1)}, u32[]{:S(2)}, u32[]{:S(2)}) collective-permute-start(bf16[144,512]{1,0:T(8,128)(2,1)S(1)} %shard_map.219.own_ref), channel_id=1, source_target_pairs={{0,68},{1,69},{2,70},{3,71},{4,64},{5,65},{6,66},{7,67},{8,76},{9,... | collective-permute-start | bytes 442376 | tf_op jit(solution)/shard_map/ppermute | solution.py:61
  87.7 5.6 %collective-permute-start.24 = (bf16[144,512]{1,0:T(8,128)(2,1)S(1)}, bf16[144,512]{1,0:T(8,128)(2,1)S(1)}, u32[]{:S(2)}, u32[]{:S(2)}) collective-permute-start(bf16[144,512]{1,0:T(8,128)(2,1)S(1)} %shard_map.219.own_ref), channel_id=1, source_target_pairs={{0,64},{1,65},{2,66},{3,67},{4,68},{5,69},{6,70},{7,71},{8,72},{9,... | collective-permute-start | bytes 442376 | tf_op jit(solution)/shard_map/ppermute | solution.py:61
  88.3 5.1 %collective-permute-start.23 = (bf16[144,512]{1,0:T(8,128)(2,1)S(1)}, bf16[144,512]{1,0:T(8,128)(2,1)S(1)}, u32[]{:S(2)}, u32[]{:S(2)}) collective-permute-start(bf16[144,512]{1,0:T(8,128)(2,1)S(1)} %shard_map.219.own_ref), channel_id=1, source_target_pairs={{0,4},{1,5},{2,6},{3,7},{4,0},{5,1},{6,2},{7,3},{8,12},{9,13},{10,... | collective-permute-start | bytes 442376 | tf_op jit(solution)/shard_map/ppermute | solution.py:61
  93.4 5.1 %collective-permute-start.28 = (bf16[128,512]{1,0:T(8,128)(2,1)S(1)}, bf16[128,512]{1,0:T(8,128)(2,1)S(1)}, u32[]{:S(2)}, u32[]{:S(2)}) collective-permute-start(bf16[128,512]{1,0:T(8,128)(2,1)S(1)} %get-tuple-element.69.refs_0_), channel_id=1, source_target_pairs={{0,24},{1,25},{2,26},{3,27},{4,28},{5,29},{6,30},{7,31},{8,16},{9,... | collective-permute-start | bytes 393224 | tf_op jit(solution)/shard_map/ppermute | solution.py:61
  95.3 5.3 %collective-permute-start.27 = (bf16[128,512]{1,0:T(8,128)(2,1)S(1)}, bf16[128,512]{1,0:T(8,128)(2,1)S(1)}, u32[]{:S(2)}, u32[]{:S(2)}) collective-permute-start(bf16[128,512]{1,0:T(8,128)(2,1)S(1)} %get-tuple-element.69.refs_0_), channel_id=1, source_target_pairs={{0,16},{1,17},{2,18},{3,19},{4,20},{5,21},{6,22},{7,23},{8,24},{9,... | collective-permute-start | bytes 393224 | tf_op jit(solution)/shard_map/ppermute | solution.py:61
  95.3 5.3 %collective-permute-start.26 = (bf16[128,512]{1,0:T(8,128)(2,1)S(1)}, bf16[128,512]{1,0:T(8,128)(2,1)S(1)}, u32[]{:S(2)}, u32[]{:S(2)}) collective-permute-start(bf16[128,512]{1,0:T(8,128)(2,1)S(1)} %get-tuple-element.69.refs_0_), channel_id=1, source_target_pairs={{0,8},{1,9},{2,10},{3,11},{4,12},{5,13},{6,14},{7,15},{8,0},{9,1},... | collective-permute-start | bytes 393224 | tf_op jit(solution)/shard_map/ppermute | solution.py:61
  101.2 15.6 %collective-permute-start.31 = (bf16[528,512]{1,0:T(8,128)(2,1)S(1)}, bf16[528,512]{1,0:T(8,128)(2,1)S(1)}, u32[]{:S(2)}, u32[]{:S(2)}) collective-permute-start(bf16[528,512]{1,0:T(8,128)(2,1)S(1)} %shard_map.221.refs_0_), channel_id=1, source_target_pairs={{0,3},{1,2},{2,1},{3,0},{4,7},{5,6},{6,5},{7,4},{8,11},{9,10},{10,... | collective-permute-start | bytes 1622024 | tf_op jit(solution)/shard_map/ppermute | solution.py:61
  102.5 20.5 %collective-permute-start.30 = (bf16[528,512]{1,0:T(8,128)(2,1)S(1)}, bf16[528,512]{1,0:T(8,128)(2,1)S(1)}, u32[]{:S(2)}, u32[]{:S(2)}) collective-permute-start(bf16[528,512]{1,0:T(8,128)(2,1)S(1)} %shard_map.221.refs_0_), channel_id=1, source_target_pairs={{0,2},{1,3},{2,0},{3,1},{4,6},{5,7},{6,4},{7,5},{8,10},{9,11},{10,... | collective-permute-start | bytes 1622024 | tf_op jit(solution)/shard_map/ppermute | solution.py:61
  105.4 17.7 %collective-permute-start.29 = (bf16[528,512]{1,0:T(8,128)(2,1)S(1)}, bf16[528,512]{1,0:T(8,128)(2,1)S(1)}, u32[]{:S(2)}, u32[]{:S(2)}) collective-permute-start(bf16[528,512]{1,0:T(8,128)(2,1)S(1)} %shard_map.221.refs_0_), channel_id=1, source_target_pairs={{0,1},{1,0},{2,3},{3,2},{4,5},{5,4},{6,7},{7,6},{8,9},{9,8},{10,11... | collective-permute-start | bytes 1622024 | tf_op jit(solution)/shard_map/ppermute | solution.py:61
  105.4 18.6 %collective-permute-start.32 = (bf16[528,512]{1,0:T(8,128)(2,1)S(1)}, bf16[528,512]{1,0:T(8,128)(2,1)S(1)}, u32[]{:S(2)}, u32[]{:S(2)}) collective-permute-start(bf16[528,512]{1,0:T(8,128)(2,1)S(1)} %shard_map.221.refs_0_), channel_id=1, source_target_pairs={{0,32},{1,33},{2,34},{3,35},{4,36},{5,37},{6,38},{7,39},{8,40},{9,... | collective-permute-start | bytes 1622024 | tf_op jit(solution)/shard_map/ppermute | solution.py:61
  116.8 7.8 %collective-permute-start.35 = (bf16[528,512]{1,0:T(8,128)(2,1)S(1)}, bf16[528,512]{1,0:T(8,128)(2,1)S(1)}, u32[]{:S(2)}, u32[]{:S(2)}) collective-permute-start(bf16[528,512]{1,0:T(8,128)(2,1)S(1)} %collective-permute-done.31.refs_3_), channel_id=1, source_target_pairs={{0,32},{1,33},{2,34},{3,35},{4,36},{5,37},{6,38},{7,39},{8,40},{9,... | collective-permute-start | bytes 1622024 | tf_op jit(solution)/shard_map/ppermute | solution.py:61
  123.1 3.1 %collective-permute-start.33 = (bf16[528,512]{1,0:T(8,128)(2,1)S(1)}, bf16[528,512]{1,0:T(8,128)(2,1)S(1)}, u32[]{:S(2)}, u32[]{:S(2)}) collective-permute-start(bf16[528,512]{1,0:T(8,128)(2,1)S(1)} %collective-permute-done.29.refs_1_), channel_id=1, source_target_pairs={{0,32},{1,33},{2,34},{3,35},{4,36},{5,37},{6,38},{7,39},{8,40},{9,... | collective-permute-start | bytes 1622024 | tf_op jit(solution)/shard_map/ppermute | solution.py:61
  (8 other events, 34.3 us)

commit v8 on v7

--- a/solution.py
+++ b/solution.py
@@ -392,23 +392,31 @@
 
 def place_kernel(where, *refs):
     groups, refs = (refs[0:4], refs[4:8]), refs[8:]
-    output, output_out, grads, gain_attn, gain_mlp = refs[0], refs[1], refs[2:8], refs[8], refs[9]
+    output, output_out, outs, gain_attn, gain_mlp = refs[0], refs[1], refs[2:8], refs[8], refs[9]
+    grads, sems = refs[10:16], refs[16]
     output_out[0] = output[...]
-    for side, group in enumerate(groups):
-        holder = where[0] ^ side
-        for mask, arranged in enumerate(group):
-            part = holder * 4 + (where[1 + side] ^ mask)
-            for j, (at, rows) in enumerate(LAYOUT):
+    copies = []
+    for j, (at, rows) in enumerate(LAYOUT):
+        i = min(j, 4) if j < 6 else 5
+        for side, group in enumerate(groups):
+            holder = where[0] ^ side
+            for mask, arranged in enumerate(group):
+                part = holder * 4 + (where[1 + side] ^ mask)
                 to = pl.ds(pl.multiple_of(part * (4 * rows), 64), 4 * rows)
                 piece = arranged[at * 4 : (at + rows) * 4, :]
                 if j in (4, 5):
                     grads[4][to, 512 * (j - 4) : 512 * (j - 3)] = piece
                 else:
-                    grads[min(j, 5)][to, :] = piece
+                    grads[i][to, :] = piece
+        if j != 4:
+            copies.append(pltpu.make_async_copy(grads[i], outs[i], sems.at[i]))
+            copies[-1].start()
     own, other = (take_gains(group[0], 4 * CHUNK) for group in groups)
     gains = jnp.where(where[0] == 0, own, other).astype(jnp.bfloat16)
     gain_attn[...] = gains[0]
     gain_mlp[...] = gains[1]
+    for copy in copies:
+        copy.wait()
 
 
 def call(kernel, outs, *operands, scalars=0):
@@ -455,14 +463,17 @@
     (mine,) = call(arrange_kernel, [message], where, gains, *chunks, scalars=1)
     own = {0: mine, **to_peers(lambda mask: mine, first)}
     other = {mask: send(own[mask], CORE) for mask in (0,) + ORDER}
-    placed = call(
+    shapes = [(512, 512)] * 4 + [(512, 1024), (1024, 512)]
+    outs = [(1, BLK, 512), *shapes, (512,), (512,)]
+    placed = pl.pallas_call(
         place_kernel,
-        [((1, BLK, 512), b16)]
-        + [((512, 512), b16)] * 4
-        + [((512, 1024), b16), ((1024, 512), b16)]
-        + [((512,), b16)] * 2,
-        where, *(own[mask] for mask in range(4)), *(other[mask] for mask in range(4)), output, scalars=1,
-    )
+        out_shape=[jax.ShapeDtypeStruct(shape, b16) for shape in outs],
+        in_specs=[SMEM] + [VMEM] * 9,
+        out_specs=[VMEM] + [ANY] * 6 + [VMEM] * 2,
+        scratch_shapes=[pltpu.VMEM(shape, b16) for shape in shapes]
+        + [pltpu.SemaphoreType.DMA((6,))],
+        compiler_params=pltpu.CompilerParams(vmem_limit_bytes=24 << 20),
+    )(where, *(own[mask] for mask in range(4)), *(other[mask] for mask in range(4)), output)
     return tuple(placed)
 
 

time: 129 us -> 130 us (level)
    pallas_call x0 -> x1, Pallas kernels: none -> 3.43 us  [sum_everywhere(): pl.pallas_call(place_kernel, out_shape=[jax.ShapeDtypeStruct(shape, b16)...]
    pallas_call x8 -> x7, Pallas kernels: 4.89 us -> 2.01 us  [call(): pl.pallas_call(kernel, out_shape=[jax.ShapeDtypeStruct(shape, dtype) for...]
where the time goes in v8:
time: 130 us
  starting transfers between devices  54.9 us (42%)
  waiting for transfers between devices  41.2 us (32%)
  Pallas kernels  25.1 us (19%)
  other arithmetic  4.13 us (3%)
  local copies, waits for them, and re-layouts  3.41 us (3%)
    ppermute x36, starting transfers between devices, send(): return lax.ppermute(value, AXES, pairs)  54.9 us
    ppermute x36, waiting for transfers between devices, send(): return lax.ppermute(value, AXES, pairs)  41.2 us
    pallas_call x1, Pallas kernels, device_step(): pl.pallas_call(step_kernel, out_shape=[jax.ShapeDtypeStruct((BLK, 512), b...  19.6 us
    pallas_call x1, Pallas kernels, sum_everywhere(): pl.pallas_call(place_kernel, out_shape=[jax.ShapeDtypeStruct(shape, b16)...  3.43 us
  transfers between devices with their start and end apart: 36, of which 23 were waited for; matrix products, arithmetic and copies ran while one was open for 4% of the time, Pallas kernels for 0%

profile of v8, /device:TPU:1, one launch (start us, length us, event | category | flops | bytes accessed | tf_op | source)
XLA Modules:
  0.0 129.8 jit_solution(5851541791855781195)
XLA Ops:
  0.6 5.1 %collective-permute-start.3 = (bf16[128,512]{1,0:T(8,128)(2,1)}, bf16[128,512]{1,0:T(8,128)(2,1)S(1)}, u32[]{:S(2)}, u32[]{:S(2)}) collective-permute-start(bf16[128,512]{1,0:T(8,128)(2,1)} %bitcast.18), channel_id=1, source_target_pairs={{0,3},{1,2},{2,1},{3,0},{4,56},{5,57},{6,58},{7,59},{8,11},{9,10},... | collective-permute-start | bytes 393224 | tf_op jit(solution)/shard_map/ppermute | solution.py:61
  5.8 3.6 %collective-permute-start.2 = (bf16[128,512]{1,0:T(8,128)(2,1)}, bf16[128,512]{1,0:T(8,128)(2,1)S(1)}, u32[]{:S(2)}, u32[]{:S(2)}) collective-permute-start(bf16[128,512]{1,0:T(8,128)(2,1)} %bitcast.19), channel_id=1, source_target_pairs={{0,2},{1,3},{2,0},{3,1},{4,48},{5,49},{6,50},{7,51},{8,10},{9,11},... | collective-permute-start | bytes 393224 | tf_op jit(solution)/shard_map/ppermute | solution.py:61
  10.4 2.3 %collective-permute-start = (bf16[128,512]{1,0:T(8,128)(2,1)}, bf16[128,512]{1,0:T(8,128)(2,1)S(1)}, u32[]{:S(2)}, u32[]{:S(2)}) collective-permute-start(bf16[128,512]{1,0:T(8,128)(2,1)} %bitcast.21), channel_id=1, source_target_pairs={{0,0},{1,1},{2,2},{3,3},{4,32},{5,33},{6,34},{7,35},{8,8},{9,9},{1... | collective-permute-start | bytes 393224 | tf_op jit(solution)/shard_map/ppermute | solution.py:61
  14.1 1.4 %collective-permute-done.1 = bf16[128,512]{1,0:T(8,128)(2,1)S(1)} collective-permute-done((bf16[128,512]{1,0:T(8,128)(2,1)}, bf16[128,512]{1,0:T(8,128)(2,1)S(1)}, u32[]{:S(2)}, u32[]{:S(2)}) %collective-permute-start.1) | collective-permute-done | bytes 131104 | tf_op jit(solution)/shard_map/ppermute | solution.py:61
  15.5 1.3 %collective-permute-done = bf16[128,512]{1,0:T(8,128)(2,1)S(1)} collective-permute-done((bf16[128,512]{1,0:T(8,128)(2,1)}, bf16[128,512]{1,0:T(8,128)(2,1)S(1)}, u32[]{:S(2)}, u32[]{:S(2)}) %collective-permute-start) | collective-permute-done | bytes 131104 | tf_op jit(solution)/shard_map/ppermute | solution.py:61
  17.8 2.9 %collective-permute-start.6 = (bf16[512,512]{1,0:T(8,128)(2,1)S(1)}, bf16[512,512]{1,0:T(8,128)(2,1)}, u32[]{:S(2)}, u32[]{:S(2)}) collective-permute-start(bf16[512,512]{1,0:T(8,128)(2,1)S(1)} %pad_maximum_fusion.1.refs_0_), channel_id=1, source_target_pairs={{0,16},{1,17},{2,18},{3,19},{4,20},{5,21},{6,22},{7,23},{8,24},{9,... | collective-permute-start | bytes 1572872 | tf_op jit(solution)/shard_map/ppermute | solution.py:61
  21.7 2.7 %collective-permute-start.4 = (bf16[272,512]{1,0:T(8,128)(2,1)S(1)}, bf16[272,512]{1,0:T(8,128)(2,1)S(1)}, u32[]{:S(2)}, u32[]{:S(2)}) collective-permute-start(bf16[272,512]{1,0:T(8,128)(2,1)S(1)} %fusion.1), channel_id=1, source_target_pairs={{0,0},{1,1},{2,2},{3,3},{4,32},{5,33},{6,34},{7,35},{8,8},{9,9},{1... | collective-permute-start | bytes 835592 | tf_op jit(solution)/shard_map/ppermute | solution.py:61
  24.6 1.7 %pad_maximum_fusion.packed = bf16[2048,512]{1,0:T(8,128)(2,1)S(1)} fusion(bf16[512,512]{1,0:T(8,128)(2,1)} %param.22, bf16[512,512]{1,0:T(8,128)(2,1)} %param.21, bf16[512,512]{1,0:T(8,128)(2,1)} %param.20, bf16[512,512]{1,0:T(8,128)(2,1)} %param.19), kind=kLoop, calls=%fused_computation.1 | loop fusion | flops 8388608 | bytes 4194304 | tf_op jit(solution)/shard_map/concatenate | solution.py:492
  26.2 5.6 %collective-permute-done.7.refs_3_ = bf16[512,512]{1,0:T(8,128)(2,1)S(1)} collective-permute-done((bf16[512,512]{1,0:T(8,128)(2,1)S(1)}, bf16[512,512]{1,0:T(8,128)(2,1)S(1)}, u32[]{:S(2)}, u32[]{:S(2)}) %collective-permute-start.7) | collective-permute-done | bytes 524320 | tf_op jit(solution)/shard_map/ppermute | solution.py:61
  38.1 19.6 %shard_map.214 = (bf16[128,512]{1,0:T(8,128)(2,1)S(1)}, f32[8,512]{1,0:T(8,128)S(1)}, bf16[512,512]{1,0:T(8,128)(2,1)S(1)}, bf16[512,512]{1,0:T(8,128)(2,1)S(1)}...) custom-call(s32[3]{0:T(128)S(1)} %pad_add_fusion.where, ...), custom_call_target="tpu_custom_call" | custom-call | flops 12000000000 | bytes 18000000 | tf_op jit(solution)/shard_map/pallas_call | solution.py:286
  58.4 1.3 collective-permute-done.13.arrived
  61.8 2.0 %collective-permute-start.19 = (bf16[528,512]{1,0:T(8,128)(2,1)S(1)}, bf16[528,512]{1,0:T(8,128)(2,1)S(1)}, u32[]{:S(2)}, u32[]{:S(2)}) collective-permute-start(bf16[528,512]{1,0:T(8,128)(2,1)S(1)} %shard_map.217), channel_id=1, source_target_pairs={{0,3},{1,2},{2,1},{3,0},{4,7},{5,6},{6,5},{7,4},{8,11},{9,10},{10,... | collective-permute-start | bytes 1622024 | tf_op jit(solution)/shard_map/ppermute | solution.py:61
  64.6 3.4 %collective-permute-start.14 = (bf16[128,512]{1,0:T(8,128)(2,1)S(1)}, bf16[128,512]{1,0:T(8,128)(2,1)S(1)}, u32[]{:S(2)}, u32[]{:S(2)}) collective-permute-start(bf16[128,512]{1,0:T(8,128)(2,1)S(1)} %get-tuple-element.54), channel_id=1, source_target_pairs={{0,0},{1,1},{2,2},{3,3},{4,32},{5,33},{6,34},{7,35},{8,8},{9,9},{1... | collective-permute-start | bytes 393224 | tf_op jit(solution)/shard_map/ppermute | solution.py:61
  68.0 3.2 %collective-permute-done.14.refs_8_ = bf16[128,512]{1,0:T(8,128)(2,1)S(1)} collective-permute-done((bf16[128,512]{1,0:T(8,128)(2,1)S(1)}, bf16[128,512]{1,0:T(8,128)(2,1)S(1)}, u32[]{:S(2)}, u32[]{:S(2)}) %collective-permute-start.14) | collective-permute-done | bytes 131104 | tf_op jit(solution)/shard_map/ppermute | solution.py:61
  71.2 2.6 %collective-permute-done.16.refs_0_ = bf16[528,512]{1,0:T(8,128)(2,1)S(1)} collective-permute-done((bf16[528,512]{1,0:T(8,128)(2,1)S(1)}, bf16[528,512]{1,0:T(8,128)(2,1)S(1)}, u32[]{:S(2)}, u32[]{:S(2)}) %collective-permute-start.16) | collective-permute-done | bytes 540704 | tf_op jit(solution)/shard_map/ppermute | solution.py:61
  73.8 1.9 %collective-permute-done.19.refs_2_ = bf16[528,512]{1,0:T(8,128)(2,1)S(1)} collective-permute-done((bf16[528,512]{1,0:T(8,128)(2,1)S(1)}, bf16[528,512]{1,0:T(8,128)(2,1)S(1)}, u32[]{:S(2)}, u32[]{:S(2)}) %collective-permute-start.19) | collective-permute-done | bytes 540704 | tf_op jit(solution)/shard_map/ppermute | solution.py:61
  78.7 1.9 %collective-permute-start.22 = (bf16[144,512]{1,0:T(8,128)(2,1)S(1)}, bf16[144,512]{1,0:T(8,128)(2,1)S(1)}, u32[]{:S(2)}, u32[]{:S(2)}) collective-permute-start(bf16[144,512]{1,0:T(8,128)(2,1)S(1)} %get-tuple-element.67), channel_id=1, source_target_pairs={{0,24},{1,25},{2,26},{3,27},{4,28},{5,29},{6,30},{7,31},{8,16},{9,... | collective-permute-start | bytes 442376 | tf_op jit(solution)/shard_map/ppermute | solution.py:61
  81.0 2.1 %collective-permute-done.21.refs_1_ = bf16[144,512]{1,0:T(8,128)(2,1)S(1)} collective-permute-done((bf16[144,512]{1,0:T(8,128)(2,1)S(1)}, bf16[144,512]{1,0:T(8,128)(2,1)S(1)}, u32[]{:S(2)}, u32[]{:S(2)}) %collective-permute-start.21) | collective-permute-done | bytes 147488 | tf_op jit(solution)/shard_map/ppermute | solution.py:61
  83.1 1.8 %collective-permute-done.22.refs_2_ = bf16[144,512]{1,0:T(8,128)(2,1)S(1)} collective-permute-done((bf16[144,512]{1,0:T(8,128)(2,1)S(1)}, bf16[144,512]{1,0:T(8,128)(2,1)S(1)}, u32[]{:S(2)}, u32[]{:S(2)}) %collective-permute-start.22) | collective-permute-done | bytes 147488 | tf_op jit(solution)/shard_map/ppermute | solution.py:61
  85.0 2.7 %collective-permute-start.25 = (bf16[144,512]{1,0:T(8,128)(2,1)S(1)}, bf16[144,512]{1,0:T(8,128)(2,1)S(1)}, u32[]{:S(2)}, u32[]{:S(2)}) collective-permute-start(bf16[144,512]{1,0:T(8,128)(2,1)S(1)} %shard_map.219.own_ref), channel_id=1, source_target_pairs={{0,68},{1,69},{2,70},{3,71},{4,64},{5,65},{6,66},{7,67},{8,76},{9,... | collective-permute-start | bytes 442376 | tf_op jit(solution)/shard_map/ppermute | solution.py:61
  88.4 3.0 %collective-permute-done.25.refs_2_ = bf16[144,512]{1,0:T(8,128)(2,1)S(1)} collective-permute-done((bf16[144,512]{1,0:T(8,128)(2,1)S(1)}, bf16[144,512]{1,0:T(8,128)(2,1)S(1)}, u32[]{:S(2)}, u32[]{:S(2)}) %collective-permute-start.25) | collective-permute-done | bytes 147488 | tf_op jit(solution)/shard_map/ppermute | solution.py:61
  91.4 1.9 %collective-permute-done.24.refs_1_ = bf16[144,512]{1,0:T(8,128)(2,1)S(1)} collective-permute-done((bf16[144,512]{1,0:T(8,128)(2,1)S(1)}, bf16[144,512]{1,0:T(8,128)(2,1)S(1)}, u32[]{:S(2)}, u32[]{:S(2)}) %collective-permute-start.24) | collective-permute-done | bytes 147488 | tf_op jit(solution)/shard_map/ppermute | solution.py:61
  93.4 1.9 %collective-permute-start.28 = (bf16[128,512]{1,0:T(8,128)(2,1)S(1)}, bf16[128,512]{1,0:T(8,128)(2,1)S(1)}, u32[]{:S(2)}, u32[]{:S(2)}) collective-permute-start(bf16[128,512]{1,0:T(8,128)(2,1)S(1)} %get-tuple-element.69.refs_0_), channel_id=1, source_target_pairs={{0,24},{1,25},{2,26},{3,27},{4,28},{5,29},{6,30},{7,31},{8,16},{9,... | collective-permute-start | bytes 393224 | tf_op jit(solution)/shard_map/ppermute | solution.py:61
  95.3 1.5 %collective-permute-start.26 = (bf16[128,512]{1,0:T(8,128)(2,1)S(1)}, bf16[128,512]{1,0:T(8,128)(2,1)S(1)}, u32[]{:S(2)}, u32[]{:S(2)}) collective-permute-start(bf16[128,512]{1,0:T(8,128)(2,1)S(1)} %get-tuple-element.69.refs_0_), channel_id=1, source_target_pairs={{0,8},{1,9},{2,10},{3,11},{4,12},{5,13},{6,14},{7,15},{8,0},{9,1},... | collective-permute-start | bytes 393224 | tf_op jit(solution)/shard_map/ppermute | solution.py:61
  96.8 1.8 %collective-permute-done.28.refs_3_ = bf16[128,512]{1,0:T(8,128)(2,1)S(1)} collective-permute-done((bf16[128,512]{1,0:T(8,128)(2,1)S(1)}, bf16[128,512]{1,0:T(8,128)(2,1)S(1)}, u32[]{:S(2)}, u32[]{:S(2)}) %collective-permute-start.28) | collective-permute-done | bytes 131104 | tf_op jit(solution)/shard_map/ppermute | solution.py:61
  98.5 2.1 %collective-permute-done.27.refs_2_ = bf16[128,512]{1,0:T(8,128)(2,1)S(1)} collective-permute-done((bf16[128,512]{1,0:T(8,128)(2,1)S(1)}, bf16[128,512]{1,0:T(8,128)(2,1)S(1)}, u32[]{:S(2)}, u32[]{:S(2)}) %collective-permute-start.27) | collective-permute-done | bytes 131104 | tf_op jit(solution)/shard_map/ppermute | solution.py:61
  101.2 1.3 collective-permute-start.31
  102.5 2.9 %collective-permute-start.30 = (bf16[528,512]{1,0:T(8,128)(2,1)S(1)}, bf16[528,512]{1,0:T(8,128)(2,1)S(1)}, u32[]{:S(2)}, u32[]{:S(2)}) collective-permute-start(bf16[528,512]{1,0:T(8,128)(2,1)S(1)} %shard_map.221.refs_0_), channel_id=1, source_target_pairs={{0,2},{1,3},{2,0},{3,1},{4,6},{5,7},{6,4},{7,5},{8,10},{9,11},{10,... | collective-permute-start | bytes 1622024 | tf_op jit(solution)/shard_map/ppermute | solution.py:61
  105.4 5.4 %collective-permute-start.32 = (bf16[528,512]{1,0:T(8,128)(2,1)S(1)}, bf16[528,512]{1,0:T(8,128)(2,1)S(1)}, u32[]{:S(2)}, u32[]{:S(2)}) collective-permute-start(bf16[528,512]{1,0:T(8,128)(2,1)S(1)} %shard_map.221.refs_0_), channel_id=1, source_target_pairs={{0,32},{1,33},{2,34},{3,35},{4,36},{5,37},{6,38},{7,39},{8,40},{9,... | collective-permute-start | bytes 1622024 | tf_op jit(solution)/shard_map/ppermute | solution.py:61
  110.8 6.0 %collective-permute-done.31.refs_3_ = bf16[528,512]{1,0:T(8,128)(2,1)S(1)} collective-permute-done((bf16[528,512]{1,0:T(8,128)(2,1)S(1)}, bf16[528,512]{1,0:T(8,128)(2,1)S(1)}, u32[]{:S(2)}, u32[]{:S(2)}) %collective-permute-start.31) | collective-permute-done | bytes 540704 | tf_op jit(solution)/shard_map/ppermute | solution.py:61
  116.8 6.2 %collective-permute-start.35 = (bf16[528,512]{1,0:T(8,128)(2,1)S(1)}, bf16[528,512]{1,0:T(8,128)(2,1)S(1)}, u32[]{:S(2)}, u32[]{:S(2)}) collective-permute-start(bf16[528,512]{1,0:T(8,128)(2,1)S(1)} %collective-permute-done.31.refs_3_), channel_id=1, source_target_pairs={{0,32},{1,33},{2,34},{3,35},{4,36},{5,37},{6,38},{7,39},{8,40},{9,... | collective-permute-start | bytes 1622024 | tf_op jit(solution)/shard_map/ppermute | solution.py:61
  126.2 3.4 %shard_map.222 = (bf16[1,128,512]{2,1,0:T(8,128)(2,1)}, bf16[512,512]{1,0:T(8,128)(2,1)}, bf16[512,512]{1,0:T(8,128)(2,1)}, bf16[512,512]{1,0:T(8,128)(2,1)}, bf...) custom-call(s32[3]{0:T(128)S(1)} %pad_add_fusion.where, ...), custom_call_target="tpu_custom_call" | custom-call | tf_op jit(solution)/shard_map/pallas_call | solution.py:468
  (70 shorter events, 22.1 us)
Async XLA Ops:
  0.6 13.5 %collective-permute-start.3 = (bf16[128,512]{1,0:T(8,128)(2,1)}, bf16[128,512]{1,0:T(8,128)(2,1)S(1)}, u32[]{:S(2)}, u32[]{:S(2)}) collective-permute-start(bf16[128,512]{1,0:T(8,128)(2,1)} %bitcast.18), channel_id=1, source_target_pairs={{0,3},{1,2},{2,1},{3,0},{4,56},{5,57},{6,58},{7,59},{8,11},{9,10},... | collective-permute-start | bytes 393224 | tf_op jit(solution)/shard_map/ppermute | solution.py:61
  5.8 8.3 %collective-permute-start.2 = (bf16[128,512]{1,0:T(8,128)(2,1)}, bf16[128,512]{1,0:T(8,128)(2,1)S(1)}, u32[]{:S(2)}, u32[]{:S(2)}) collective-permute-start(bf16[128,512]{1,0:T(8,128)(2,1)} %bitcast.19), channel_id=1, source_target_pairs={{0,2},{1,3},{2,0},{3,1},{4,48},{5,49},{6,50},{7,51},{8,10},{9,11},... | collective-permute-start | bytes 393224 | tf_op jit(solution)/shard_map/ppermute | solution.py:61
  9.4 6.1 %collective-permute-start.1 = (bf16[128,512]{1,0:T(8,128)(2,1)}, bf16[128,512]{1,0:T(8,128)(2,1)S(1)}, u32[]{:S(2)}, u32[]{:S(2)}) collective-permute-start(bf16[128,512]{1,0:T(8,128)(2,1)} %bitcast.20), channel_id=1, source_target_pairs={{0,1},{1,0},{2,3},{3,2},{4,40},{5,41},{6,42},{7,43},{8,9},{9,8},{1... | collective-permute-start | bytes 393224 | tf_op jit(solution)/shard_map/ppermute | solution.py:61
  10.4 6.5 %collective-permute-start = (bf16[128,512]{1,0:T(8,128)(2,1)}, bf16[128,512]{1,0:T(8,128)(2,1)S(1)}, u32[]{:S(2)}, u32[]{:S(2)}) collective-permute-start(bf16[128,512]{1,0:T(8,128)(2,1)} %bitcast.21), channel_id=1, source_target_pairs={{0,0},{1,1},{2,2},{3,3},{4,32},{5,33},{6,34},{7,35},{8,8},{9,9},{1... | collective-permute-start | bytes 393224 | tf_op jit(solution)/shard_map/ppermute | solution.py:61
  16.9 14.9 %collective-permute-start.7 = (bf16[512,512]{1,0:T(8,128)(2,1)S(1)}, bf16[512,512]{1,0:T(8,128)(2,1)S(1)}, u32[]{:S(2)}, u32[]{:S(2)}) collective-permute-start(bf16[512,512]{1,0:T(8,128)(2,1)S(1)} %pad_maximum_fusion.1.refs_0_), channel_id=1, source_target_pairs={{0,24},{1,25},{2,26},{3,27},{4,28},{5,29},{6,30},{7,31},{8,16},{9,... | collective-permute-start | bytes 1572872 | tf_op jit(solution)/shard_map/ppermute | solution.py:61
  17.8 14.1 %collective-permute-start.6 = (bf16[512,512]{1,0:T(8,128)(2,1)S(1)}, bf16[512,512]{1,0:T(8,128)(2,1)}, u32[]{:S(2)}, u32[]{:S(2)}) collective-permute-start(bf16[512,512]{1,0:T(8,128)(2,1)S(1)} %pad_maximum_fusion.1.refs_0_), channel_id=1, source_target_pairs={{0,16},{1,17},{2,18},{3,19},{4,20},{5,21},{6,22},{7,23},{8,24},{9,... | collective-permute-start | bytes 1572872 | tf_op jit(solution)/shard_map/ppermute | solution.py:61
  20.7 11.9 %collective-permute-start.5 = (bf16[512,512]{1,0:T(8,128)(2,1)S(1)}, bf16[512,512]{1,0:T(8,128)(2,1)}, u32[]{:S(2)}, u32[]{:S(2)}) collective-permute-start(bf16[512,512]{1,0:T(8,128)(2,1)S(1)} %pad_maximum_fusion.1.refs_0_), channel_id=1, source_target_pairs={{0,8},{1,9},{2,10},{3,11},{4,12},{5,13},{6,14},{7,15},{8,0},{9,1},... | collective-permute-start | bytes 1572872 | tf_op jit(solution)/shard_map/ppermute | solution.py:61
  21.7 10.9 %collective-permute-start.4 = (bf16[272,512]{1,0:T(8,128)(2,1)S(1)}, bf16[272,512]{1,0:T(8,128)(2,1)S(1)}, u32[]{:S(2)}, u32[]{:S(2)}) collective-permute-start(bf16[272,512]{1,0:T(8,128)(2,1)S(1)} %fusion.1), channel_id=1, source_target_pairs={{0,0},{1,1},{2,2},{3,3},{4,32},{5,33},{6,34},{7,35},{8,8},{9,9},{1... | collective-permute-start | bytes 835592 | tf_op jit(solution)/shard_map/ppermute | solution.py:61
  24.5 9.1 %collective-permute-start.8 = (bf16[512,512]{1,0:T(8,128)(2,1)S(1)}, bf16[512,512]{1,0:T(8,128)(2,1)}, u32[]{:S(2)}, u32[]{:S(2)}) collective-permute-start(bf16[512,512]{1,0:T(8,128)(2,1)S(1)} %pad_maximum_fusion.1.refs_0_), channel_id=1, source_target_pairs={{0,32},{1,33},{2,34},{3,35},{4,36},{5,37},{6,38},{7,39},{8,40},{9,... | collective-permute-start | bytes 1572872 | tf_op jit(solution)/shard_map/ppermute | solution.py:61
  31.9 3.0 %collective-permute-start.10 = (bf16[512,512]{1,0:T(8,128)(2,1)}, bf16[512,512]{1,0:T(8,128)(2,1)}, u32[]{:S(2)}, u32[]{:S(2)}) collective-permute-start(bf16[512,512]{1,0:T(8,128)(2,1)} %collective-permute-done.6.refs_2_), channel_id=1, source_target_pairs={{0,32},{1,33},{2,34},{3,35},{4,36},{5,37},{6,38},{7,39},{8,40},{9,... | collective-permute-start | bytes 1572872 | tf_op jit(solution)/shard_map/ppermute | solution.py:61
  32.6 3.0 %collective-permute-start.9 = (bf16[512,512]{1,0:T(8,128)(2,1)}, bf16[512,512]{1,0:T(8,128)(2,1)}, u32[]{:S(2)}, u32[]{:S(2)}) collective-permute-start(bf16[512,512]{1,0:T(8,128)(2,1)} %collective-permute-done.5.refs_1_), channel_id=1, source_target_pairs={{0,32},{1,33},{2,34},{3,35},{4,36},{5,37},{6,38},{7,39},{8,40},{9,... | collective-permute-start | bytes 1572872 | tf_op jit(solution)/shard_map/ppermute | solution.py:61
  58.3 3.4 %collective-permute-start.18 = (bf16[512,512]{1,0:T(8,128)(2,1)S(1)}, bf16[512,512]{1,0:T(8,128)(2,1)S(1)}, u32[]{:S(2)}, u32[]{:S(2)}) collective-permute-start(bf16[512,512]{1,0:T(8,128)(2,1)S(1)} %get-tuple-element.59), channel_id=1, source_target_pairs={{0,32},{1,33},{2,34},{3,35},{4,36},{5,37},{6,38},{7,39},{8,40},{9,... | collective-permute-start | bytes 1572872 | tf_op jit(solution)/shard_map/ppermute | solution.py:61
  59.9 11.3 %collective-permute-start.17 = (bf16[528,512]{1,0:T(8,128)(2,1)S(1)}, bf16[528,512]{1,0:T(8,128)(2,1)S(1)}, u32[]{:S(2)}, u32[]{:S(2)}) collective-permute-start(bf16[528,512]{1,0:T(8,128)(2,1)S(1)} %get-tuple-element.57), channel_id=1, source_target_pairs={{0,2},{1,3},{2,0},{3,1},{4,6},{5,7},{6,4},{7,5},{8,10},{9,11},{10,... | collective-permute-start | bytes 1622024 | tf_op jit(solution)/shard_map/ppermute | solution.py:61
  60.6 13.2 %collective-permute-start.16 = (bf16[528,512]{1,0:T(8,128)(2,1)S(1)}, bf16[528,512]{1,0:T(8,128)(2,1)S(1)}, u32[]{:S(2)}, u32[]{:S(2)}) collective-permute-start(bf16[528,512]{1,0:T(8,128)(2,1)S(1)} %shard_map.216), channel_id=1, source_target_pairs={{0,1},{1,0},{2,3},{3,2},{4,5},{5,4},{6,7},{7,6},{8,9},{9,8},{10,11... | collective-permute-start | bytes 1622024 | tf_op jit(solution)/shard_map/ppermute | solution.py:61
  61.8 13.9 %collective-permute-start.19 = (bf16[528,512]{1,0:T(8,128)(2,1)S(1)}, bf16[528,512]{1,0:T(8,128)(2,1)S(1)}, u32[]{:S(2)}, u32[]{:S(2)}) collective-permute-start(bf16[528,512]{1,0:T(8,128)(2,1)S(1)} %shard_map.217), channel_id=1, source_target_pairs={{0,3},{1,2},{2,1},{3,0},{4,7},{5,6},{6,5},{7,4},{8,11},{9,10},{10,... | collective-permute-start | bytes 1622024 | tf_op jit(solution)/shard_map/ppermute | solution.py:61
  63.8 11.9 %collective-permute-start.12 = (bf16[512,512]{1,0:T(8,128)(2,1)S(1)}, bf16[512,512]{1,0:T(8,128)(2,1)S(1)}, u32[]{:S(2)}, u32[]{:S(2)}) collective-permute-start(bf16[512,512]{1,0:T(8,128)(2,1)S(1)} %get-tuple-element.49), channel_id=1, source_target_pairs={{0,32},{1,33},{2,34},{3,35},{4,36},{5,37},{6,38},{7,39},{8,40},{9,... | collective-permute-start | bytes 1572872 | tf_op jit(solution)/shard_map/ppermute | solution.py:61
  64.6 6.6 %collective-permute-start.14 = (bf16[128,512]{1,0:T(8,128)(2,1)S(1)}, bf16[128,512]{1,0:T(8,128)(2,1)S(1)}, u32[]{:S(2)}, u32[]{:S(2)}) collective-permute-start(bf16[128,512]{1,0:T(8,128)(2,1)S(1)} %get-tuple-element.54), channel_id=1, source_target_pairs={{0,0},{1,1},{2,2},{3,3},{4,32},{5,33},{6,34},{7,35},{8,8},{9,9},{1... | collective-permute-start | bytes 393224 | tf_op jit(solution)/shard_map/ppermute | solution.py:61
  76.6 4.4 %collective-permute-start.20 = (bf16[144,512]{1,0:T(8,128)(2,1)S(1)}, bf16[144,512]{1,0:T(8,128)(2,1)S(1)}, u32[]{:S(2)}, u32[]{:S(2)}) collective-permute-start(bf16[144,512]{1,0:T(8,128)(2,1)S(1)} %get-tuple-element.65), channel_id=1, source_target_pairs={{0,8},{1,9},{2,10},{3,11},{4,12},{5,13},{6,14},{7,15},{8,0},{9,1},... | collective-permute-start | bytes 442376 | tf_op jit(solution)/shard_map/ppermute | solution.py:61
  77.6 5.6 %collective-permute-start.21 = (bf16[144,512]{1,0:T(8,128)(2,1)S(1)}, bf16[144,512]{1,0:T(8,128)(2,1)S(1)}, u32[]{:S(2)}, u32[]{:S(2)}) collective-permute-start(bf16[144,512]{1,0:T(8,128)(2,1)S(1)} %get-tuple-element.66), channel_id=1, source_target_pairs={{0,16},{1,17},{2,18},{3,19},{4,20},{5,21},{6,22},{7,23},{8,24},{9,... | collective-permute-start | bytes 442376 | tf_op jit(solution)/shard_map/ppermute | solution.py:61
  78.7 6.2 %collective-permute-start.22 = (bf16[144,512]{1,0:T(8,128)(2,1)S(1)}, bf16[144,512]{1,0:T(8,128)(2,1)S(1)}, u32[]{:S(2)}, u32[]{:S(2)}) collective-permute-start(bf16[144,512]{1,0:T(8,128)(2,1)S(1)} %get-tuple-element.67), channel_id=1, source_target_pairs={{0,24},{1,25},{2,26},{3,27},{4,28},{5,29},{6,30},{7,31},{8,16},{9,... | collective-permute-start | bytes 442376 | tf_op jit(solution)/shard_map/ppermute | solution.py:61
  85.0 6.4 %collective-permute-start.25 = (bf16[144,512]{1,0:T(8,128)(2,1)S(1)}, bf16[144,512]{1,0:T(8,128)(2,1)S(1)}, u32[]{:S(2)}, u32[]{:S(2)}) collective-permute-start(bf16[144,512]{1,0:T(8,128)(2,1)S(1)} %shard_map.219.own_ref), channel_id=1, source_target_pairs={{0,68},{1,69},{2,70},{3,71},{4,64},{5,65},{6,66},{7,67},{8,76},{9,... | collective-permute-start | bytes 442376 | tf_op jit(solution)/shard_map/ppermute | solution.py:61
  87.7 5.6 %collective-permute-start.24 = (bf16[144,512]{1,0:T(8,128)(2,1)S(1)}, bf16[144,512]{1,0:T(8,128)(2,1)S(1)}, u32[]{:S(2)}, u32[]{:S(2)}) collective-permute-start(bf16[144,512]{1,0:T(8,128)(2,1)S(1)} %shard_map.219.own_ref), channel_id=1, source_target_pairs={{0,64},{1,65},{2,66},{3,67},{4,68},{5,69},{6,70},{7,71},{8,72},{9,... | collective-permute-start | bytes 442376 | tf_op jit(solution)/shard_map/ppermute | solution.py:61
  88.3 5.1 %collective-permute-start.23 = (bf16[144,512]{1,0:T(8,128)(2,1)S(1)}, bf16[144,512]{1,0:T(8,128)(2,1)S(1)}, u32[]{:S(2)}, u32[]{:S(2)}) collective-permute-start(bf16[144,512]{1,0:T(8,128)(2,1)S(1)} %shard_map.219.own_ref), channel_id=1, source_target_pairs={{0,4},{1,5},{2,6},{3,7},{4,0},{5,1},{6,2},{7,3},{8,12},{9,13},{10,... | collective-permute-start | bytes 442376 | tf_op jit(solution)/shard_map/ppermute | solution.py:61
  93.4 5.1 %collective-permute-start.28 = (bf16[128,512]{1,0:T(8,128)(2,1)S(1)}, bf16[128,512]{1,0:T(8,128)(2,1)S(1)}, u32[]{:S(2)}, u32[]{:S(2)}) collective-permute-start(bf16[128,512]{1,0:T(8,128)(2,1)S(1)} %get-tuple-element.69.refs_0_), channel_id=1, source_target_pairs={{0,24},{1,25},{2,26},{3,27},{4,28},{5,29},{6,30},{7,31},{8,16},{9,... | collective-permute-start | bytes 393224 | tf_op jit(solution)/shard_map/ppermute | solution.py:61
  95.3 5.3 %collective-permute-start.27 = (bf16[128,512]{1,0:T(8,128)(2,1)S(1)}, bf16[128,512]{1,0:T(8,128)(2,1)S(1)}, u32[]{:S(2)}, u32[]{:S(2)}) collective-permute-start(bf16[128,512]{1,0:T(8,128)(2,1)S(1)} %get-tuple-element.69.refs_0_), channel_id=1, source_target_pairs={{0,16},{1,17},{2,18},{3,19},{4,20},{5,21},{6,22},{7,23},{8,24},{9,... | collective-permute-start | bytes 393224 | tf_op jit(solution)/shard_map/ppermute | solution.py:61
  95.3 5.3 %collective-permute-start.26 = (bf16[128,512]{1,0:T(8,128)(2,1)S(1)}, bf16[128,512]{1,0:T(8,128)(2,1)S(1)}, u32[]{:S(2)}, u32[]{:S(2)}) collective-permute-start(bf16[128,512]{1,0:T(8,128)(2,1)S(1)} %get-tuple-element.69.refs_0_), channel_id=1, source_target_pairs={{0,8},{1,9},{2,10},{3,11},{4,12},{5,13},{6,14},{7,15},{8,0},{9,1},... | collective-permute-start | bytes 393224 | tf_op jit(solution)/shard_map/ppermute | solution.py:61
  101.2 15.6 %collective-permute-start.31 = (bf16[528,512]{1,0:T(8,128)(2,1)S(1)}, bf16[528,512]{1,0:T(8,128)(2,1)S(1)}, u32[]{:S(2)}, u32[]{:S(2)}) collective-permute-start(bf16[528,512]{1,0:T(8,128)(2,1)S(1)} %shard_map.221.refs_0_), channel_id=1, source_target_pairs={{0,3},{1,2},{2,1},{3,0},{4,7},{5,6},{6,5},{7,4},{8,11},{9,10},{10,... | collective-permute-start | bytes 1622024 | tf_op jit(solution)/shard_map/ppermute | solution.py:61
  102.5 20.5 %collective-permute-start.30 = (bf16[528,512]{1,0:T(8,128)(2,1)S(1)}, bf16[528,512]{1,0:T(8,128)(2,1)S(1)}, u32[]{:S(2)}, u32[]{:S(2)}) collective-permute-start(bf16[528,512]{1,0:T(8,128)(2,1)S(1)} %shard_map.221.refs_0_), channel_id=1, source_target_pairs={{0,2},{1,3},{2,0},{3,1},{4,6},{5,7},{6,4},{7,5},{8,10},{9,11},{10,... | collective-permute-start | bytes 1622024 | tf_op jit(solution)/shard_map/ppermute | solution.py:61
  105.4 17.7 %collective-permute-start.29 = (bf16[528,512]{1,0:T(8,128)(2,1)S(1)}, bf16[528,512]{1,0:T(8,128)(2,1)S(1)}, u32[]{:S(2)}, u32[]{:S(2)}) collective-permute-start(bf16[528,512]{1,0:T(8,128)(2,1)S(1)} %shard_map.221.refs_0_), channel_id=1, source_target_pairs={{0,1},{1,0},{2,3},{3,2},{4,5},{5,4},{6,7},{7,6},{8,9},{9,8},{10,11... | collective-permute-start | bytes 1622024 | tf_op jit(solution)/shard_map/ppermute | solution.py:61
  105.4 18.6 %collective-permute-start.32 = (bf16[528,512]{1,0:T(8,128)(2,1)S(1)}, bf16[528,512]{1,0:T(8,128)(2,1)S(1)}, u32[]{:S(2)}, u32[]{:S(2)}) collective-permute-start(bf16[528,512]{1,0:T(8,128)(2,1)S(1)} %shard_map.221.refs_0_), channel_id=1, source_target_pairs={{0,32},{1,33},{2,34},{3,35},{4,36},{5,37},{6,38},{7,39},{8,40},{9,... | collective-permute-start | bytes 1622024 | tf_op jit(solution)/shard_map/ppermute | solution.py:61
  116.8 7.8 %collective-permute-start.35 = (bf16[528,512]{1,0:T(8,128)(2,1)S(1)}, bf16[528,512]{1,0:T(8,128)(2,1)S(1)}, u32[]{:S(2)}, u32[]{:S(2)}) collective-permute-start(bf16[528,512]{1,0:T(8,128)(2,1)S(1)} %collective-permute-done.31.refs_3_), channel_id=1, source_target_pairs={{0,32},{1,33},{2,34},{3,35},{4,36},{5,37},{6,38},{7,39},{8,40},{9,... | collective-permute-start | bytes 1622024 | tf_op jit(solution)/shard_map/ppermute | solution.py:61
  123.1 3.1 %collective-permute-start.33 = (bf16[528,512]{1,0:T(8,128)(2,1)S(1)}, bf16[528,512]{1,0:T(8,128)(2,1)S(1)}, u32[]{:S(2)}, u32[]{:S(2)}) collective-permute-start(bf16[528,512]{1,0:T(8,128)(2,1)S(1)} %collective-permute-done.29.refs_1_), channel_id=1, source_target_pairs={{0,32},{1,33},{2,34},{3,35},{4,36},{5,37},{6,38},{7,39},{8,40},{9,... | collective-permute-start | bytes 1622024 | tf_op jit(solution)/shard_map/ppermute | solution.py:61
  (8 other events, 34.3 us)
